TPU v7x, 512 devices: a whole 4x8x8 slice. The times are simulated.
512 devices in a mesh: row: 64 (over z, y), bundle: 8 (over x, core).
Axes of the slice: x: 4, y: 8, z: 8, core: 2. Of those that a mesh axis runs over, the one named last changes fastest.
Arguments:
- vectors: float32 [256, 131072], P('bundle', 'row'), may hold values from -6 to 6
- blocks: float32 [2048, 64, 384], P('row'), may hold values from -0.30618622 to 0.30618622, as said below
- columns: int32 [2048, 6], P('row'), may hold values from 0 to 2047, as said below
- bounds: float32 [2], replicated, may hold values from -0.9 to 0.5, as said below
Outputs:
- basis: float32 [256, 131072], P(None, ('row', 'bundle'))
- factor: float32 [256, 256], replicated
Inputs may be any that keep to these rules, and one draw needn't show every extreme that they name: Slot 0 of block row i is i itself; every block column of block row i lies within 32 block rows of i, counted cyclically over the 2048 block rows, and a distance of exactly 32 occurs; columns of one block row may repeat. `blocks`: together with columns they make H symmetric. bounds[0] < 0 < bounds[1].
All inputs are finite; a program needn't handle non-finite values.
Results may differ from a plain program's by a relative error of at most 0.00011.
Values sent between devices are 32-bit elements; how exact they have to be, the bound alone decides.
No kernel may reach another device: no remote copies, remote signals or barrier semaphores. Data moves between devices by JAX's collectives and lax.ppermute only.
A program may use at most 64 MiB of HBM per device.

v0:
```python
import jax
import jax.numpy as jnp
from jax import lax
from jax.sharding import PartitionSpec as P


def extended_2(block, sides, width):
    for axis, dim in sides:
        count = lax.axis_size(axis)
        forward = [(i, i + 1) for i in range(count - 1)]
        forward.append((count - 1, 0))
        backward = [(target, source) for source, target in forward]
        low = lax.ppermute(
            lax.slice_in_dim(block, block.shape[dim] - width, None, axis=dim), axis, forward
        )
        high = lax.ppermute(lax.slice_in_dim(block, 0, width, axis=dim), axis, backward)
        block = jnp.concatenate([low, block, high], axis=dim)
    return block


def local(vectors, blocks, columns, bounds):
    block_rows = blocks.shape[0]
    block_size = blocks.shape[1]
    slot_count = columns.shape[1]
    row_count = lax.axis_size("row")
    total_rows = block_rows * row_count
    first_row = lax.axis_index("row") * block_rows
    center = (bounds[0] + bounds[1]) * 0.5
    half = (bounds[1] - bounds[0]) * 0.5
    local_cols = jnp.mod(columns - first_row + block_rows, total_rows).reshape(-1)

    def apply_operator(field):
        extended = extended_2(field, (("row", 1),), block_rows * block_size)
        width = field.shape[0]
        extended3 = extended.reshape(width, 3 * block_rows, block_size)
        picked = jnp.take(extended3, local_cols, axis=1).reshape(
            width, block_rows, slot_count * block_size
        )
        result = jnp.einsum("iam,cim->cia", blocks, picked, precision=lax.Precision.HIGHEST)
        return result.reshape(width, block_rows * block_size)

    first = (apply_operator(vectors) - center * vectors) / half
    second = 2.0 * (apply_operator(first) - center * first) / half - vectors
    filtered = 2.0 * (apply_operator(second) - center * second) / half - first
    stacked = lax.all_to_all(filtered, "bundle", split_axis=1, concat_axis=0, tiled=True)
    gram = jnp.dot(
        stacked, stacked.T, precision=lax.Precision.HIGHEST, preferred_element_type=jnp.float32
    )
    gram = lax.psum(gram, ("row", "bundle"))
    lower = jnp.linalg.cholesky(gram)
    basis = jax.scipy.linalg.solve_triangular(lower, stacked, lower=True)
    return (basis, lower.T)


def solution(mesh):
    placed = (P("bundle", "row"), P("row", None, None), P("row", None), P())
    return jax.shard_map(
        local,
        mesh=mesh,
        in_specs=placed,
        out_specs=(P(None, ("row", "bundle")), P()),
        check_vma=False,
    )
```

profile of v0, /device:TPU:1, one launch (start us, length us, event | category | flops | bytes accessed | tf_op | source)
XLA Modules:
  0.0 516.3 jit_solution(1491135728791172816)
XLA Ops:
  7.2 4.3 collective-permute-start
  11.5 12.3 %collective-permute-start.1 = (f32[32,2048]{1,0:T(8,128)}, f32[32,2048]{1,0:T(8,128)}, u32[]{:S(2)}, u32[]{:S(2)}) collective-permute-start(f32[32,2048]{1,0:T(8,128)} %param.6), channel_id=1, source_target_pairs={{8,0},{16,8},{24,16},{32,24},{40,32},{48,40},{56,48},{64,56},{72,6... | collective-permute-start | bytes 786440 | tf_op jit(solution)/shard_map/ppermute | solution.py:16
  33.9 3.5 copy.10
  37.4 3.8 gather_fusion
  46.8 3.8 reshape.71
  50.6 5.6 %fusion.6 = f32[32,32,64]{2,0,1:T(8,128)S(1)} fusion(f32[32,64,384]{2,1,0:T(8,128)S(1)} %copy-done, f32[32,32,384]{2,1,0:T(8,128)} %reshape.71), kind=kOutput, calls=%fused_computation.14 | convolution fusion | flops 301989888 | bytes 4980736 | tf_op jit(solution)/shard_map/iam,cim->cia/dot_general | solution.py:39
  62.3 8.0 %collective-permute-start.3 = (f32[32,2048]{1,0:T(8,128)S(1)}, f32[32,2048]{1,0:T(8,128)S(1)}, u32[]{:S(2)}, u32[]{:S(2)}) collective-permute-start(f32[32,2048]{1,0:T(8,128)S(1)} %subtract_divide_fusion), channel_id=1, source_target_pairs={{8,0},{16,8},{24,16},{32,24},{40,32},{48,40},{56,48},{64,56},{72,6... | collective-permute-start | bytes 786440 | tf_op jit(solution)/shard_map/ppermute | solution.py:16
  77.7 3.5 copy.14
  81.1 3.8 gather_fusion.1
  90.6 3.8 reshape.74
  94.4 5.6 %fusion.9 = f32[32,32,64]{2,0,1:T(8,128)S(1)} fusion(f32[32,64,384]{2,1,0:T(8,128)S(1)} %copy-done, f32[32,32,384]{2,1,0:T(8,128)} %reshape.74), kind=kOutput, calls=%fused_computation.15 | convolution fusion | flops 301989888 | bytes 4980736 | tf_op jit(solution)/shard_map/iam,cim->cia/dot_general | solution.py:39
  106.0 7.6 %collective-permute-start.5 = (f32[32,2048]{1,0:T(8,128)S(1)}, f32[32,2048]{1,0:T(8,128)S(1)}, u32[]{:S(2)}, u32[]{:S(2)}) collective-permute-start(f32[32,2048]{1,0:T(8,128)S(1)} %divide_subtract_fusion.1), channel_id=1, source_target_pairs={{8,0},{16,8},{24,16},{32,24},{40,32},{48,40},{56,48},{64,56},{72,6... | collective-permute-start | bytes 786440 | tf_op jit(solution)/shard_map/ppermute | solution.py:16
  120.6 3.5 copy.18
  124.1 3.8 gather_fusion.2
  133.5 3.8 reshape.77
  137.3 5.6 %fusion.12 = f32[32,32,64]{2,0,1:T(8,128)S(1)} fusion(f32[32,64,384]{2,1,0:T(8,128)S(1)} %copy-done, f32[32,32,384]{2,1,0:T(8,128)} %reshape.77), kind=kOutput, calls=%fused_computation.16 | convolution fusion | flops 301989888 | bytes 4980736 | tf_op jit(solution)/shard_map/iam,cim->cia/dot_general | solution.py:39
  147.8 7.5 %all-to-all-start = ((f32[32,8,256]{2,0,1:T(8,128)}), f32[32,8,256]{2,0,1:T(8,128)S(1)}, u32[]{:S(2)}, u32[]{:S(2)}) async-start(f32[32,8,256]{2,0,1:T(8,128)} %bitcast.65), calls=%async_computation | async-start | bytes 524288 | tf_op jit(solution)/shard_map/all_to_all | solution.py:45
  155.5 6.2 %all-to-all-done = f32[32,8,256]{2,0,1:T(8,128)S(1)} async-done(((f32[32,8,256]{2,0,1:T(8,128)}), f32[32,8,256]{2,0,1:T(8,128)S(1)}, u32[]{:S(2)}, u32[]{:S(2)}) %all-to-all-start) | async-done | bytes 262176 | tf_op jit(solution)/shard_map/all_to_all | solution.py:45
  163.6 265.5 %all-reduce.3.cloned.1.call-done = f32[256,256]{0,1:T(8,128)} async-done(((f32[256,256]{0,1:T(8,128)}), f32[256,256]{0,1:T(8,128)}) %all-reduce.3.cloned.1.call-update) | async-done | bytes 262160 | tf_op jit(solution)/shard_map/psum | solution.py:49
  431.8 11.7 %cholesky.50 = f32[128,128]{1,0:T(8,128)S(1)} custom-call(f32[128,128]{1,0:T(8,128)S(1)} %cholesky.118), custom_call_target="Cholesky" | custom-call | tf_op jit(solution)/shard_map/jit(cholesky)/cholesky | solution.py:50
  445.7 11.3 %custom-call.15 = f32[1,128,128]{1,2,0:T(8,128)} custom-call(f32[1,128,128]{2,1,0:T(8,128)} %get-tuple-element.32), custom_call_target="InvertDiagBlocksLowerTriangular" | custom-call | tf_op jit(solution)/shard_map/jit(cholesky)/cholesky | solution.py:50
  459.8 13.2 %cholesky.105 = f32[128,128]{1,0:T(8,128)} custom-call(f32[128,128]{1,0:T(8,128)} %convolution_subtract_fusion.1), custom_call_target="Cholesky" | custom-call | tf_op jit(solution)/shard_map/jit(cholesky)/cholesky | solution.py:50
  477.6 5.3 %while.1 = (s32[]{:T(128)}, f32[256,256]{1,0:T(8,128)S(1)}, s32[2,2]{1,0:T(2,128)S(1)}, f32[2,128,128]{2,1,0:T(8,128)}, s32[]{:T(128)}) while((s32[]{:T(128)}, f32[256,256]{1,0:T(8,128)S(1)}, s32[2,2]{1,0:T(2,128)S(1)}, f32[2,128,128]{2,1,0:T(8,128)}, s32[]{:T(128)}) %tuple.33), condition=%wide.while_cond, body=%wide.while_body.sunk | while | flops 2 | bytes 132705 | solution.py:51
  482.8 21.1 %custom-call.16 = f32[2,128,128]{1,2,0:T(8,128)} custom-call(f32[2,128,128]{2,1,0:T(8,128)} %get-tuple-element.10), custom_call_target="InvertDiagBlocksLowerTriangular" | custom-call | tf_op jit(solution)/shard_map/jit(_solve_triangular)/triangular_solve | solution.py:51
  (75 shorter events, 79.0 us)
Async XLA Ops:
  7.2 43.5 %copy-start = (f32[32,64,384]{2,1,0:T(8,128)S(1)}, f32[32,64,384]{2,1,0:T(8,128)}, u32[]{:S(2)}) copy-start(f32[32,64,384]{2,1,0:T(8,128)} %param.7) | copy-start | bytes 9437188
  7.2 21.4 %collective-permute-start = (f32[32,2048]{1,0:T(8,128)}, f32[32,2048]{1,0:T(8,128)S(1)}, u32[]{:S(2)}, u32[]{:S(2)}) collective-permute-start(f32[32,2048]{1,0:T(8,128)} %param.6), channel_id=1, source_target_pairs={{0,8},{8,16},{16,24},{24,32},{32,40},{40,48},{48,56},{56,64},{64,7... | collective-permute-start | bytes 786440 | tf_op jit(solution)/shard_map/ppermute | solution.py:13
  11.5 17.6 %collective-permute-start.1 = (f32[32,2048]{1,0:T(8,128)}, f32[32,2048]{1,0:T(8,128)}, u32[]{:S(2)}, u32[]{:S(2)}) collective-permute-start(f32[32,2048]{1,0:T(8,128)} %param.6), channel_id=1, source_target_pairs={{8,0},{16,8},{24,16},{32,24},{40,32},{48,40},{56,48},{64,56},{72,6... | collective-permute-start | bytes 786440 | tf_op jit(solution)/shard_map/ppermute | solution.py:16
  60.3 12.6 %collective-permute-start.2 = (f32[32,2048]{1,0:T(8,128)S(1)}, f32[32,2048]{1,0:T(8,128)S(1)}, u32[]{:S(2)}, u32[]{:S(2)}) collective-permute-start(f32[32,2048]{1,0:T(8,128)S(1)} %subtract_divide_fusion), channel_id=1, source_target_pairs={{0,8},{8,16},{16,24},{24,32},{32,40},{40,48},{48,56},{56,64},{64,7... | collective-permute-start | bytes 786440 | tf_op jit(solution)/shard_map/ppermute | solution.py:13
  62.3 11.5 %collective-permute-start.3 = (f32[32,2048]{1,0:T(8,128)S(1)}, f32[32,2048]{1,0:T(8,128)S(1)}, u32[]{:S(2)}, u32[]{:S(2)}) collective-permute-start(f32[32,2048]{1,0:T(8,128)S(1)} %subtract_divide_fusion), channel_id=1, source_target_pairs={{8,0},{16,8},{24,16},{32,24},{40,32},{48,40},{56,48},{64,56},{72,6... | collective-permute-start | bytes 786440 | tf_op jit(solution)/shard_map/ppermute | solution.py:16
  104.1 12.7 %copy-start.1 = (f32[32,2048]{1,0:T(8,128)}, f32[32,2048]{1,0:T(8,128)S(1)}, u32[]{:S(2)}) copy-start(f32[32,2048]{1,0:T(8,128)S(1)} %divide_subtract_fusion.1) | copy-start | bytes 786436
  104.1 11.7 %collective-permute-start.4 = (f32[32,2048]{1,0:T(8,128)S(1)}, f32[32,2048]{1,0:T(8,128)S(1)}, u32[]{:S(2)}, u32[]{:S(2)}) collective-permute-start(f32[32,2048]{1,0:T(8,128)S(1)} %divide_subtract_fusion.1), channel_id=1, source_target_pairs={{0,8},{8,16},{16,24},{24,32},{32,40},{40,48},{48,56},{56,64},{64,7... | collective-permute-start | bytes 786440 | tf_op jit(solution)/shard_map/ppermute | solution.py:13
  106.0 10.7 %collective-permute-start.5 = (f32[32,2048]{1,0:T(8,128)S(1)}, f32[32,2048]{1,0:T(8,128)S(1)}, u32[]{:S(2)}, u32[]{:S(2)}) collective-permute-start(f32[32,2048]{1,0:T(8,128)S(1)} %divide_subtract_fusion.1), channel_id=1, source_target_pairs={{8,0},{16,8},{24,16},{32,24},{40,32},{48,40},{56,48},{64,56},{72,6... | collective-permute-start | bytes 786440 | tf_op jit(solution)/shard_map/ppermute | solution.py:16
  147.8 14.0 %all-to-all-start = ((f32[32,8,256]{2,0,1:T(8,128)}), f32[32,8,256]{2,0,1:T(8,128)S(1)}, u32[]{:S(2)}, u32[]{:S(2)}) async-start(f32[32,8,256]{2,0,1:T(8,128)} %bitcast.65), calls=%async_computation | async-start | bytes 524288 | tf_op jit(solution)/shard_map/all_to_all | solution.py:45
  155.3 273.8 %all-reduce.3.cloned.1.call-start = ((), (), s32[]{:S(2)}) async-start(), calls=%async_computation.1 | async-start | bytes 524288 | tf_op jit(solution)/shard_map/psum | solution.py:49
  431.1 0.7 copy-start.3
  443.5 0.6 copy-start.4
  473.8 2.0 copy-start.2
Sparse Core Ops, SparseCore 0:
  163.0 265.9 all-reduce.2
where the time goes:
time: 525 us; the launch traced here: 516 us
  waiting for transfers between devices  279 us (53%)
  other arithmetic  77.2 us (15%)
  local copies, waits for them, and re-layouts  74.4 us (14%)
  starting transfers between devices  43.7 us (8%)
  matrix products  23.4 us (4%)
  between operations  18.4 us (4%)
    psum x1, waiting for transfers between devices, local(): gram = lax.psum(gram, ('row', 'bundle'))  265 us
    another operation x6, other arithmetic, local(): lower = jnp.linalg.cholesky(gram)  38.4 us
    ppermute x3, starting transfers between devices, extended_2(): lax.ppermute(lax.slice_in_dim(block, 0, width, axis=dim), axis, backward)  27.8 us
    another operation x3, other arithmetic, local(): basis = jax.scipy.linalg.solve_triangular(lower, stacked, lower=True)  21.8 us
    reshape x6, local copies, waits for them, and re-layouts, apply_operator(): extended3 = extended.reshape(width, 3 * block_rows, block_size)  19.2 us
    dot_general x3, matrix products, apply_operator(): jnp.einsum('iam,cim->cia', blocks, picked, precision=lax.Precision.HIGHEST)  16.8 us
    gather x3, local copies, waits for them, and re-layouts, apply_operator(): jnp.take(extended3, local_cols, axis=1)  11.4 us
    reshape x3, local copies, waits for them, and re-layouts, apply_operator(): jnp.take(extended3, local_cols, axis=1)  11.3 us
  transfers between devices with their start and end apart: 8, of which 7 were waited for; matrix products, arithmetic and copies ran while one was open for 1% of the time, Pallas kernels for 0%

commit v1 on v0

v1 whole, which is shorter than its diff:
```python
import functools

import jax
import jax.numpy as jnp
from jax import lax
from jax.experimental import pallas as pl
from jax.experimental.pallas import tpu as pltpu
from jax.sharding import PartitionSpec as P

BF = jnp.bfloat16
F32 = jnp.float32
HIGHEST = lax.Precision.HIGHEST
VMEM = pl.BlockSpec(memory_space=pltpu.VMEM)
SMEM = pl.BlockSpec(memory_space=pltpu.SMEM)
NB = 64
PIV = 4


def split(x):
    hi = x.astype(BF)
    lo = (x - hi.astype(F32)).astype(BF)
    return hi, lo


def dot_nt(a, b):
    return lax.dot_general(a, b, (((1,), (1,)), ((), ())), preferred_element_type=F32)


def split_kernel(b_ref, w_ref):
    hi, lo = split(b_ref[...])
    w_ref[:, 0:64, :] = hi
    w_ref[:, 64:128, :] = lo


def split_blocks(blocks):
    n, a, m = blocks.shape
    step = 8
    return pl.pallas_call(
        split_kernel,
        out_shape=jax.ShapeDtypeStruct((n, 2 * a, m), BF),
        grid=(n // step,),
        in_specs=[pl.BlockSpec((step, a, m), lambda i: (i, 0, 0))],
        out_specs=pl.BlockSpec((step, 2 * a, m), lambda i: (i, 0, 0)),
        name="split_blocks",
    )(blocks)


def apply_kernel(stage, total_rows, cols_ref, base_ref, bounds_ref, *refs):
    if stage == 0:
        f_ref, low_ref, high_ref, w_ref, out_ref, ehi, elo = refs
        prev_ref = None
    else:
        f_ref, low_ref, high_ref, prev_ref, w_ref, out_ref, ehi, elo = refs
    width = f_ref.shape[0]
    tiles = f_ref.shape[1] // 128

    for part, ref in enumerate((low_ref, f_ref, high_ref)):

        def build(t, carry, part=part, ref=ref):
            x = ref[:, pl.ds(pl.multiple_of(t * 128, 128), 128)]
            hi, lo = split(x)
            swapped = pltpu.roll(x, 64, 1)
            shi, slo = split(swapped)
            ehi[0, part * tiles + t] = hi
            elo[0, part * tiles + t] = lo
            ehi[1, part * tiles + t] = shi
            elo[1, part * tiles + t] = slo
            return carry

        lax.fori_loop(0, tiles, build, 0, unroll=4)

    base = base_ref[0]
    center = (bounds_ref[0] + bounds_ref[1]) * 0.5
    half = (bounds_ref[1] - bounds_ref[0]) * 0.5
    left_b = lax.broadcasted_iota(jnp.int32, (width, 128), 1) < 64
    slots = cols_ref.shape[1]

    def one(i):
        his, los = [], []
        for sp in range(slots // 2):
            ca = (cols_ref[i, 2 * sp] - base) & (total_rows - 1)
            cb = (cols_ref[i, 2 * sp + 1] - base) & (total_rows - 1)
            ta, va = ca >> 1, ca & 1
            tb, vb = cb >> 1, 1 - (cb & 1)
            his.append(jnp.where(left_b, ehi[va, ta], ehi[vb, tb]))
            los.append(jnp.where(left_b, elo[va, ta], elo[vb, tb]))
        lhs = jnp.concatenate(
            [jnp.concatenate(his, axis=1), jnp.concatenate(los, axis=1)], axis=0
        )
        out = dot_nt(lhs, w_ref[i])
        acc = out[:width] + jnp.where(left_b, out[width:], 0.0)
        return acc + pltpu.roll(acc, 64, 1)

    def pair(g, carry):
        y = jnp.where(left_b, one(2 * g), one(2 * g + 1))
        lanes = pl.ds(pl.multiple_of(g * 128, 128), 128)
        f = f_ref[:, lanes]
        r = (y - center * f) / half
        if stage > 0:
            r = 2.0 * r - prev_ref[:, lanes]
        if stage < 2:
            out_ref[:, lanes] = r
        else:
            out_ref[g] = r
        return carry

    lax.fori_loop(0, tiles, pair, 0, unroll=4)


def apply_step(stage, total_rows, cols, base, bounds, f, low, high, prev, w):
    width, n = f.shape
    tiles = n // 128
    args = (f, low, high) + (() if prev is None else (prev,)) + (w,)
    out = (width, n) if stage < 2 else (tiles, width, 128)
    return pl.pallas_call(
        functools.partial(apply_kernel, stage, total_rows),
        out_shape=jax.ShapeDtypeStruct(out, F32),
        in_specs=[SMEM] * 3 + [VMEM] * len(args),
        out_specs=VMEM,
        scratch_shapes=[pltpu.VMEM((2, 3 * tiles, width, 128), BF)] * 2,
        name=f"apply_{stage}",
    )(cols, base, bounds, *args)


def gram_kernel(s_ref, out_ref):
    s = jnp.concatenate(
        [
            s_ref[:, j].reshape(s_ref.shape[0] * s_ref.shape[2], 128)
            for j in range(s_ref.shape[1])
        ],
        axis=1,
    )
    g = lax.dot_general(
        s, s, (((1,), (1,)), ((), ())), precision=HIGHEST, preferred_element_type=F32
    )
    k = g.shape[0]
    for j in range(k // 128):
        out_ref[j] = g[:, j * 128 : (j + 1) * 128].reshape(k // 8, 8, 128)


def gram_tiles(s):
    k = s.shape[0] * s.shape[2]
    return pl.pallas_call(
        gram_kernel,
        out_shape=jax.ShapeDtypeStruct((k // 128, k // 8, 8, 128), F32),
        in_specs=[VMEM],
        out_specs=VMEM,
        name="gram",
    )(s)


def factor_block(m):
    n = m.shape[0]
    lane = lax.broadcasted_iota(jnp.int32, (8, 128), 1)
    sub = lax.broadcasted_iota(jnp.int32, (n, 128), 0)
    vregs = [m[8 * v : 8 * v + 8] for v in range(n // 8)]
    sub8 = lax.broadcasted_iota(jnp.int32, (8, 128), 0)
    done = [jnp.zeros((8, 128), F32) for _ in range(n // 8)]
    for j in range(0, n, PIV):
        v0 = j // 8
        rows = [
            jnp.broadcast_to(vregs[v0][j - 8 * v0 + k : j - 8 * v0 + k + 1, :], (8, 128))
            for k in range(PIV)
        ]
        p = {
            (k, c): jnp.broadcast_to(rows[k][:, j + c : j + c + 1], (8, 128))
            for k in range(PIV)
            for c in range(k, PIV)
        }
        cols = [
            [jnp.broadcast_to(vregs[v][:, j + c : j + c + 1], (8, 128)) for c in range(PIV)]
            for v in range(v0, n // 8)
        ]
        inv = []
        mult = {}
        for k in range(PIV):
            inv.append(1.0 / p[k, k])
            for r in range(k + 1, PIV):
                f = p[k, r] * inv[k]
                mult[r, k] = f
                for c in range(r, PIV):
                    p[r, c] = p[r, c] - f * p[k, c]
                rows[r] = rows[r] - f * rows[k]
        for k in range(PIV):
            u = rows[k] * lax.rsqrt(p[k, k])
            done[v0] = jnp.where(sub8 == j - 8 * v0 + k, u, done[v0])
        z = [rows[k] * inv[k] for k in range(PIV)]
        for k in range(PIV - 1, -1, -1):
            for r in range(k):
                z[r] = z[r] - mult[k, r] * z[k]
        for v in range(v0, n // 8):
            c = cols[v - v0]
            vregs[v] = vregs[v] - (
                (c[0] * z[0] + c[1] * z[1]) + (c[2] * z[2] + c[3] * z[3])
            )
    return jnp.concatenate(done, axis=0)


def solve_kernel(g_ref, s_ref, basis_ref, factor_ref, a_ref):
    k = factor_ref.shape[0]
    halves = k // 128
    for j in range(halves):
        a_ref[:, j * 128 : (j + 1) * 128] = g_ref[j].reshape(k, 128)
    for j in range(s_ref.shape[1]):
        a_ref[:, k + j * 128 : k + (j + 1) * 128] = s_ref[:, j].reshape(k, 128)
    total = a_ref.shape[1]
    lane = lax.broadcasted_iota(jnp.int32, (NB, 128), 1)
    sub = lax.broadcasted_iota(jnp.int32, (NB, 128), 0)
    eye = jnp.where(lane == sub + NB, 1.0, 0.0)

    def step(b, carry):
        first = pl.multiple_of(b * NB, NB)
        rows = pl.ds(first, NB)
        tile = a_ref[rows, pl.ds(pl.multiple_of((b // 2) * 128, 128), 128)]
        tile = jnp.where(b % 2 == 1, pltpu.roll(tile, NB, 1), tile)
        u = factor_block(jnp.where(lane < NB, tile, eye))
        linv = pltpu.roll(u, NB, 1)[:, :NB]
        x = lax.dot_general(
            linv,
            a_ref[rows, :],
            (((1,), (0,)), ((), ())),
            precision=HIGHEST,
            preferred_element_type=F32,
        )
        row_id = first + lax.broadcasted_iota(jnp.int32, (NB, k), 0)
        col_id = lax.broadcasted_iota(jnp.int32, (NB, k), 1)
        factor_ref[rows, :] = jnp.where(col_id >= row_id, x[:, :k], 0.0)
        basis_ref[rows, :] = x[:, k:]
        later = jnp.where(col_id >= first + NB, x[:, :k], 0.0)
        a_ref[...] -= lax.dot_general(
            later,
            x,
            (((0,), (0,)), ((), ())),
            precision=HIGHEST,
            preferred_element_type=F32,
        )
        return carry

    lax.fori_loop(0, k // NB, step, 0)


def orthonormalize(g, s):
    k = s.shape[0] * s.shape[2]
    n = s.shape[1] * 128
    return pl.pallas_call(
        solve_kernel,
        out_shape=(
            jax.ShapeDtypeStruct((k, n), F32),
            jax.ShapeDtypeStruct((k, k), F32),
        ),
        in_specs=[VMEM, VMEM],
        out_specs=(VMEM, VMEM),
        scratch_shapes=[pltpu.VMEM((k, k + n), F32)],
        name="orthonormalize",
    )(g, s)


def sum_over_devices(tiles):
    shape = tiles.shape
    rows = lax.axis_size("row")
    bundles = lax.axis_size("bundle")
    parts = lax.all_to_all(
        tiles.reshape(rows, -1, 128), "row", split_axis=0, concat_axis=0, tiled=True
    )
    mine = jnp.sum(parts, axis=0)
    parts = lax.all_to_all(
        jnp.broadcast_to(mine[None], (bundles,) + mine.shape),
        "bundle",
        split_axis=0,
        concat_axis=0,
        tiled=True,
    )
    mine = jnp.sum(parts, axis=0)
    parts = lax.all_to_all(
        jnp.broadcast_to(mine[None], (rows,) + mine.shape),
        "row",
        split_axis=0,
        concat_axis=0,
        tiled=True,
    )
    return parts.reshape(shape)


def local(vectors, blocks, columns, bounds):
    block_rows = blocks.shape[0]
    row_count = lax.axis_size("row")
    bundles = lax.axis_size("bundle")
    total_rows = block_rows * row_count
    base = ((lax.axis_index("row") - 1) * block_rows).astype(jnp.int32).reshape(1)
    forward = [(i, (i + 1) % row_count) for i in range(row_count)]
    backward = [(j, i) for i, j in forward]

    def sides(field):
        return (
            lax.ppermute(field, "row", forward),
            lax.ppermute(field, "row", backward),
        )

    low, high = sides(vectors)
    w = split_blocks(blocks)
    first = apply_step(
        0, total_rows, columns, base, bounds, vectors, low, high, None, w
    )
    low, high = sides(first)
    second = apply_step(
        1, total_rows, columns, base, bounds, first, low, high, vectors, w
    )
    low, high = sides(second)
    filtered = apply_step(
        2, total_rows, columns, base, bounds, second, low, high, first, w
    )
    tiles, width, lanes = filtered.shape
    stacked = lax.all_to_all(
        filtered.reshape(bundles, tiles // bundles, width, lanes),
        "bundle",
        split_axis=0,
        concat_axis=0,
        tiled=True,
    )
    gram = sum_over_devices(gram_tiles(stacked))
    return orthonormalize(gram, stacked)


def solution(mesh):
    placed = (P("bundle", "row"), P("row", None, None), P("row", None), P())
    return jax.shard_map(
        local,
        mesh=mesh,
        in_specs=placed,
        out_specs=(P(None, ("row", "bundle")), P()),
        check_vma=False,
    )
```

time: 525 us -> 155 us (0.30); the launches traced: 516 us -> 153 us
  waiting for transfers between devices: 279 us -> 20.4 us
  other arithmetic: 77.2 us -> 0.08 us
  local copies, waits for them, and re-layouts: 74.4 us -> 3.51 us
  blocking collectives: 0 us -> 59.6 us
  Pallas kernels: 0 us -> 42.3 us
  matrix products: 23.4 us -> 0 us
  between operations: 18.4 us -> 0.7 us
  starting transfers between devices: 43.7 us -> 26.9 us
    psum x1 -> x0, waiting for transfers between devices: 265 us -> none  [local(): gram = lax.psum(gram, ('row', 'bundle'))]
    another operation x9 -> x0, other arithmetic: 60.2 us -> none  [the longest x6 38.4 us: local(): lower = jnp.linalg.cholesky(gram)]
    all_to_all x0 -> x4, blocking collectives: none -> 59.6 us  [the longest x1 17.4 us: sum_over_devices(): lax.all_to_all(jnp.broadcast_to(mine[None], (rows,) + mine.shape), 'row',...]
    pallas_call x0 -> x6, Pallas kernels: none -> 42.3 us  [the longest x3 18.4 us: apply_step(): pl.pallas_call(functools.partial(apply_kernel, stage, total_rows), out_sh...]
    reshape x13 -> x0, local copies, waits for them, and re-layouts: 36.4 us -> none  [the longest x6 19.2 us: apply_operator(): extended3 = extended.reshape(width, 3 * block_rows, block_size)]
    dot_general x4 -> x0, matrix products: 17.9 us -> none  [the longest x3 16.8 us: apply_operator(): jnp.einsum('iam,cim->cia', blocks, picked, precision=lax.Precision.HIGHEST)]
    ppermute x6, waiting for transfers between devices: 7.15 us -> 20.4 us  [the longest x3 15.5 us: sides(): lax.ppermute(field, 'row', forward)]
    gather x3 -> x0, local copies, waits for them, and re-layouts: 11.4 us -> none  [apply_operator(): jnp.take(extended3, local_cols, axis=1)]
  transfers between devices with their start and end apart: 8 -> 6, of which waited for: 7 -> 5; matrix products, arithmetic and copies ran while one was open for 1% -> 1% of each run, Pallas kernels for 0% -> 3%
where the time goes in v1:
time: 155 us; the launch traced here: 153 us
  blocking collectives  59.6 us (38%)
  Pallas kernels  42.3 us (27%)
  starting transfers between devices  26.9 us (17%)
  waiting for transfers between devices  20.4 us (13%)
  local copies, waits for them, and re-layouts  3.51 us (2%)
    pallas_call x3, Pallas kernels, apply_step(): pl.pallas_call(functools.partial(apply_kernel, stage, total_rows), out_sh...  18.4 us
    ppermute x3, starting transfers between devices, sides(): lax.ppermute(field, 'row', backward)  18.3 us
    pallas_call x1, Pallas kernels, orthonormalize(): pl.pallas_call(solve_kernel, out_shape=(jax.ShapeDtypeStruct((k, n), F32)...  17.4 us
    all_to_all x1, blocking collectives, sum_over_devices(): lax.all_to_all(jnp.broadcast_to(mine[None], (rows,) + mine.shape), 'row',...  17.4 us
    all_to_all x1, blocking collectives, sum_over_devices(): lax.all_to_all(tiles.reshape(rows, -1, 128), 'row', split_axis=0, concat_...  17.4 us
    ppermute x3, waiting for transfers between devices, sides(): lax.ppermute(field, 'row', forward)  15.5 us
    all_to_all x1, blocking collectives, local(): lax.all_to_all(filtered.reshape(bundles, tiles // bundles, width, lanes),...  14.5 us
    all_to_all x1, blocking collectives, sum_over_devices(): lax.all_to_all(jnp.broadcast_to(mine[None], (bundles,) + mine.shape), 'bu...  10.3 us
  transfers between devices with their start and end apart: 6, of which 5 were waited for; matrix products, arithmetic and copies ran while one was open for 1% of the time, Pallas kernels for 3%

profile of v1, /device:TPU:1, one launch (start us, length us, event | category | flops | bytes accessed | tf_op | source)
XLA Modules:
  0.0 153.4 jit_solution(16257283933715469342)
XLA Ops:
  0.6 14.4 %collective-permute-start.1 = (f32[32,2048]{1,0:T(8,128)}, f32[32,2048]{1,0:T(8,128)S(1)}, u32[]{:S(2)}, u32[]{:S(2)}) collective-permute-start(f32[32,2048]{1,0:T(8,128)} %refs_3_.1), channel_id=1, source_target_pairs={{8,0},{16,8},{24,16},{32,24},{40,32},{48,40},{56,48},{64,56},{72,6... | collective-permute-start | bytes 786440 | tf_op jit(solution)/shard_map/ppermute | solution.py:296
  15.0 1.9 %collective-permute-start = (f32[32,2048]{1,0:T(8,128)}, f32[32,2048]{1,0:T(8,128)S(1)}, u32[]{:S(2)}, u32[]{:S(2)}) collective-permute-start(f32[32,2048]{1,0:T(8,128)} %refs_3_.1), channel_id=1, source_target_pairs={{0,8},{8,16},{16,24},{24,32},{32,40},{40,48},{48,56},{56,64},{64,7... | collective-permute-start | bytes 786440 | tf_op jit(solution)/shard_map/ppermute | solution.py:295
  17.0 1.4 copy.11.cols_ref
  18.3 4.3 %split_blocks.1.refs_3_.refs_4_ = bf16[32,128,384]{2,1,0:T(8,128)(2,1)} custom-call(f32[32,64,384]{2,1,0:T(8,128)} %b_ref.1), custom_call_target="tpu_custom_call" | custom-call | tf_op jit(solution)/shard_map/split_blocks/pallas_call | solution.py:38
  22.7 4.7 %collective-permute-done.refs_1_ = f32[32,2048]{1,0:T(8,128)S(1)} collective-permute-done((f32[32,2048]{1,0:T(8,128)}, f32[32,2048]{1,0:T(8,128)S(1)}, u32[]{:S(2)}, u32[]{:S(2)}) %collective-permute-start) | collective-permute-done | bytes 262176 | tf_op jit(solution)/shard_map/ppermute | solution.py:295
  28.1 6.1 %apply_0.1.refs_0_.refs_3_ = f32[32,2048]{1,0:T(8,128)} custom-call(s32[32,6]{1,0:T(8,128)} %copy.11.cols_ref, s32[1]{0:T(128)} %bitcast.base_ref, f32[2]{0:T(128)} %bounds_ref.5, f32[32,2048]{1,0:T(8,128)} %refs_3_.1, f32[32,2048]{1,0:T(8,128)} %copy-done.1, f32[32,2048]{1,0:T(8,128)} %copy-done, bf16[32,128,384]{2,1,0:T(8,128)(2,1)} %split_blocks.1.refs_3_.refs_4_), custom_call_target="tpu_custom_call" | custom-call | tf_op jit(solution)/shard_map/apply_0/pallas_call | solution.py:115
  34.1 2.0 %collective-permute-start.3 = (f32[32,2048]{1,0:T(8,128)}, f32[32,2048]{1,0:T(8,128)S(1)}, u32[]{:S(2)}, u32[]{:S(2)}) collective-permute-start(f32[32,2048]{1,0:T(8,128)} %apply_0.1.refs_0_.refs_3_), channel_id=1, source_target_pairs={{8,0},{16,8},{24,16},{32,24},{40,32},{48,40},{56,48},{64,56},{72,6... | collective-permute-start | bytes 786440 | tf_op jit(solution)/shard_map/ppermute | solution.py:296
  36.2 3.2 %collective-permute-start.2 = (f32[32,2048]{1,0:T(8,128)}, f32[32,2048]{1,0:T(8,128)S(1)}, u32[]{:S(2)}, u32[]{:S(2)}) collective-permute-start(f32[32,2048]{1,0:T(8,128)} %apply_0.1.refs_0_.refs_3_), channel_id=1, source_target_pairs={{0,8},{8,16},{16,24},{24,32},{32,40},{40,48},{48,56},{56,64},{64,7... | collective-permute-start | bytes 786440 | tf_op jit(solution)/shard_map/ppermute | solution.py:295
  39.4 2.9 %collective-permute-done.3.refs_2_ = f32[32,2048]{1,0:T(8,128)S(1)} collective-permute-done((f32[32,2048]{1,0:T(8,128)}, f32[32,2048]{1,0:T(8,128)S(1)}, u32[]{:S(2)}, u32[]{:S(2)}) %collective-permute-start.3) | collective-permute-done | bytes 262176 | tf_op jit(solution)/shard_map/ppermute | solution.py:296
  42.3 5.5 %collective-permute-done.2.refs_1_ = f32[32,2048]{1,0:T(8,128)S(1)} collective-permute-done((f32[32,2048]{1,0:T(8,128)}, f32[32,2048]{1,0:T(8,128)S(1)}, u32[]{:S(2)}, u32[]{:S(2)}) %collective-permute-start.2) | collective-permute-done | bytes 262176 | tf_op jit(solution)/shard_map/ppermute | solution.py:295
  47.8 0.7 copy-done.5
  48.5 6.2 %apply_1.1.refs_0_ = f32[32,2048]{1,0:T(8,128)} custom-call(s32[32,6]{1,0:T(8,128)} %copy.11.cols_ref, s32[1]{0:T(128)} %bitcast.base_ref, f32[2]{0:T(128)} %bounds_ref.5, f32[32,2048]{1,0:T(8,128)} %apply_0.1.refs_0_.refs_3_, f32[32,2048]{1,0:T(8,128)} %copy-done.5, f32[32,2048]{1,0:T(8,128)} %copy-done.4, f32[32,2048]{1,0:T(8,128)} %refs_3_.1, ...), custom_call_target="tpu_custom_call" | custom-call | tf_op jit(solution)/shard_map/apply_1/pallas_call | solution.py:115
  54.7 1.9 %collective-permute-start.5 = (f32[32,2048]{1,0:T(8,128)}, f32[32,2048]{1,0:T(8,128)S(1)}, u32[]{:S(2)}, u32[]{:S(2)}) collective-permute-start(f32[32,2048]{1,0:T(8,128)} %apply_1.1.refs_0_), channel_id=1, source_target_pairs={{8,0},{16,8},{24,16},{32,24},{40,32},{48,40},{56,48},{64,56},{72,6... | collective-permute-start | bytes 786440 | tf_op jit(solution)/shard_map/ppermute | solution.py:296
  56.6 3.4 %collective-permute-start.4 = (f32[32,2048]{1,0:T(8,128)}, f32[32,2048]{1,0:T(8,128)S(1)}, u32[]{:S(2)}, u32[]{:S(2)}) collective-permute-start(f32[32,2048]{1,0:T(8,128)} %apply_1.1.refs_0_), channel_id=1, source_target_pairs={{0,8},{8,16},{16,24},{24,32},{32,40},{40,48},{48,56},{56,64},{64,7... | collective-permute-start | bytes 786440 | tf_op jit(solution)/shard_map/ppermute | solution.py:295
  60.0 2.0 %collective-permute-done.5.refs_2_ = f32[32,2048]{1,0:T(8,128)S(1)} collective-permute-done((f32[32,2048]{1,0:T(8,128)}, f32[32,2048]{1,0:T(8,128)S(1)}, u32[]{:S(2)}, u32[]{:S(2)}) %collective-permute-start.5) | collective-permute-done | bytes 262176 | tf_op jit(solution)/shard_map/ppermute | solution.py:296
  62.0 5.2 %collective-permute-done.4.refs_1_ = f32[32,2048]{1,0:T(8,128)S(1)} collective-permute-done((f32[32,2048]{1,0:T(8,128)}, f32[32,2048]{1,0:T(8,128)S(1)}, u32[]{:S(2)}, u32[]{:S(2)}) %collective-permute-start.4) | collective-permute-done | bytes 262176 | tf_op jit(solution)/shard_map/ppermute | solution.py:295
  67.3 0.7 copy-done.3
  68.0 6.2 %apply_2.1 = f32[16,32,128]{2,1,0:T(8,128)} custom-call(s32[32,6]{1,0:T(8,128)} %copy.11.cols_ref, s32[1]{0:T(128)} %bitcast.base_ref, f32[2]{0:T(128)} %bounds_ref.5, f32[32,2048]{1,0:T(8,128)} %apply_1.1.refs_0_, f32[32,2048]{1,0:T(8,128)} %copy-done.3, f32[32,2048]{1,0:T(8,128)} %copy-done.2, f32[32,2048]{1,0:T(8,128)} %apply_0.1.refs_0_.refs_3_, ...), custom_call_target="tpu_custom_call" | custom-call | tf_op jit(solution)/shard_map/apply_2/pallas_call | solution.py:115
  74.1 14.5 %all_to_all.20.s_ref = f32[8,2,32,128]{3,2,1,0:T(8,128)} all-to-all(f32[8,2,32,128]{3,2,1,0:T(8,128)} %bitcast.4), channel_id=1, replica_groups=mesh['row'=64,'bundle'=8] {'bundle'}, dimensions={0} | all-to-all | bytes 524288 | tf_op jit(solution)/shard_map/all_to_all | solution.py:313
  88.7 2.1 %gram.1 = f32[2,32,8,128]{3,2,1,0:T(8,128)} custom-call(f32[8,2,32,128]{3,2,1,0:T(8,128)} %all_to_all.20.s_ref), custom_call_target="tpu_custom_call" | custom-call | tf_op jit(solution)/shard_map/gram/pallas_call | solution.py:143
  90.7 17.4 %all_to_all.21 = f32[64,8,128]{2,1,0:T(8,128)S(1)} all-to-all(f32[64,8,128]{2,1,0:T(8,128)} %bitcast.6), channel_id=1, replica_groups=mesh['row'=64,'bundle'=8] {'row'}, dimensions={0} | all-to-all | bytes 524288 | tf_op jit(solution)/shard_map/all_to_all | solution.py:262
  108.2 10.3 %all_to_all.22 = f32[8,8,128]{2,1,0:T(8,128)S(1)} all-to-all(f32[8,8,128]{2,1,0:T(8,128)S(1)} %broadcast_in_dim.4), channel_id=1, replica_groups=mesh['row'=64,'bundle'=8] {'bundle'}, dimensions={0} | all-to-all | bytes 65536 | tf_op jit(solution)/shard_map/all_to_all | solution.py:266
  118.5 17.4 %all_to_all.23 = f32[64,8,128]{2,1,0:T(8,128)} all-to-all(f32[64,8,128]{2,1,0:T(8,128)S(1)} %broadcast_in_dim.5), channel_id=1, replica_groups=mesh['row'=64,'bundle'=8] {'row'}, dimensions={0} | all-to-all | bytes 524288 | tf_op jit(solution)/shard_map/all_to_all | solution.py:274
  135.9 17.4 %orthonormalize.1 = (f32[256,256]{1,0:T(8,128)}, f32[256,256]{1,0:T(8,128)}) custom-call(f32[2,32,8,128]{3,2,1,0:T(8,128)} %bitcast.5, f32[8,2,32,128]{3,2,1,0:T(8,128)} %all_to_all.20.s_ref), custom_call_target="tpu_custom_call" | custom-call | tf_op jit(solution)/shard_map/orthonormalize/pallas_call | solution.py:245
  (15 shorter events, 0.8 us)
Async XLA Ops:
  0.6 22.0 %collective-permute-start.1 = (f32[32,2048]{1,0:T(8,128)}, f32[32,2048]{1,0:T(8,128)S(1)}, u32[]{:S(2)}, u32[]{:S(2)}) collective-permute-start(f32[32,2048]{1,0:T(8,128)} %refs_3_.1), channel_id=1, source_target_pairs={{8,0},{16,8},{24,16},{32,24},{40,32},{48,40},{56,48},{64,56},{72,6... | collective-permute-start | bytes 786440 | tf_op jit(solution)/shard_map/ppermute | solution.py:296
  15.0 12.3 %collective-permute-start = (f32[32,2048]{1,0:T(8,128)}, f32[32,2048]{1,0:T(8,128)S(1)}, u32[]{:S(2)}, u32[]{:S(2)}) collective-permute-start(f32[32,2048]{1,0:T(8,128)} %refs_3_.1), channel_id=1, source_target_pairs={{0,8},{8,16},{16,24},{24,32},{32,40},{40,48},{48,56},{56,64},{64,7... | collective-permute-start | bytes 786440 | tf_op jit(solution)/shard_map/ppermute | solution.py:295
  22.7 4.7 %copy-start = (f32[32,2048]{1,0:T(8,128)}, f32[32,2048]{1,0:T(8,128)S(1)}, u32[]{:S(2)}) copy-start(f32[32,2048]{1,0:T(8,128)S(1)} %collective-permute-done.1.refs_2_) | copy-start | bytes 786436
  27.4 0.7 copy-start.1
  34.1 8.1 %collective-permute-start.3 = (f32[32,2048]{1,0:T(8,128)}, f32[32,2048]{1,0:T(8,128)S(1)}, u32[]{:S(2)}, u32[]{:S(2)}) collective-permute-start(f32[32,2048]{1,0:T(8,128)} %apply_0.1.refs_0_.refs_3_), channel_id=1, source_target_pairs={{8,0},{16,8},{24,16},{32,24},{40,32},{48,40},{56,48},{64,56},{72,6... | collective-permute-start | bytes 786440 | tf_op jit(solution)/shard_map/ppermute | solution.py:296
  36.2 11.6 %collective-permute-start.2 = (f32[32,2048]{1,0:T(8,128)}, f32[32,2048]{1,0:T(8,128)S(1)}, u32[]{:S(2)}, u32[]{:S(2)}) collective-permute-start(f32[32,2048]{1,0:T(8,128)} %apply_0.1.refs_0_.refs_3_), channel_id=1, source_target_pairs={{0,8},{8,16},{16,24},{24,32},{32,40},{40,48},{48,56},{56,64},{64,7... | collective-permute-start | bytes 786440 | tf_op jit(solution)/shard_map/ppermute | solution.py:295
  42.3 5.5 %copy-start.4 = (f32[32,2048]{1,0:T(8,128)}, f32[32,2048]{1,0:T(8,128)S(1)}, u32[]{:S(2)}) copy-start(f32[32,2048]{1,0:T(8,128)S(1)} %collective-permute-done.3.refs_2_) | copy-start | bytes 786436
  47.8 0.7 copy-start.5
  54.7 7.3 %collective-permute-start.5 = (f32[32,2048]{1,0:T(8,128)}, f32[32,2048]{1,0:T(8,128)S(1)}, u32[]{:S(2)}, u32[]{:S(2)}) collective-permute-start(f32[32,2048]{1,0:T(8,128)} %apply_1.1.refs_0_), channel_id=1, source_target_pairs={{8,0},{16,8},{24,16},{32,24},{40,32},{48,40},{56,48},{64,56},{72,6... | collective-permute-start | bytes 786440 | tf_op jit(solution)/shard_map/ppermute | solution.py:296
  56.6 10.6 %collective-permute-start.4 = (f32[32,2048]{1,0:T(8,128)}, f32[32,2048]{1,0:T(8,128)S(1)}, u32[]{:S(2)}, u32[]{:S(2)}) collective-permute-start(f32[32,2048]{1,0:T(8,128)} %apply_1.1.refs_0_), channel_id=1, source_target_pairs={{0,8},{8,16},{16,24},{24,32},{32,40},{40,48},{48,56},{56,64},{64,7... | collective-permute-start | bytes 786440 | tf_op jit(solution)/shard_map/ppermute | solution.py:295
  62.0 5.2 %copy-start.2 = (f32[32,2048]{1,0:T(8,128)}, f32[32,2048]{1,0:T(8,128)S(1)}, u32[]{:S(2)}) copy-start(f32[32,2048]{1,0:T(8,128)S(1)} %collective-permute-done.5.refs_2_) | copy-start | bytes 786436
  67.3 0.7 copy-start.3

commit v2 on v1

v2 whole, which is shorter than its diff:
```python
import functools

import jax
import jax.numpy as jnp
from jax import lax
from jax.experimental import pallas as pl
from jax.experimental.pallas import tpu as pltpu
from jax.sharding import PartitionSpec as P

BF = jnp.bfloat16
F32 = jnp.float32
HIGHEST = lax.Precision.HIGHEST
VMEM = pl.BlockSpec(memory_space=pltpu.VMEM)
SMEM = pl.BlockSpec(memory_space=pltpu.SMEM)
NB = 64
BUILD_UNROLL = 8
PAIR_UNROLL = 8
PARAMS = pltpu.CompilerParams(vmem_limit_bytes=20 * 1024 * 1024)


def near(x):
    return pltpu.with_memory_space_constraint(x, pltpu.VMEM)


def split(x):
    hi = x.astype(BF)
    lo = (x - hi.astype(F32)).astype(BF)
    return hi, lo


def dot_nt(a, b):
    return lax.dot_general(a, b, (((1,), (1,)), ((), ())), preferred_element_type=F32)


def split_kernel(b_ref, w_ref):
    hi, lo = split(b_ref[...])
    w_ref[:, 0:64, :] = hi
    w_ref[:, 64:128, :] = lo


def split_blocks(blocks):
    n, a, m = blocks.shape
    step = 8
    return pl.pallas_call(
        split_kernel,
        out_shape=pltpu.VMEM((n, 2 * a, m), BF),
        grid=(n // step,),
        in_specs=[pl.BlockSpec((step, a, m), lambda i: (i, 0, 0))],
        out_specs=pl.BlockSpec((step, 2 * a, m), lambda i: (i, 0, 0)),
        compiler_params=PARAMS,
        name="split_blocks",
    )(blocks)


def apply_kernel(stage, slot_ref, bounds_ref, *refs):
    if stage == 0:
        f_ref, low_ref, high_ref, w_ref, out_ref, e_ref = refs
        prev_ref = None
    else:
        f_ref, low_ref, high_ref, prev_ref, w_ref, out_ref, e_ref = refs
    width = f_ref.shape[0]
    tiles = f_ref.shape[1] // 128
    left = lax.broadcasted_iota(jnp.int32, (width, 128), 1) < 64
    left2 = lax.broadcasted_iota(jnp.int32, (2 * width, 128), 1) < 64

    def build(t, carry):
        for part, ref in enumerate((low_ref, f_ref, high_ref)):
            x = ref[:, pl.ds(pl.multiple_of(t * 128, 128), 128)]
            for v, y in enumerate((x, pltpu.roll(x, 64, 1))):
                hi, lo = split(y)
                at = (3 * v + part) * tiles + t
                e_ref[at, 0:width] = hi
                e_ref[at, width : 2 * width] = lo
        return carry

    lax.fori_loop(0, tiles, build, 0, unroll=BUILD_UNROLL)

    center = (bounds_ref[0] + bounds_ref[1]) * 0.5
    half = (bounds_ref[1] - bounds_ref[0]) * 0.5
    slots = w_ref.shape[2] // 64

    def one(i):
        at = [slot_ref[i * slots + s] for s in range(slots)]
        lhs = jnp.concatenate(
            [
                jnp.where(left2, e_ref[at[s]], e_ref[at[s + 1]])
                for s in range(0, slots, 2)
            ],
            axis=1,
        )
        out = dot_nt(lhs, w_ref[i])
        acc = out[:width] + jnp.where(left, out[width:], 0.0)
        return acc + pltpu.roll(acc, 64, 1)

    def pair(g, carry):
        y = jnp.where(left, one(2 * g), one(2 * g + 1))
        lanes = pl.ds(pl.multiple_of(g * 128, 128), 128)
        f = f_ref[:, lanes]
        r = (y - center * f) / half
        if stage > 0:
            r = 2.0 * r - prev_ref[:, lanes]
        if stage < 2:
            out_ref[:, lanes] = r
        else:
            out_ref[g] = r
        return carry

    lax.fori_loop(0, tiles, pair, 0, unroll=PAIR_UNROLL)


def apply_step(stage, slot_table, bounds, f, low, high, prev, w):
    width, n = f.shape
    tiles = n // 128
    args = (f, low, high) + (() if prev is None else (prev,)) + (w,)
    out = (width, n) if stage < 2 else (tiles, width, 128)
    return pl.pallas_call(
        functools.partial(apply_kernel, stage),
        out_shape=pltpu.VMEM(out, F32),
        in_specs=[SMEM] * 2 + [VMEM] * len(args),
        out_specs=VMEM,
        scratch_shapes=[pltpu.VMEM((6 * tiles, 2 * width, 128), BF)],
        compiler_params=PARAMS,
        name=f"apply_{stage}",
    )(slot_table, bounds, *map(near, args))


def slot_places(columns, first_row, block_rows, total_rows):
    reach = jnp.mod(columns - first_row + block_rows, total_rows)
    right = jnp.arange(columns.shape[1], dtype=jnp.int32) % 2
    exchanged = (reach + right) % 2
    return (exchanged * (3 * block_rows // 2) + reach // 2).reshape(-1)


def gram_kernel(s_ref, out_ref):
    s = jnp.concatenate(
        [
            s_ref[:, j].reshape(s_ref.shape[0] * s_ref.shape[2], 128)
            for j in range(s_ref.shape[1])
        ],
        axis=1,
    )
    g = lax.dot_general(
        s, s, (((1,), (1,)), ((), ())), precision=HIGHEST, preferred_element_type=F32
    )
    k = g.shape[0]
    for j in range(k // 128):
        out_ref[j] = g[:, j * 128 : (j + 1) * 128].reshape(k // 8, 8, 128)


def gram_tiles(s):
    k = s.shape[0] * s.shape[2]
    return pl.pallas_call(
        gram_kernel,
        out_shape=pltpu.VMEM((k // 128, k // 8, 8, 128), F32),
        in_specs=[VMEM],
        out_specs=VMEM,
        compiler_params=PARAMS,
        name="gram",
    )(near(s))


def row_of(x, r):
    return jnp.broadcast_to(x[r : r + 1, :], (8, 128))


def lane_of(x, c):
    return jnp.broadcast_to(x[:, c : c + 1], (8, 128))


def factor_block(m):
    n = m.shape[0]
    sub = lax.broadcasted_iota(jnp.int32, (8, 128), 0)
    vregs = [m[8 * v : 8 * v + 8] for v in range(n // 8)]
    done = []
    for v0 in range(n // 8):
        head = vregs[v0]
        cols = [
            [lane_of(vregs[v], 8 * v0 + c) for c in range(8)]
            for v in range(v0, n // 8)
        ]
        rows = [row_of(head, k) for k in range(8)]
        p = {(k, c): row_of(cols[0][c], k) for c in range(8) for k in range(c + 1)}
        inv, mult = [], {}
        out = jnp.zeros((8, 128), F32)
        for k in range(8):
            inv.append(1.0 / p[k, k])
            for r in range(k + 1, 8):
                f = p[k, r] * inv[k]
                mult[k, r] = f
                for c in range(r, 8):
                    p[r, c] = p[r, c] - f * p[k, c]
                rows[r] = rows[r] - f * rows[k]
            out = jnp.where(sub == k, rows[k] * lax.rsqrt(p[k, k]), out)
        done.append(out)
        if v0 + 1 == n // 8:
            break
        z = [rows[k] * inv[k] for k in range(8)]
        for k in range(7, -1, -1):
            for r in range(k):
                z[r] = z[r] - mult[r, k] * z[k]
        for v in range(v0 + 1, n // 8):
            t = [cols[v - v0][k] * z[k] for k in range(8)]
            while len(t) > 1:
                t = [t[i] + t[i + 1] for i in range(0, len(t), 2)]
            vregs[v] = vregs[v] - t[0]
    return jnp.concatenate(done, axis=0)


def split3(x):
    a = x.astype(BF)
    r = x - a.astype(F32)
    b = r.astype(BF)
    c = (r - b.astype(F32)).astype(BF)
    return a, b, c


def six_lanes(twice):
    a, b, c = split3(twice)
    left = lax.broadcasted_iota(jnp.int32, twice.shape, 1) < NB
    return jnp.concatenate([a, jnp.where(left, b, a), jnp.where(left, b, c)], axis=1)


def six_rows(x):
    a, b, c = split3(x)
    return jnp.concatenate([a, b, a, c, b, a], axis=0)


def dot_nn(a, b):
    return lax.dot_general(a, b, (((1,), (0,)), ((), ())), preferred_element_type=F32)


def solve_kernel(g_ref, s_ref, basis_ref, factor_ref, a_ref):
    k = factor_ref.shape[0]
    halves = k // 128
    for j in range(halves):
        a_ref[:, j * 128 : (j + 1) * 128] = g_ref[j].reshape(k, 128)
    for j in range(s_ref.shape[1]):
        a_ref[:, k + j * 128 : k + (j + 1) * 128] = s_ref[:, j].reshape(k, 128)
    lane = lax.broadcasted_iota(jnp.int32, (NB, 128), 1)
    sub = lax.broadcasted_iota(jnp.int32, (NB, 128), 0)
    eye = jnp.where(lane == sub + NB, 1.0, 0.0)

    def step(b, carry):
        first = pl.multiple_of(b * NB, NB)
        rows = pl.ds(first, NB)
        tile = a_ref[rows, pl.ds(pl.multiple_of((b // 2) * 128, 128), 128)]
        tile = jnp.where(b % 2 == 1, pltpu.roll(tile, NB, 1), tile)
        u = factor_block(jnp.where(lane < NB, tile, eye))
        twice = jnp.where(lane < NB, pltpu.roll(u, NB, 1), u)
        x = dot_nn(six_lanes(twice), six_rows(a_ref[rows, :]))
        row_id = first + lax.broadcasted_iota(jnp.int32, (NB, k), 0)
        col_id = lax.broadcasted_iota(jnp.int32, (NB, k), 1)
        factor_ref[rows, :] = jnp.where(col_id >= row_id, x[:, :k], 0.0)
        basis_ref[rows, :] = x[:, k:]
        later = jnp.where(col_id >= first + NB, x[:, :k], 0.0)
        turned = jnp.concatenate([later, later], axis=0).T
        a_ref[...] -= dot_nn(six_lanes(turned), six_rows(x))
        return carry

    lax.fori_loop(0, k // NB, step, 0)


def orthonormalize(g, s):
    k = s.shape[0] * s.shape[2]
    n = s.shape[1] * 128
    return pl.pallas_call(
        solve_kernel,
        out_shape=(
            jax.ShapeDtypeStruct((k, n), F32),
            jax.ShapeDtypeStruct((k, k), F32),
        ),
        in_specs=[VMEM, VMEM],
        out_specs=(VMEM, VMEM),
        scratch_shapes=[pltpu.VMEM((k, k + n), F32)],
        compiler_params=PARAMS,
        name="orthonormalize",
    )(near(g), near(s))


def sum_over_devices(tiles):
    shape = tiles.shape
    rows = lax.axis_size("row")
    bundles = lax.axis_size("bundle")
    parts = lax.all_to_all(
        tiles.reshape(rows, -1, 128), "row", split_axis=0, concat_axis=0, tiled=True
    )
    mine = jnp.sum(parts, axis=0)
    parts = lax.all_to_all(
        jnp.broadcast_to(mine[None], (bundles,) + mine.shape),
        "bundle",
        split_axis=0,
        concat_axis=0,
        tiled=True,
    )
    mine = jnp.sum(parts, axis=0)
    parts = lax.all_to_all(
        jnp.broadcast_to(mine[None], (rows,) + mine.shape),
        "row",
        split_axis=0,
        concat_axis=0,
        tiled=True,
    )
    return parts.reshape(shape)


def local(vectors, blocks, columns, bounds):
    block_rows = blocks.shape[0]
    row_count = lax.axis_size("row")
    bundles = lax.axis_size("bundle")
    total_rows = block_rows * row_count
    first_row = lax.axis_index("row") * block_rows
    places = slot_places(columns, first_row, block_rows, total_rows)
    forward = [(i, (i + 1) % row_count) for i in range(row_count)]
    backward = [(j, i) for i, j in forward]

    def sides(field):
        return (
            lax.ppermute(field, "row", forward),
            lax.ppermute(field, "row", backward),
        )

    low, high = sides(vectors)
    w = split_blocks(blocks)
    first = apply_step(
        0, places, bounds, vectors, low, high, None, w
    )
    low, high = sides(first)
    second = apply_step(
        1, places, bounds, first, low, high, vectors, w
    )
    low, high = sides(second)
    filtered = apply_step(
        2, places, bounds, second, low, high, first, w
    )
    tiles, width, lanes = filtered.shape
    stacked = lax.all_to_all(
        filtered.reshape(bundles, tiles // bundles, width, lanes),
        "bundle",
        split_axis=0,
        concat_axis=0,
        tiled=True,
    )
    gram = sum_over_devices(gram_tiles(stacked))
    return orthonormalize(gram, stacked)


def solution(mesh):
    placed = (P("bundle", "row"), P("row", None, None), P("row", None), P())
    return jax.shard_map(
        local,
        mesh=mesh,
        in_specs=placed,
        out_specs=(P(None, ("row", "bundle")), P()),
        check_vma=False,
    )
```

time: 155 us -> 133 us (0.86)
  Pallas kernels: 42.3 us -> 20.9 us
  blocking collectives: 59.6 us -> 57.9 us
  waiting for transfers between devices: 20.4 us -> 22 us
    pallas_call x5, Pallas kernels: 24.8 us -> 9.05 us  [the longest x3 8.14 us: apply_step(): pl.pallas_call(functools.partial(apply_kernel, stage), out_shape=pltpu.VM...]
    pallas_call x1, Pallas kernels: 17.4 us -> 11.8 us  [orthonormalize(): pl.pallas_call(solve_kernel, out_shape=(jax.ShapeDtypeStruct((k, n), F32)...]
    ppermute x3, waiting for transfers between devices: 15.5 us -> 17.5 us  [sides(): lax.ppermute(field, 'row', forward)]
    unnamed x13 -> x6, local copies, waits for them, and re-layouts: 3.48 us -> 1.89 us
  transfers between devices with their start and end apart: 6 -> 6, of which waited for: 5 -> 5; matrix products, arithmetic and copies ran while one was open for 1% -> 1% of each run, Pallas kernels for 3% -> 0%
where the time goes in v2:
time: 133 us; the launch traced here: 131 us
  blocking collectives  57.9 us (44%)
  starting transfers between devices  26.9 us (20%)
  waiting for transfers between devices  22 us (17%)
  Pallas kernels  20.9 us (16%)
  local copies, waits for them, and re-layouts  2.11 us (2%)
    ppermute x3, starting transfers between devices, sides(): lax.ppermute(field, 'row', backward)  18.2 us
    ppermute x3, waiting for transfers between devices, sides(): lax.ppermute(field, 'row', forward)  17.5 us
    all_to_all x1, blocking collectives, sum_over_devices(): lax.all_to_all(jnp.broadcast_to(mine[None], (rows,) + mine.shape), 'row',...  16.7 us
    all_to_all x1, blocking collectives, sum_over_devices(): lax.all_to_all(tiles.reshape(rows, -1, 128), 'row', split_axis=0, concat_...  16.5 us
    all_to_all x1, blocking collectives, local(): lax.all_to_all(filtered.reshape(bundles, tiles // bundles, width, lanes),...  14.4 us
    pallas_call x1, Pallas kernels, orthonormalize(): pl.pallas_call(solve_kernel, out_shape=(jax.ShapeDtypeStruct((k, n), F32)...  11.8 us
    all_to_all x1, blocking collectives, sum_over_devices(): lax.all_to_all(jnp.broadcast_to(mine[None], (bundles,) + mine.shape), 'bu...  10.3 us
    ppermute x3, starting transfers between devices, sides(): lax.ppermute(field, 'row', forward)  8.65 us
  transfers between devices with their start and end apart: 6, of which 5 were waited for; matrix products, arithmetic and copies ran while one was open for 1% of the time, Pallas kernels for 0%

profile of v2, /device:TPU:1, one launch (start us, length us, event | category | flops | bytes accessed | tf_op | source)
XLA Modules:
  0.0 131.3 jit_solution(10185336069676041131)
XLA Ops:
  0.6 14.4 %collective-permute-start.1 = (f32[32,2048]{1,0:T(8,128)}, f32[32,2048]{1,0:T(8,128)S(1)}, u32[]{:S(2)}, u32[]{:S(2)}) collective-permute-start(f32[32,2048]{1,0:T(8,128)} %refs_3_.1), channel_id=1, source_target_pairs={{8,0},{16,8},{24,16},{32,24},{40,32},{48,40},{56,48},{64,56},{72,6... | collective-permute-start | bytes 786440 | tf_op jit(solution)/shard_map/ppermute | solution.py:319
  15.0 1.9 %collective-permute-start = (f32[32,2048]{1,0:T(8,128)}, f32[32,2048]{1,0:T(8,128)S(1)}, u32[]{:S(2)}, u32[]{:S(2)}) collective-permute-start(f32[32,2048]{1,0:T(8,128)} %refs_3_.1), channel_id=1, source_target_pairs={{0,8},{8,16},{16,24},{24,32},{32,40},{40,48},{48,56},{56,64},{64,7... | collective-permute-start | bytes 786440 | tf_op jit(solution)/shard_map/ppermute | solution.py:318
  17.0 0.8 fusion.3
  17.8 0.1 reshape.27.slot_ref
  18.0 1.9 %copy-done = f32[32,64,384]{2,1,0:T(8,128)S(1)} copy-done((f32[32,64,384]{2,1,0:T(8,128)S(1)}, f32[32,64,384]{2,1,0:T(8,128)}, u32[]{:S(2)}) %copy-start) | copy-done | bytes 3145752
  19.8 0.5 split_blocks.1.refs_3_.refs_4_
  20.4 7.0 %collective-permute-done.refs_1_ = f32[32,2048]{1,0:T(8,128)S(1)} collective-permute-done((f32[32,2048]{1,0:T(8,128)}, f32[32,2048]{1,0:T(8,128)S(1)}, u32[]{:S(2)}, u32[]{:S(2)}) %collective-permute-start) | collective-permute-done | bytes 262176 | tf_op jit(solution)/shard_map/ppermute | solution.py:318
  27.4 2.7 %apply_0.1.refs_0_.refs_3_ = f32[32,2048]{1,0:T(8,128)S(1)} custom-call(s32[192]{0:T(256)S(1)} %reshape.27.slot_ref, f32[2]{0:T(128)S(1)} %copy-done.2, f32[32,2048]{1,0:T(8,128)S(1)} %copy-done.1, f32[32,2048]{1,0:T(8,128)S(1)} %collective-permute-done.refs_1_, f32[32,2048]{1,0:T(8,128)S(1)} %collective-permute-done.1.refs_2_, ...), custom_call_target="tpu_custom_call" | custom-call | tf_op jit(solution)/shard_map/apply_0/pallas_call | solution.py:116
  30.1 1.9 %collective-permute-start.3 = (f32[32,2048]{1,0:T(8,128)S(1)}, f32[32,2048]{1,0:T(8,128)S(1)}, u32[]{:S(2)}, u32[]{:S(2)}) collective-permute-start(f32[32,2048]{1,0:T(8,128)S(1)} %apply_0.1.refs_0_.refs_3_), channel_id=1, source_target_pairs={{8,0},{16,8},{24,16},{32,24},{40,32},{48,40},{56,48},{64,56},{72,6... | collective-permute-start | bytes 786440 | tf_op jit(solution)/shard_map/ppermute | solution.py:319
  32.0 3.4 %collective-permute-start.2 = (f32[32,2048]{1,0:T(8,128)S(1)}, f32[32,2048]{1,0:T(8,128)S(1)}, u32[]{:S(2)}, u32[]{:S(2)}) collective-permute-start(f32[32,2048]{1,0:T(8,128)S(1)} %apply_0.1.refs_0_.refs_3_), channel_id=1, source_target_pairs={{0,8},{8,16},{16,24},{24,32},{32,40},{40,48},{48,56},{56,64},{64,7... | collective-permute-start | bytes 786440 | tf_op jit(solution)/shard_map/ppermute | solution.py:318
  35.4 2.7 %collective-permute-done.3.refs_2_ = f32[32,2048]{1,0:T(8,128)S(1)} collective-permute-done((f32[32,2048]{1,0:T(8,128)S(1)}, f32[32,2048]{1,0:T(8,128)S(1)}, u32[]{:S(2)}, u32[]{:S(2)}) %collective-permute-start.3) | collective-permute-done | bytes 262176 | tf_op jit(solution)/shard_map/ppermute | solution.py:319
  38.0 5.2 %collective-permute-done.2.refs_1_ = f32[32,2048]{1,0:T(8,128)S(1)} collective-permute-done((f32[32,2048]{1,0:T(8,128)S(1)}, f32[32,2048]{1,0:T(8,128)S(1)}, u32[]{:S(2)}, u32[]{:S(2)}) %collective-permute-start.2) | collective-permute-done | bytes 262176 | tf_op jit(solution)/shard_map/ppermute | solution.py:318
  43.3 2.7 %apply_1.1.refs_0_ = f32[32,2048]{1,0:T(8,128)S(1)} custom-call(s32[192]{0:T(256)S(1)} %reshape.27.slot_ref, f32[2]{0:T(128)S(1)} %copy-done.2, f32[32,2048]{1,0:T(8,128)S(1)} %apply_0.1.refs_0_.refs_3_, f32[32,2048]{1,0:T(8,128)S(1)} %collective-permute-done.2.refs_1_, f32[32,2048]{1,0:T(8,128)S(1)} %collective-permute-done.3.refs_2_, ...), custom_call_target="tpu_custom_call" | custom-call | tf_op jit(solution)/shard_map/apply_1/pallas_call | solution.py:116
  46.0 1.9 %collective-permute-start.5 = (f32[32,2048]{1,0:T(8,128)S(1)}, f32[32,2048]{1,0:T(8,128)S(1)}, u32[]{:S(2)}, u32[]{:S(2)}) collective-permute-start(f32[32,2048]{1,0:T(8,128)S(1)} %apply_1.1.refs_0_), channel_id=1, source_target_pairs={{8,0},{16,8},{24,16},{32,24},{40,32},{48,40},{56,48},{64,56},{72,6... | collective-permute-start | bytes 786440 | tf_op jit(solution)/shard_map/ppermute | solution.py:319
  47.9 3.4 %collective-permute-start.4 = (f32[32,2048]{1,0:T(8,128)S(1)}, f32[32,2048]{1,0:T(8,128)S(1)}, u32[]{:S(2)}, u32[]{:S(2)}) collective-permute-start(f32[32,2048]{1,0:T(8,128)S(1)} %apply_1.1.refs_0_), channel_id=1, source_target_pairs={{0,8},{8,16},{16,24},{24,32},{32,40},{40,48},{48,56},{56,64},{64,7... | collective-permute-start | bytes 786440 | tf_op jit(solution)/shard_map/ppermute | solution.py:318
  51.3 1.8 %collective-permute-done.5.refs_2_ = f32[32,2048]{1,0:T(8,128)S(1)} collective-permute-done((f32[32,2048]{1,0:T(8,128)S(1)}, f32[32,2048]{1,0:T(8,128)S(1)}, u32[]{:S(2)}, u32[]{:S(2)}) %collective-permute-start.5) | collective-permute-done | bytes 262176 | tf_op jit(solution)/shard_map/ppermute | solution.py:319
  53.1 5.2 %collective-permute-done.4.refs_1_ = f32[32,2048]{1,0:T(8,128)S(1)} collective-permute-done((f32[32,2048]{1,0:T(8,128)S(1)}, f32[32,2048]{1,0:T(8,128)S(1)}, u32[]{:S(2)}, u32[]{:S(2)}) %collective-permute-start.4) | collective-permute-done | bytes 262176 | tf_op jit(solution)/shard_map/ppermute | solution.py:318
  58.4 2.7 %apply_2.1 = f32[16,32,128]{2,1,0:T(8,128)S(1)} custom-call(s32[192]{0:T(256)S(1)} %reshape.27.slot_ref, f32[2]{0:T(128)S(1)} %copy-done.2, f32[32,2048]{1,0:T(8,128)S(1)} %apply_1.1.refs_0_, f32[32,2048]{1,0:T(8,128)S(1)} %collective-permute-done.4.refs_1_, f32[32,2048]{1,0:T(8,128)S(1)} %collective-permute-done.5.refs_2_, ...), custom_call_target="tpu_custom_call" | custom-call | tf_op jit(solution)/shard_map/apply_2/pallas_call | solution.py:116
  61.1 14.4 %all_to_all.20.s_ref = f32[8,2,32,128]{3,2,1,0:T(8,128)S(1)} all-to-all(f32[8,2,32,128]{3,2,1,0:T(8,128)S(1)} %bitcast.5), channel_id=1, replica_groups=mesh['row'=64,'bundle'=8] {'bundle'}, dimensions={0} | all-to-all | bytes 524288 | tf_op jit(solution)/shard_map/all_to_all | solution.py:336
  75.5 0.4 gram.1
  75.9 16.5 %all_to_all.21 = f32[64,8,128]{2,1,0:T(8,128)S(1)} all-to-all(f32[64,8,128]{2,1,0:T(8,128)S(1)} %bitcast.4), channel_id=1, replica_groups=mesh['row'=64,'bundle'=8] {'row'}, dimensions={0} | all-to-all | bytes 524288 | tf_op jit(solution)/shard_map/all_to_all | solution.py:284
  92.4 10.3 %all_to_all.22 = f32[8,8,128]{2,1,0:T(8,128)S(1)} all-to-all(f32[8,8,128]{2,1,0:T(8,128)S(1)} %broadcast_in_dim.4), channel_id=1, replica_groups=mesh['row'=64,'bundle'=8] {'bundle'}, dimensions={0} | all-to-all | bytes 65536 | tf_op jit(solution)/shard_map/all_to_all | solution.py:288
  102.8 16.7 %all_to_all.23 = f32[64,8,128]{2,1,0:T(8,128)S(1)} all-to-all(f32[64,8,128]{2,1,0:T(8,128)S(1)} %broadcast_in_dim.5), channel_id=1, replica_groups=mesh['row'=64,'bundle'=8] {'row'}, dimensions={0} | all-to-all | bytes 524288 | tf_op jit(solution)/shard_map/all_to_all | solution.py:296
  119.5 11.8 %orthonormalize.1 = (f32[256,256]{1,0:T(8,128)}, f32[256,256]{1,0:T(8,128)}) custom-call(f32[2,32,8,128]{3,2,1,0:T(8,128)S(1)} %bitcast.3, f32[8,2,32,128]{3,2,1,0:T(8,128)S(1)} %all_to_all.20.s_ref), custom_call_target="tpu_custom_call" | custom-call | tf_op jit(solution)/shard_map/orthonormalize/pallas_call | solution.py:266
  (12 shorter events, 0.2 us)
Async XLA Ops:
  0.6 19.7 %collective-permute-start.1 = (f32[32,2048]{1,0:T(8,128)}, f32[32,2048]{1,0:T(8,128)S(1)}, u32[]{:S(2)}, u32[]{:S(2)}) collective-permute-start(f32[32,2048]{1,0:T(8,128)} %refs_3_.1), channel_id=1, source_target_pairs={{8,0},{16,8},{24,16},{32,24},{40,32},{48,40},{56,48},{64,56},{72,6... | collective-permute-start | bytes 786440 | tf_op jit(solution)/shard_map/ppermute | solution.py:319
  15.0 12.3 %collective-permute-start = (f32[32,2048]{1,0:T(8,128)}, f32[32,2048]{1,0:T(8,128)S(1)}, u32[]{:S(2)}, u32[]{:S(2)}) collective-permute-start(f32[32,2048]{1,0:T(8,128)} %refs_3_.1), channel_id=1, source_target_pairs={{0,8},{8,16},{16,24},{24,32},{32,40},{40,48},{48,56},{56,64},{64,7... | collective-permute-start | bytes 786440 | tf_op jit(solution)/shard_map/ppermute | solution.py:318
  17.9 1.9 %copy-start = (f32[32,64,384]{2,1,0:T(8,128)S(1)}, f32[32,64,384]{2,1,0:T(8,128)}, u32[]{:S(2)}) copy-start(f32[32,64,384]{2,1,0:T(8,128)} %b_ref.1) | copy-start | bytes 9437188
  19.8 7.5 %copy-start.1 = (f32[32,2048]{1,0:T(8,128)S(1)}, f32[32,2048]{1,0:T(8,128)}, u32[]{:S(2)}) copy-start(f32[32,2048]{1,0:T(8,128)} %refs_3_.1) | copy-start | bytes 786436
  19.8 7.5 %copy-start.2 = (f32[2]{0:T(128)S(1)}, f32[2]{0:T(128)}, u32[]{:S(2)}) copy-start(f32[2]{0:T(128)} %bounds_ref.5) | copy-start | bytes 28
  30.1 7.9 %collective-permute-start.3 = (f32[32,2048]{1,0:T(8,128)S(1)}, f32[32,2048]{1,0:T(8,128)S(1)}, u32[]{:S(2)}, u32[]{:S(2)}) collective-permute-start(f32[32,2048]{1,0:T(8,128)S(1)} %apply_0.1.refs_0_.refs_3_), channel_id=1, source_target_pairs={{8,0},{16,8},{24,16},{32,24},{40,32},{48,40},{56,48},{64,56},{72,6... | collective-permute-start | bytes 786440 | tf_op jit(solution)/shard_map/ppermute | solution.py:319
  32.0 11.3 %collective-permute-start.2 = (f32[32,2048]{1,0:T(8,128)S(1)}, f32[32,2048]{1,0:T(8,128)S(1)}, u32[]{:S(2)}, u32[]{:S(2)}) collective-permute-start(f32[32,2048]{1,0:T(8,128)S(1)} %apply_0.1.refs_0_.refs_3_), channel_id=1, source_target_pairs={{0,8},{8,16},{16,24},{24,32},{32,40},{40,48},{48,56},{56,64},{64,7... | collective-permute-start | bytes 786440 | tf_op jit(solution)/shard_map/ppermute | solution.py:318
  46.0 7.1 %collective-permute-start.5 = (f32[32,2048]{1,0:T(8,128)S(1)}, f32[32,2048]{1,0:T(8,128)S(1)}, u32[]{:S(2)}, u32[]{:S(2)}) collective-permute-start(f32[32,2048]{1,0:T(8,128)S(1)} %apply_1.1.refs_0_), channel_id=1, source_target_pairs={{8,0},{16,8},{24,16},{32,24},{40,32},{48,40},{56,48},{64,56},{72,6... | collective-permute-start | bytes 786440 | tf_op jit(solution)/shard_map/ppermute | solution.py:319
  47.9 10.4 %collective-permute-start.4 = (f32[32,2048]{1,0:T(8,128)S(1)}, f32[32,2048]{1,0:T(8,128)S(1)}, u32[]{:S(2)}, u32[]{:S(2)}) collective-permute-start(f32[32,2048]{1,0:T(8,128)S(1)} %apply_1.1.refs_0_), channel_id=1, source_target_pairs={{0,8},{8,16},{16,24},{24,32},{32,40},{40,48},{48,56},{56,64},{64,7... | collective-permute-start | bytes 786440 | tf_op jit(solution)/shard_map/ppermute | solution.py:318

commit v3 on v2

--- a/solution.py
+++ b/solution.py
@@ -13,6 +13,8 @@
 VMEM = pl.BlockSpec(memory_space=pltpu.VMEM)
 SMEM = pl.BlockSpec(memory_space=pltpu.SMEM)
 NB = 64
+PACKED = 320
+PLANE = 64
 BUILD_UNROLL = 8
 PAIR_UNROLL = 8
 PARAMS = pltpu.CompilerParams(vmem_limit_bytes=20 * 1024 * 1024)
@@ -131,6 +133,13 @@
     return (exchanged * (3 * block_rows // 2) + reach // 2).reshape(-1)
 
 
+def square():
+    return (
+        lax.broadcasted_iota(jnp.int32, (128, 128), 0),
+        lax.broadcasted_iota(jnp.int32, (128, 128), 1),
+    )
+
+
 def gram_kernel(s_ref, out_ref):
     s = jnp.concatenate(
         [
@@ -142,16 +151,20 @@
     g = lax.dot_general(
         s, s, (((1,), (1,)), ((), ())), precision=HIGHEST, preferred_element_type=F32
     )
-    k = g.shape[0]
-    for j in range(k // 128):
-        out_ref[j] = g[:, j * 128 : (j + 1) * 128].reshape(k // 8, 8, 128)
-
-
-def gram_tiles(s):
-    k = s.shape[0] * s.shape[2]
+    row, col = square()
+    last = g[128:, 128:]
+    out_ref[0:128] = g[:128, 128:]
+    out_ref[128:256] = jnp.where(row >= col, g[:128, :128], last)
+    out_ref[256:] = jnp.zeros((out_ref.shape[0] - 256, 128), F32)
+    out_ref[256:257] = jnp.sum(
+        jnp.where(row == col, last, 0.0), axis=0, keepdims=True
+    )
+
+
+def gram_packed(s):
     return pl.pallas_call(
         gram_kernel,
-        out_shape=pltpu.VMEM((k // 128, k // 8, 8, 128), F32),
+        out_shape=pltpu.VMEM((PACKED, 128), F32),
         in_specs=[VMEM],
         out_specs=VMEM,
         compiler_params=PARAMS,
@@ -160,7 +173,7 @@
 
 
 def row_of(x, r):
-    return jnp.broadcast_to(x[r : r + 1, :], (8, 128))
+    return jnp.take_along_axis(x, jnp.full((8, 128), r, jnp.int32), axis=0)
 
 
 def lane_of(x, c):
@@ -170,6 +183,7 @@
 def factor_block(m):
     n = m.shape[0]
     sub = lax.broadcasted_iota(jnp.int32, (8, 128), 0)
+    here = [sub == k for k in range(8)]
     vregs = [m[8 * v : 8 * v + 8] for v in range(n // 8)]
     done = []
     for v0 in range(n // 8):
@@ -178,26 +192,22 @@
             [lane_of(vregs[v], 8 * v0 + c) for c in range(8)]
             for v in range(v0, n // 8)
         ]
-        rows = [row_of(head, k) for k in range(8)]
-        p = {(k, c): row_of(cols[0][c], k) for c in range(8) for k in range(c + 1)}
-        inv, mult = [], {}
+        p = list(cols[0])
         out = jnp.zeros((8, 128), F32)
         for k in range(8):
-            inv.append(1.0 / p[k, k])
-            for r in range(k + 1, 8):
-                f = p[k, r] * inv[k]
-                mult[k, r] = f
-                for c in range(r, 8):
-                    p[r, c] = p[r, c] - f * p[k, c]
-                rows[r] = rows[r] - f * rows[k]
-            out = jnp.where(sub == k, rows[k] * lax.rsqrt(p[k, k]), out)
+            pivot = row_of(p[k], k)
+            inv = 1.0 / pivot
+            row = row_of(head, k)
+            out = jnp.where(here[k], row * lax.rsqrt(pivot), out)
+            for c in range(k + 1, 8):
+                r = row_of(p[c], k) * inv
+                p[c] = jnp.where(here[k], r, p[c] - p[k] * r)
+            r = row * inv
+            head = jnp.where(here[k], r, head - p[k] * r)
         done.append(out)
         if v0 + 1 == n // 8:
             break
-        z = [rows[k] * inv[k] for k in range(8)]
-        for k in range(7, -1, -1):
-            for r in range(k):
-                z[r] = z[r] - mult[r, k] * z[k]
+        z = [row_of(head, k) for k in range(8)]
         for v in range(v0 + 1, n // 8):
             t = [cols[v - v0][k] * z[k] for k in range(8)]
             while len(t) > 1:
@@ -231,33 +241,42 @@
 
 def solve_kernel(g_ref, s_ref, basis_ref, factor_ref, a_ref):
     k = factor_ref.shape[0]
-    halves = k // 128
-    for j in range(halves):
-        a_ref[:, j * 128 : (j + 1) * 128] = g_ref[j].reshape(k, 128)
+    row, col = square()
+    mixed = g_ref[128:256]
+    turned = mixed.T
+    a_ref[:128, :128] = jnp.where(row >= col, mixed, turned)
+    a_ref[:128, 128:k] = g_ref[0:128]
+    last = jnp.where(row < col, mixed, turned)
+    a_ref[128:, 128:k] = jnp.where(row == col, g_ref[256:257], last)
     for j in range(s_ref.shape[1]):
         a_ref[:, k + j * 128 : k + (j + 1) * 128] = s_ref[:, j].reshape(k, 128)
     lane = lax.broadcasted_iota(jnp.int32, (NB, 128), 1)
     sub = lax.broadcasted_iota(jnp.int32, (NB, 128), 0)
     eye = jnp.where(lane == sub + NB, 1.0, 0.0)
-
-    def step(b, carry):
-        first = pl.multiple_of(b * NB, NB)
-        rows = pl.ds(first, NB)
-        tile = a_ref[rows, pl.ds(pl.multiple_of((b // 2) * 128, 128), 128)]
-        tile = jnp.where(b % 2 == 1, pltpu.roll(tile, NB, 1), tile)
+    for first in range(0, k, NB):
+        rows = slice(first, first + NB)
+        at = first // 128 * 128
+        tile = a_ref[rows, at : at + 128]
+        if first > at:
+            tile = pltpu.roll(tile, NB, 1)
         u = factor_block(jnp.where(lane < NB, tile, eye))
         twice = jnp.where(lane < NB, pltpu.roll(u, NB, 1), u)
-        x = dot_nn(six_lanes(twice), six_rows(a_ref[rows, :]))
-        row_id = first + lax.broadcasted_iota(jnp.int32, (NB, k), 0)
-        col_id = lax.broadcasted_iota(jnp.int32, (NB, k), 1)
-        factor_ref[rows, :] = jnp.where(col_id >= row_id, x[:, :k], 0.0)
-        basis_ref[rows, :] = x[:, k:]
-        later = jnp.where(col_id >= first + NB, x[:, :k], 0.0)
-        turned = jnp.concatenate([later, later], axis=0).T
-        a_ref[...] -= dot_nn(six_lanes(turned), six_rows(x))
-        return carry
-
-    lax.fori_loop(0, k // NB, step, 0)
+        x = dot_nn(six_lanes(twice), six_rows(a_ref[rows, at:]))
+        col_id = at + lax.broadcasted_iota(jnp.int32, (NB, k - at), 1)
+        row_id = first + lax.broadcasted_iota(jnp.int32, (NB, k - at), 0)
+        upper = jnp.where(col_id >= row_id, x[:, : k - at], 0.0)
+        if at > 0:
+            upper = jnp.concatenate([jnp.zeros((NB, at), F32), upper], axis=1)
+        factor_ref[rows, :] = upper
+        basis_ref[rows, :] = x[:, k - at :]
+        after = first + NB
+        if after < k:
+            start = after // 128 * 128
+            turned = x[:, start - at : k - at]
+            turned = jnp.concatenate([turned, turned], axis=0).T[after - start :]
+            a_ref[after:, start:] -= dot_nn(
+                six_lanes(turned), six_rows(x[:, start - at :])
+            )
 
 
 def orthonormalize(g, s):
@@ -277,30 +296,24 @@
     )(near(g), near(s))
 
 
-def sum_over_devices(tiles):
-    shape = tiles.shape
-    rows = lax.axis_size("row")
-    bundles = lax.axis_size("bundle")
-    parts = lax.all_to_all(
-        tiles.reshape(rows, -1, 128), "row", split_axis=0, concat_axis=0, tiled=True
-    )
-    mine = jnp.sum(parts, axis=0)
-    parts = lax.all_to_all(
-        jnp.broadcast_to(mine[None], (bundles,) + mine.shape),
-        "bundle",
-        split_axis=0,
-        concat_axis=0,
-        tiled=True,
-    )
-    mine = jnp.sum(parts, axis=0)
-    parts = lax.all_to_all(
-        jnp.broadcast_to(mine[None], (rows,) + mine.shape),
-        "row",
-        split_axis=0,
-        concat_axis=0,
-        tiled=True,
-    )
-    return parts.reshape(shape)
+def sum_over_devices(packed):
+    axes = ("row", "bundle")
+    count = lax.axis_size("row") * lax.axis_size("bundle")
+    planes = count // PLANE
+    plane = [[p * PLANE + i for i in range(PLANE)] for p in range(planes)]
+    across = [[p * PLANE + i for p in range(planes)] for i in range(PLANE)]
+
+    def exchange(x, groups):
+        return lax.all_to_all(
+            x, axes, 0, 0, axis_index_groups=groups, tiled=True
+        )
+
+    def copies(x, n):
+        return jnp.broadcast_to(x[None], (n,) + x.shape)
+
+    mine = jnp.sum(exchange(packed.reshape(PLANE, 1, -1), plane), axis=0)
+    mine = jnp.sum(exchange(copies(mine, planes), across), axis=0)
+    return exchange(copies(mine, PLANE), plane).reshape(packed.shape)
 
 
 def local(vectors, blocks, columns, bounds):
@@ -340,7 +353,7 @@
         concat_axis=0,
         tiled=True,
     )
-    gram = sum_over_devices(gram_tiles(stacked))
+    gram = sum_over_devices(gram_packed(stacked))
     return orthonormalize(gram, stacked)
 
 

time: 133 us -> 129 us (0.970)
  Pallas kernels: 20.9 us -> 19.2 us
  blocking collectives: 57.9 us -> 56.2 us
    all_to_all x3, blocking collectives: 43.5 us -> 41.8 us  [exchange(): return lax.all_to_all(x, axes, 0, 0, axis_index_groups=groups, tiled=True)]
    pallas_call x1, Pallas kernels: 11.8 us -> 10.2 us  [orthonormalize(): pl.pallas_call(solve_kernel, out_shape=(jax.ShapeDtypeStruct((k, n), F32)...]
where the time goes in v3:
time: 129 us; the launch traced here: 128 us
  blocking collectives  56.2 us (44%)
  starting transfers between devices  26.9 us (21%)
  waiting for transfers between devices  22 us (17%)
  Pallas kernels  19.2 us (15%)
  local copies, waits for them, and re-layouts  2.19 us (2%)
    all_to_all x3, blocking collectives, exchange(): return lax.all_to_all(x, axes, 0, 0, axis_index_groups=groups, tiled=True)  41.8 us
    ppermute x3, starting transfers between devices, sides(): lax.ppermute(field, 'row', backward)  18.2 us
    ppermute x3, waiting for transfers between devices, sides(): lax.ppermute(field, 'row', forward)  17.5 us
    all_to_all x1, blocking collectives, local(): lax.all_to_all(filtered.reshape(bundles, tiles // bundles, width, lanes),...  14.4 us
    pallas_call x1, Pallas kernels, orthonormalize(): pl.pallas_call(solve_kernel, out_shape=(jax.ShapeDtypeStruct((k, n), F32)...  10.2 us
    ppermute x3, starting transfers between devices, sides(): lax.ppermute(field, 'row', forward)  8.65 us
    pallas_call x3, Pallas kernels, apply_step(): pl.pallas_call(functools.partial(apply_kernel, stage), out_shape=pltpu.VM...  8.14 us
    ppermute x3, waiting for transfers between devices, sides(): lax.ppermute(field, 'row', backward)  4.47 us
  transfers between devices with their start and end apart: 6, of which 5 were waited for; matrix products, arithmetic and copies ran while one was open for 1% of the time, Pallas kernels for 0%

profile of v3, /device:TPU:1, one launch (start us, length us, event | category | flops | bytes accessed | tf_op | source)
XLA Modules:
  0.0 128.1 jit_solution(1716332491343951166)
XLA Ops:
  0.6 14.4 %collective-permute-start.1 = (f32[32,2048]{1,0:T(8,128)}, f32[32,2048]{1,0:T(8,128)S(1)}, u32[]{:S(2)}, u32[]{:S(2)}) collective-permute-start(f32[32,2048]{1,0:T(8,128)} %refs_3_.1), channel_id=1, source_target_pairs={{8,0},{16,8},{24,16},{32,24},{40,32},{48,40},{56,48},{64,56},{72,6... | collective-permute-start | bytes 786440 | tf_op jit(solution)/shard_map/ppermute | solution.py:332
  15.0 1.9 %collective-permute-start = (f32[32,2048]{1,0:T(8,128)}, f32[32,2048]{1,0:T(8,128)S(1)}, u32[]{:S(2)}, u32[]{:S(2)}) collective-permute-start(f32[32,2048]{1,0:T(8,128)} %refs_3_.1), channel_id=1, source_target_pairs={{0,8},{8,16},{16,24},{24,32},{32,40},{40,48},{48,56},{56,64},{64,7... | collective-permute-start | bytes 786440 | tf_op jit(solution)/shard_map/ppermute | solution.py:331
  17.0 0.8 fusion.3
  18.0 1.9 %copy-done = f32[32,64,384]{2,1,0:T(8,128)S(1)} copy-done((f32[32,64,384]{2,1,0:T(8,128)S(1)}, f32[32,64,384]{2,1,0:T(8,128)}, u32[]{:S(2)}) %copy-start) | copy-done | bytes 3145752
  19.8 0.5 split_blocks.1.refs_3_.refs_4_
  20.4 7.0 %collective-permute-done.refs_1_ = f32[32,2048]{1,0:T(8,128)S(1)} collective-permute-done((f32[32,2048]{1,0:T(8,128)}, f32[32,2048]{1,0:T(8,128)S(1)}, u32[]{:S(2)}, u32[]{:S(2)}) %collective-permute-start) | collective-permute-done | bytes 262176 | tf_op jit(solution)/shard_map/ppermute | solution.py:331
  27.4 2.7 %apply_0.1.refs_0_.refs_3_ = f32[32,2048]{1,0:T(8,128)S(1)} custom-call(s32[192]{0:T(256)S(1)} %reshape.35.slot_ref, f32[2]{0:T(128)S(1)} %copy-done.2, f32[32,2048]{1,0:T(8,128)S(1)} %copy-done.1, f32[32,2048]{1,0:T(8,128)S(1)} %collective-permute-done.refs_1_, f32[32,2048]{1,0:T(8,128)S(1)} %collective-permute-done.1.refs_2_, ...), custom_call_target="tpu_custom_call" | custom-call | tf_op jit(solution)/shard_map/apply_0/pallas_call | solution.py:118
  30.1 1.9 %collective-permute-start.3 = (f32[32,2048]{1,0:T(8,128)S(1)}, f32[32,2048]{1,0:T(8,128)S(1)}, u32[]{:S(2)}, u32[]{:S(2)}) collective-permute-start(f32[32,2048]{1,0:T(8,128)S(1)} %apply_0.1.refs_0_.refs_3_), channel_id=1, source_target_pairs={{8,0},{16,8},{24,16},{32,24},{40,32},{48,40},{56,48},{64,56},{72,6... | collective-permute-start | bytes 786440 | tf_op jit(solution)/shard_map/ppermute | solution.py:332
  32.0 3.4 %collective-permute-start.2 = (f32[32,2048]{1,0:T(8,128)S(1)}, f32[32,2048]{1,0:T(8,128)S(1)}, u32[]{:S(2)}, u32[]{:S(2)}) collective-permute-start(f32[32,2048]{1,0:T(8,128)S(1)} %apply_0.1.refs_0_.refs_3_), channel_id=1, source_target_pairs={{0,8},{8,16},{16,24},{24,32},{32,40},{40,48},{48,56},{56,64},{64,7... | collective-permute-start | bytes 786440 | tf_op jit(solution)/shard_map/ppermute | solution.py:331
  35.4 2.7 %collective-permute-done.3.refs_2_ = f32[32,2048]{1,0:T(8,128)S(1)} collective-permute-done((f32[32,2048]{1,0:T(8,128)S(1)}, f32[32,2048]{1,0:T(8,128)S(1)}, u32[]{:S(2)}, u32[]{:S(2)}) %collective-permute-start.3) | collective-permute-done | bytes 262176 | tf_op jit(solution)/shard_map/ppermute | solution.py:332
  38.0 5.2 %collective-permute-done.2.refs_1_ = f32[32,2048]{1,0:T(8,128)S(1)} collective-permute-done((f32[32,2048]{1,0:T(8,128)S(1)}, f32[32,2048]{1,0:T(8,128)S(1)}, u32[]{:S(2)}, u32[]{:S(2)}) %collective-permute-start.2) | collective-permute-done | bytes 262176 | tf_op jit(solution)/shard_map/ppermute | solution.py:331
  43.3 2.7 %apply_1.1.refs_0_ = f32[32,2048]{1,0:T(8,128)S(1)} custom-call(s32[192]{0:T(256)S(1)} %reshape.35.slot_ref, f32[2]{0:T(128)S(1)} %copy-done.2, f32[32,2048]{1,0:T(8,128)S(1)} %apply_0.1.refs_0_.refs_3_, f32[32,2048]{1,0:T(8,128)S(1)} %collective-permute-done.2.refs_1_, f32[32,2048]{1,0:T(8,128)S(1)} %collective-permute-done.3.refs_2_, ...), custom_call_target="tpu_custom_call" | custom-call | tf_op jit(solution)/shard_map/apply_1/pallas_call | solution.py:118
  46.0 1.9 %collective-permute-start.5 = (f32[32,2048]{1,0:T(8,128)S(1)}, f32[32,2048]{1,0:T(8,128)S(1)}, u32[]{:S(2)}, u32[]{:S(2)}) collective-permute-start(f32[32,2048]{1,0:T(8,128)S(1)} %apply_1.1.refs_0_), channel_id=1, source_target_pairs={{8,0},{16,8},{24,16},{32,24},{40,32},{48,40},{56,48},{64,56},{72,6... | collective-permute-start | bytes 786440 | tf_op jit(solution)/shard_map/ppermute | solution.py:332
  47.9 3.4 %collective-permute-start.4 = (f32[32,2048]{1,0:T(8,128)S(1)}, f32[32,2048]{1,0:T(8,128)S(1)}, u32[]{:S(2)}, u32[]{:S(2)}) collective-permute-start(f32[32,2048]{1,0:T(8,128)S(1)} %apply_1.1.refs_0_), channel_id=1, source_target_pairs={{0,8},{8,16},{16,24},{24,32},{32,40},{40,48},{48,56},{56,64},{64,7... | collective-permute-start | bytes 786440 | tf_op jit(solution)/shard_map/ppermute | solution.py:331
  51.3 1.8 %collective-permute-done.5.refs_2_ = f32[32,2048]{1,0:T(8,128)S(1)} collective-permute-done((f32[32,2048]{1,0:T(8,128)S(1)}, f32[32,2048]{1,0:T(8,128)S(1)}, u32[]{:S(2)}, u32[]{:S(2)}) %collective-permute-start.5) | collective-permute-done | bytes 262176 | tf_op jit(solution)/shard_map/ppermute | solution.py:332
  53.1 5.2 %collective-permute-done.4.refs_1_ = f32[32,2048]{1,0:T(8,128)S(1)} collective-permute-done((f32[32,2048]{1,0:T(8,128)S(1)}, f32[32,2048]{1,0:T(8,128)S(1)}, u32[]{:S(2)}, u32[]{:S(2)}) %collective-permute-start.4) | collective-permute-done | bytes 262176 | tf_op jit(solution)/shard_map/ppermute | solution.py:331
  58.4 2.7 %apply_2.1 = f32[16,32,128]{2,1,0:T(8,128)S(1)} custom-call(s32[192]{0:T(256)S(1)} %reshape.35.slot_ref, f32[2]{0:T(128)S(1)} %copy-done.2, f32[32,2048]{1,0:T(8,128)S(1)} %apply_1.1.refs_0_, f32[32,2048]{1,0:T(8,128)S(1)} %collective-permute-done.4.refs_1_, f32[32,2048]{1,0:T(8,128)S(1)} %collective-permute-done.5.refs_2_, ...), custom_call_target="tpu_custom_call" | custom-call | tf_op jit(solution)/shard_map/apply_2/pallas_call | solution.py:118
  61.1 14.4 %all_to_all.20.s_ref = f32[8,2,32,128]{3,2,1,0:T(8,128)S(1)} all-to-all(f32[8,2,32,128]{3,2,1,0:T(8,128)S(1)} %bitcast.3), channel_id=1, replica_groups=mesh['row'=64,'bundle'=8] {'bundle'}, dimensions={0} | all-to-all | bytes 524288 | tf_op jit(solution)/shard_map/all_to_all | solution.py:349
  75.5 0.4 gram.1
  75.9 16.0 %all_to_all.21 = f32[64,1,640]{2,1,0:T(1,128)S(1)} all-to-all(f32[64,1,640]{2,1,0:T(1,128)S(1)} %bitcast.5), channel_id=1, replica_groups={{0,1,2,3,4,5,6,7,8,9,10,11,12,13,14,15,16,17,18,19,20,21,22,23,24,25,26..., dimensions={0} | all-to-all | bytes 327680 | tf_op jit(solution)/shard_map/all_to_all | solution.py:307
  91.9 0.1 reduce_sum.18
  92.1 9.0 %all_to_all.22 = f32[8,1,640]{2,1,0:T(1,128)S(1)} all-to-all(f32[8,1,640]{2,1,0:T(1,128)S(1)} %broadcast_in_dim.4), channel_id=1, replica_groups={{0,64,128,192,256,320,384,448},{1,65,129,193,257,321,385,449},{2,66,130..., dimensions={0} | all-to-all | bytes 40960 | tf_op jit(solution)/shard_map/all_to_all | solution.py:307
  101.2 16.7 %all_to_all.23 = f32[64,1,640]{2,1,0:T(1,128)S(1)} all-to-all(f32[64,1,640]{2,1,0:T(1,128)S(1)} %broadcast_in_dim.5), channel_id=1, replica_groups={{0,1,2,3,4,5,6,7,8,9,10,11,12,13,14,15,16,17,18,19,20,21,22,23,24,25,26..., dimensions={0} | all-to-all | bytes 327680 | tf_op jit(solution)/shard_map/all_to_all | solution.py:307
  117.9 10.2 %orthonormalize.1 = (f32[256,256]{1,0:T(8,128)}, f32[256,256]{1,0:T(8,128)}) custom-call(f32[320,128]{1,0:T(8,128)S(1)} %bitcast.4, f32[8,2,32,128]{3,2,1,0:T(8,128)S(1)} %all_to_all.20.s_ref), custom_call_target="tpu_custom_call" | custom-call | tf_op jit(solution)/shard_map/orthonormalize/pallas_call | solution.py:285
  (12 shorter events, 0.3 us)
Async XLA Ops:
  0.6 19.7 %collective-permute-start.1 = (f32[32,2048]{1,0:T(8,128)}, f32[32,2048]{1,0:T(8,128)S(1)}, u32[]{:S(2)}, u32[]{:S(2)}) collective-permute-start(f32[32,2048]{1,0:T(8,128)} %refs_3_.1), channel_id=1, source_target_pairs={{8,0},{16,8},{24,16},{32,24},{40,32},{48,40},{56,48},{64,56},{72,6... | collective-permute-start | bytes 786440 | tf_op jit(solution)/shard_map/ppermute | solution.py:332
  15.0 12.3 %collective-permute-start = (f32[32,2048]{1,0:T(8,128)}, f32[32,2048]{1,0:T(8,128)S(1)}, u32[]{:S(2)}, u32[]{:S(2)}) collective-permute-start(f32[32,2048]{1,0:T(8,128)} %refs_3_.1), channel_id=1, source_target_pairs={{0,8},{8,16},{16,24},{24,32},{32,40},{40,48},{48,56},{56,64},{64,7... | collective-permute-start | bytes 786440 | tf_op jit(solution)/shard_map/ppermute | solution.py:331
  17.9 1.9 %copy-start = (f32[32,64,384]{2,1,0:T(8,128)S(1)}, f32[32,64,384]{2,1,0:T(8,128)}, u32[]{:S(2)}) copy-start(f32[32,64,384]{2,1,0:T(8,128)} %b_ref.1) | copy-start | bytes 9437188
  19.8 7.5 %copy-start.1 = (f32[32,2048]{1,0:T(8,128)S(1)}, f32[32,2048]{1,0:T(8,128)}, u32[]{:S(2)}) copy-start(f32[32,2048]{1,0:T(8,128)} %refs_3_.1) | copy-start | bytes 786436
  19.8 7.5 %copy-start.2 = (f32[2]{0:T(128)S(1)}, f32[2]{0:T(128)}, u32[]{:S(2)}) copy-start(f32[2]{0:T(128)} %bounds_ref.5) | copy-start | bytes 28
  30.1 7.9 %collective-permute-start.3 = (f32[32,2048]{1,0:T(8,128)S(1)}, f32[32,2048]{1,0:T(8,128)S(1)}, u32[]{:S(2)}, u32[]{:S(2)}) collective-permute-start(f32[32,2048]{1,0:T(8,128)S(1)} %apply_0.1.refs_0_.refs_3_), channel_id=1, source_target_pairs={{8,0},{16,8},{24,16},{32,24},{40,32},{48,40},{56,48},{64,56},{72,6... | collective-permute-start | bytes 786440 | tf_op jit(solution)/shard_map/ppermute | solution.py:332
  32.0 11.3 %collective-permute-start.2 = (f32[32,2048]{1,0:T(8,128)S(1)}, f32[32,2048]{1,0:T(8,128)S(1)}, u32[]{:S(2)}, u32[]{:S(2)}) collective-permute-start(f32[32,2048]{1,0:T(8,128)S(1)} %apply_0.1.refs_0_.refs_3_), channel_id=1, source_target_pairs={{0,8},{8,16},{16,24},{24,32},{32,40},{40,48},{48,56},{56,64},{64,7... | collective-permute-start | bytes 786440 | tf_op jit(solution)/shard_map/ppermute | solution.py:331
  46.0 7.1 %collective-permute-start.5 = (f32[32,2048]{1,0:T(8,128)S(1)}, f32[32,2048]{1,0:T(8,128)S(1)}, u32[]{:S(2)}, u32[]{:S(2)}) collective-permute-start(f32[32,2048]{1,0:T(8,128)S(1)} %apply_1.1.refs_0_), channel_id=1, source_target_pairs={{8,0},{16,8},{24,16},{32,24},{40,32},{48,40},{56,48},{64,56},{72,6... | collective-permute-start | bytes 786440 | tf_op jit(solution)/shard_map/ppermute | solution.py:332
  47.9 10.4 %collective-permute-start.4 = (f32[32,2048]{1,0:T(8,128)S(1)}, f32[32,2048]{1,0:T(8,128)S(1)}, u32[]{:S(2)}, u32[]{:S(2)}) collective-permute-start(f32[32,2048]{1,0:T(8,128)S(1)} %apply_1.1.refs_0_), channel_id=1, source_target_pairs={{0,8},{8,16},{16,24},{24,32},{32,40},{40,48},{48,56},{56,64},{64,7... | collective-permute-start | bytes 786440 | tf_op jit(solution)/shard_map/ppermute | solution.py:331

commit v4 on v3

--- a/solution.py
+++ b/solution.py
@@ -14,7 +14,6 @@
 SMEM = pl.BlockSpec(memory_space=pltpu.SMEM)
 NB = 64
 PACKED = 320
-PLANE = 64
 BUILD_UNROLL = 8
 PAIR_UNROLL = 8
 PARAMS = pltpu.CompilerParams(vmem_limit_bytes=20 * 1024 * 1024)
@@ -56,17 +55,17 @@
 
 def apply_kernel(stage, slot_ref, bounds_ref, *refs):
     if stage == 0:
-        f_ref, low_ref, high_ref, w_ref, out_ref, e_ref = refs
+        f_ref, inner_ref, outer_ref, w_ref, out_ref, e_ref = refs
         prev_ref = None
     else:
-        f_ref, low_ref, high_ref, prev_ref, w_ref, out_ref, e_ref = refs
+        f_ref, inner_ref, outer_ref, prev_ref, w_ref, out_ref, e_ref = refs
     width = f_ref.shape[0]
     tiles = f_ref.shape[1] // 128
     left = lax.broadcasted_iota(jnp.int32, (width, 128), 1) < 64
     left2 = lax.broadcasted_iota(jnp.int32, (2 * width, 128), 1) < 64
 
     def build(t, carry):
-        for part, ref in enumerate((low_ref, f_ref, high_ref)):
+        for part, ref in enumerate((inner_ref, f_ref, outer_ref)):
             x = ref[:, pl.ds(pl.multiple_of(t * 128, 128), 128)]
             for v, y in enumerate((x, pltpu.roll(x, 64, 1))):
                 hi, lo = split(y)
@@ -110,10 +109,10 @@
     lax.fori_loop(0, tiles, pair, 0, unroll=PAIR_UNROLL)
 
 
-def apply_step(stage, slot_table, bounds, f, low, high, prev, w):
+def apply_step(stage, slot_table, bounds, f, inner, outer, prev, w):
     width, n = f.shape
     tiles = n // 128
-    args = (f, low, high) + (() if prev is None else (prev,)) + (w,)
+    args = (f, inner, outer) + (() if prev is None else (prev,)) + (w,)
     out = (width, n) if stage < 2 else (tiles, width, 128)
     return pl.pallas_call(
         functools.partial(apply_kernel, stage),
@@ -126,11 +125,14 @@
     )(slot_table, bounds, *map(near, args))
 
 
-def slot_places(columns, first_row, block_rows, total_rows):
-    reach = jnp.mod(columns - first_row + block_rows, total_rows)
+def slot_places(columns, row, block_rows, total_rows):
+    reach = jnp.mod(columns - (row - 1) * block_rows, total_rows)
+    side, inner = reach // block_rows, reach % block_rows
+    side = jnp.where(row % 2 == 0, 2 - side, side)
     right = jnp.arange(columns.shape[1], dtype=jnp.int32) % 2
-    exchanged = (reach + right) % 2
-    return (exchanged * (3 * block_rows // 2) + reach // 2).reshape(-1)
+    exchanged = (inner + right) % 2
+    tiles = block_rows // 2
+    return ((exchanged * 3 + side) * tiles + inner // 2).reshape(-1)
 
 
 def square():
@@ -298,10 +300,24 @@
 
 def sum_over_devices(packed):
     axes = ("row", "bundle")
-    count = lax.axis_size("row") * lax.axis_size("bundle")
-    planes = count // PLANE
-    plane = [[p * PLANE + i for i in range(PLANE)] for p in range(planes)]
-    across = [[p * PLANE + i for p in range(planes)] for i in range(PLANE)]
+    rows, bundles = lax.axis_size("row"), lax.axis_size("bundle")
+    chips, planes = bundles // 2, 8
+    line = rows // planes
+    part = chips * line
+
+    def device(z, y, x, core):
+        return ((z * line + y) * chips + x) * 2 + core
+
+    plane = [
+        [device(z, y, x, core) for y in range(line) for x in range(chips)]
+        for z in range(planes)
+        for core in range(2)
+    ]
+    across = [
+        [device(z, y, x, core) for z in range(planes) for core in range(2)]
+        for y in range(line)
+        for x in range(chips)
+    ]
 
     def exchange(x, groups):
         return lax.all_to_all(
@@ -311,9 +327,9 @@
     def copies(x, n):
         return jnp.broadcast_to(x[None], (n,) + x.shape)
 
-    mine = jnp.sum(exchange(packed.reshape(PLANE, 1, -1), plane), axis=0)
-    mine = jnp.sum(exchange(copies(mine, planes), across), axis=0)
-    return exchange(copies(mine, PLANE), plane).reshape(packed.shape)
+    mine = jnp.sum(exchange(packed.reshape(part, 1, -1), plane), axis=0)
+    mine = jnp.sum(exchange(copies(mine, 2 * planes), across), axis=0)
+    return exchange(copies(mine, part), plane).reshape(packed.shape)
 
 
 def local(vectors, blocks, columns, bounds):
@@ -321,29 +337,32 @@
     row_count = lax.axis_size("row")
     bundles = lax.axis_size("bundle")
     total_rows = block_rows * row_count
-    first_row = lax.axis_index("row") * block_rows
-    places = slot_places(columns, first_row, block_rows, total_rows)
-    forward = [(i, (i + 1) % row_count) for i in range(row_count)]
-    backward = [(j, i) for i, j in forward]
+    places = slot_places(
+        columns, lax.axis_index("row"), block_rows, total_rows
+    )
+    inside = [(i, i ^ 1) for i in range(row_count)]
+    outside = [
+        (i, (i + 1 if i % 2 else i - 1) % row_count) for i in range(row_count)
+    ]
 
     def sides(field):
         return (
-            lax.ppermute(field, "row", forward),
-            lax.ppermute(field, "row", backward),
+            lax.ppermute(field, "row", inside),
+            lax.ppermute(field, "row", outside),
         )
 
-    low, high = sides(vectors)
+    inner, outer = sides(vectors)
     w = split_blocks(blocks)
     first = apply_step(
-        0, places, bounds, vectors, low, high, None, w
-    )
-    low, high = sides(first)
+        0, places, bounds, vectors, inner, outer, None, w
+    )
+    inner, outer = sides(first)
     second = apply_step(
-        1, places, bounds, first, low, high, vectors, w
-    )
-    low, high = sides(second)
+        1, places, bounds, first, inner, outer, vectors, w
+    )
+    inner, outer = sides(second)
     filtered = apply_step(
-        2, places, bounds, second, low, high, first, w
+        2, places, bounds, second, inner, outer, first, w
     )
     tiles, width, lanes = filtered.shape
     stacked = lax.all_to_all(

time: 129 us -> 121 us (0.938)
  waiting for transfers between devices: 22 us -> 15.2 us
  blocking collectives: 56.2 us -> 53.5 us
  starting transfers between devices: 26.9 us -> 28.5 us
    ppermute x6, waiting for transfers between devices: 22 us -> 15.2 us  [the longest x3 10.4 us: sides(): lax.ppermute(field, 'row', outside)]
    all_to_all x3, blocking collectives: 41.8 us -> 38.8 us  [exchange(): return lax.all_to_all(x, axes, 0, 0, axis_index_groups=groups, tiled=True)]
    ppermute x6, starting transfers between devices: 26.9 us -> 28.5 us  [the longest x3 22.7 us: sides(): lax.ppermute(field, 'row', outside)]
  transfers between devices with their start and end apart: 6 -> 6, of which waited for: 5 -> 6; matrix products, arithmetic and copies ran while one was open for 1% -> 1% of each run, Pallas kernels for 0% -> 0%
where the time goes in v4:
time: 121 us; the launch traced here: 120 us
  blocking collectives  53.5 us (44%)
  starting transfers between devices  28.5 us (24%)
  Pallas kernels  19.3 us (16%)
  waiting for transfers between devices  15.2 us (13%)
  local copies, waits for them, and re-layouts  2.21 us (2%)
    all_to_all x3, blocking collectives, exchange(): return lax.all_to_all(x, axes, 0, 0, axis_index_groups=groups, tiled=True)  38.8 us
    ppermute x3, starting transfers between devices, sides(): lax.ppermute(field, 'row', outside)  22.7 us
    all_to_all x1, blocking collectives, local(): lax.all_to_all(filtered.reshape(bundles, tiles // bundles, width, lanes),...  14.6 us
    ppermute x3, waiting for transfers between devices, sides(): lax.ppermute(field, 'row', outside)  10.4 us
    pallas_call x1, Pallas kernels, orthonormalize(): pl.pallas_call(solve_kernel, out_shape=(jax.ShapeDtypeStruct((k, n), F32)...  10.2 us
    pallas_call x3, Pallas kernels, apply_step(): pl.pallas_call(functools.partial(apply_kernel, stage), out_shape=pltpu.VM...  8.15 us
    ppermute x3, starting transfers between devices, sides(): lax.ppermute(field, 'row', inside)  5.76 us
    ppermute x3, waiting for transfers between devices, sides(): lax.ppermute(field, 'row', inside)  4.79 us
  transfers between devices with their start and end apart: 6, of which 6 were waited for; matrix products, arithmetic and copies ran while one was open for 1% of the time, Pallas kernels for 0%

profile of v4, /device:TPU:1, one launch (start us, length us, event | category | flops | bytes accessed | tf_op | source)
XLA Modules:
  0.0 120.3 jit_solution(3111917255420169720)
XLA Ops:
  0.6 14.4 %collective-permute-start.1 = (f32[32,2048]{1,0:T(8,128)}, f32[32,2048]{1,0:T(8,128)S(1)}, u32[]{:S(2)}, u32[]{:S(2)}) collective-permute-start(f32[32,2048]{1,0:T(8,128)} %refs_3_.1), channel_id=1, source_target_pairs={{0,504},{8,16},{16,8},{24,32},{32,24},{40,48},{48,40},{56,64},{64,... | collective-permute-start | bytes 786440 | tf_op jit(solution)/shard_map/ppermute | solution.py:351
  15.0 1.9 %collective-permute-start = (f32[32,2048]{1,0:T(8,128)}, f32[32,2048]{1,0:T(8,128)S(1)}, u32[]{:S(2)}, u32[]{:S(2)}) collective-permute-start(f32[32,2048]{1,0:T(8,128)} %refs_3_.1), channel_id=1, source_target_pairs={{0,8},{8,0},{16,24},{24,16},{32,40},{40,32},{48,56},{56,48},{64,72... | collective-permute-start | bytes 786440 | tf_op jit(solution)/shard_map/ppermute | solution.py:350
  17.0 0.8 fusion.5
  18.0 1.9 %copy-done = f32[32,64,384]{2,1,0:T(8,128)S(1)} copy-done((f32[32,64,384]{2,1,0:T(8,128)S(1)}, f32[32,64,384]{2,1,0:T(8,128)}, u32[]{:S(2)}) %copy-start) | copy-done | bytes 3145752
  19.8 0.5 split_blocks.1.refs_3_.refs_4_
  20.4 0.9 collective-permute-done.1.refs_2_
  21.2 2.8 %collective-permute-done.refs_1_ = f32[32,2048]{1,0:T(8,128)S(1)} collective-permute-done((f32[32,2048]{1,0:T(8,128)}, f32[32,2048]{1,0:T(8,128)S(1)}, u32[]{:S(2)}, u32[]{:S(2)}) %collective-permute-start) | collective-permute-done | bytes 262176 | tf_op jit(solution)/shard_map/ppermute | solution.py:350
  24.1 2.7 %apply_0.1.refs_0_.refs_3_ = f32[32,2048]{1,0:T(8,128)S(1)} custom-call(s32[192]{0:T(256)S(1)} %reshape.35.slot_ref, f32[2]{0:T(128)S(1)} %copy-done.2, f32[32,2048]{1,0:T(8,128)S(1)} %copy-done.1, f32[32,2048]{1,0:T(8,128)S(1)} %collective-permute-done.refs_1_, f32[32,2048]{1,0:T(8,128)S(1)} %collective-permute-done.1.refs_2_, ...), custom_call_target="tpu_custom_call" | custom-call | tf_op jit(solution)/shard_map/apply_0/pallas_call | solution.py:117
  26.8 3.6 %collective-permute-start.3 = (f32[32,2048]{1,0:T(8,128)S(1)}, f32[32,2048]{1,0:T(8,128)S(1)}, u32[]{:S(2)}, u32[]{:S(2)}) collective-permute-start(f32[32,2048]{1,0:T(8,128)S(1)} %apply_0.1.refs_0_.refs_3_), channel_id=1, source_target_pairs={{0,504},{8,16},{16,8},{24,32},{32,24},{40,48},{48,40},{56,64},{64,... | collective-permute-start | bytes 786440 | tf_op jit(solution)/shard_map/ppermute | solution.py:351
  30.4 1.9 %collective-permute-start.2 = (f32[32,2048]{1,0:T(8,128)S(1)}, f32[32,2048]{1,0:T(8,128)S(1)}, u32[]{:S(2)}, u32[]{:S(2)}) collective-permute-start(f32[32,2048]{1,0:T(8,128)S(1)} %apply_0.1.refs_0_.refs_3_), channel_id=1, source_target_pairs={{0,8},{8,0},{16,24},{24,16},{32,40},{40,32},{48,56},{56,48},{64,72... | collective-permute-start | bytes 786440 | tf_op jit(solution)/shard_map/ppermute | solution.py:350
  32.3 5.7 %collective-permute-done.3.refs_2_ = f32[32,2048]{1,0:T(8,128)S(1)} collective-permute-done((f32[32,2048]{1,0:T(8,128)S(1)}, f32[32,2048]{1,0:T(8,128)S(1)}, u32[]{:S(2)}, u32[]{:S(2)}) %collective-permute-start.3) | collective-permute-done | bytes 262176 | tf_op jit(solution)/shard_map/ppermute | solution.py:351
  38.0 0.3 collective-permute-done.2.refs_1_
  38.3 2.7 %apply_1.1.refs_0_ = f32[32,2048]{1,0:T(8,128)S(1)} custom-call(s32[192]{0:T(256)S(1)} %reshape.35.slot_ref, f32[2]{0:T(128)S(1)} %copy-done.2, f32[32,2048]{1,0:T(8,128)S(1)} %apply_0.1.refs_0_.refs_3_, f32[32,2048]{1,0:T(8,128)S(1)} %collective-permute-done.2.refs_1_, f32[32,2048]{1,0:T(8,128)S(1)} %collective-permute-done.3.refs_2_, ...), custom_call_target="tpu_custom_call" | custom-call | tf_op jit(solution)/shard_map/apply_1/pallas_call | solution.py:117
  41.0 4.7 %collective-permute-start.5 = (f32[32,2048]{1,0:T(8,128)S(1)}, f32[32,2048]{1,0:T(8,128)S(1)}, u32[]{:S(2)}, u32[]{:S(2)}) collective-permute-start(f32[32,2048]{1,0:T(8,128)S(1)} %apply_1.1.refs_0_), channel_id=1, source_target_pairs={{0,504},{8,16},{16,8},{24,32},{32,24},{40,48},{48,40},{56,64},{64,... | collective-permute-start | bytes 786440 | tf_op jit(solution)/shard_map/ppermute | solution.py:351
  45.8 1.9 %collective-permute-start.4 = (f32[32,2048]{1,0:T(8,128)S(1)}, f32[32,2048]{1,0:T(8,128)S(1)}, u32[]{:S(2)}, u32[]{:S(2)}) collective-permute-start(f32[32,2048]{1,0:T(8,128)S(1)} %apply_1.1.refs_0_), channel_id=1, source_target_pairs={{0,8},{8,0},{16,24},{24,16},{32,40},{40,32},{48,56},{56,48},{64,72... | collective-permute-start | bytes 786440 | tf_op jit(solution)/shard_map/ppermute | solution.py:350
  47.7 3.8 %collective-permute-done.5.refs_2_ = f32[32,2048]{1,0:T(8,128)S(1)} collective-permute-done((f32[32,2048]{1,0:T(8,128)S(1)}, f32[32,2048]{1,0:T(8,128)S(1)}, u32[]{:S(2)}, u32[]{:S(2)}) %collective-permute-start.5) | collective-permute-done | bytes 262176 | tf_op jit(solution)/shard_map/ppermute | solution.py:351
  51.5 1.7 %collective-permute-done.4.refs_1_ = f32[32,2048]{1,0:T(8,128)S(1)} collective-permute-done((f32[32,2048]{1,0:T(8,128)S(1)}, f32[32,2048]{1,0:T(8,128)S(1)}, u32[]{:S(2)}, u32[]{:S(2)}) %collective-permute-start.4) | collective-permute-done | bytes 262176 | tf_op jit(solution)/shard_map/ppermute | solution.py:350
  53.2 2.7 %apply_2.1 = f32[16,32,128]{2,1,0:T(8,128)S(1)} custom-call(s32[192]{0:T(256)S(1)} %reshape.35.slot_ref, f32[2]{0:T(128)S(1)} %copy-done.2, f32[32,2048]{1,0:T(8,128)S(1)} %apply_1.1.refs_0_, f32[32,2048]{1,0:T(8,128)S(1)} %collective-permute-done.4.refs_1_, f32[32,2048]{1,0:T(8,128)S(1)} %collective-permute-done.5.refs_2_, ...), custom_call_target="tpu_custom_call" | custom-call | tf_op jit(solution)/shard_map/apply_2/pallas_call | solution.py:117
  55.9 14.6 %all_to_all.20.s_ref = f32[8,2,32,128]{3,2,1,0:T(8,128)S(1)} all-to-all(f32[8,2,32,128]{3,2,1,0:T(8,128)S(1)} %bitcast.3), channel_id=1, replica_groups=mesh['row'=64,'bundle'=8] {'bundle'}, dimensions={0} | all-to-all | bytes 524288 | tf_op jit(solution)/shard_map/all_to_all | solution.py:368
  70.5 0.4 gram.1
  70.9 12.7 %all_to_all.21 = f32[32,1,1280]{2,1,0:T(1,128)S(1)} all-to-all(f32[32,1,1280]{2,1,0:T(1,128)S(1)} %bitcast.5), channel_id=1, replica_groups={{0,2,4,6,8,10,12,14,16,18,20,22,24,26,28,30,32,34,36,38,40,42,44,46,48,..., dimensions={0} | all-to-all | bytes 327680 | tf_op jit(solution)/shard_map/all_to_all | solution.py:323
  83.8 13.0 %all_to_all.22 = f32[16,1,1280]{2,1,0:T(1,128)S(1)} all-to-all(f32[16,1,1280]{2,1,0:T(1,128)S(1)} %broadcast_in_dim.4), channel_id=1, replica_groups={{0,1,64,65,128,129,192,193,256,257,320,321,384,385,448,449},{2,3,66,67,..., dimensions={0} | all-to-all | bytes 163840 | tf_op jit(solution)/shard_map/all_to_all | solution.py:323
  96.9 13.2 %all_to_all.23 = f32[32,1,1280]{2,1,0:T(1,128)S(1)} all-to-all(f32[32,1,1280]{2,1,0:T(1,128)S(1)} %broadcast_in_dim.5), channel_id=1, replica_groups={{0,2,4,6,8,10,12,14,16,18,20,22,24,26,28,30,32,34,36,38,40,42,44,46,48,..., dimensions={0} | all-to-all | bytes 327680 | tf_op jit(solution)/shard_map/all_to_all | solution.py:323
  110.1 10.2 %orthonormalize.1 = (f32[256,256]{1,0:T(8,128)}, f32[256,256]{1,0:T(8,128)}) custom-call(f32[320,128]{1,0:T(8,128)S(1)} %bitcast.4, f32[8,2,32,128]{3,2,1,0:T(8,128)S(1)} %all_to_all.20.s_ref), custom_call_target="tpu_custom_call" | custom-call | tf_op jit(solution)/shard_map/orthonormalize/pallas_call | solution.py:287
  (12 shorter events, 0.5 us)
Async XLA Ops:
  0.6 20.6 %collective-permute-start.1 = (f32[32,2048]{1,0:T(8,128)}, f32[32,2048]{1,0:T(8,128)S(1)}, u32[]{:S(2)}, u32[]{:S(2)}) collective-permute-start(f32[32,2048]{1,0:T(8,128)} %refs_3_.1), channel_id=1, source_target_pairs={{0,504},{8,16},{16,8},{24,32},{32,24},{40,48},{48,40},{56,64},{64,... | collective-permute-start | bytes 786440 | tf_op jit(solution)/shard_map/ppermute | solution.py:351
  15.0 9.0 %collective-permute-start = (f32[32,2048]{1,0:T(8,128)}, f32[32,2048]{1,0:T(8,128)S(1)}, u32[]{:S(2)}, u32[]{:S(2)}) collective-permute-start(f32[32,2048]{1,0:T(8,128)} %refs_3_.1), channel_id=1, source_target_pairs={{0,8},{8,0},{16,24},{24,16},{32,40},{40,32},{48,56},{56,48},{64,72... | collective-permute-start | bytes 786440 | tf_op jit(solution)/shard_map/ppermute | solution.py:350
  17.9 1.9 %copy-start = (f32[32,64,384]{2,1,0:T(8,128)S(1)}, f32[32,64,384]{2,1,0:T(8,128)}, u32[]{:S(2)}) copy-start(f32[32,64,384]{2,1,0:T(8,128)} %b_ref.1) | copy-start | bytes 9437188
  19.8 4.2 %copy-start.1 = (f32[32,2048]{1,0:T(8,128)S(1)}, f32[32,2048]{1,0:T(8,128)}, u32[]{:S(2)}) copy-start(f32[32,2048]{1,0:T(8,128)} %refs_3_.1) | copy-start | bytes 786436
  19.8 4.2 %copy-start.2 = (f32[2]{0:T(128)S(1)}, f32[2]{0:T(128)}, u32[]{:S(2)}) copy-start(f32[2]{0:T(128)} %bounds_ref.5) | copy-start | bytes 28
  26.8 11.3 %collective-permute-start.3 = (f32[32,2048]{1,0:T(8,128)S(1)}, f32[32,2048]{1,0:T(8,128)S(1)}, u32[]{:S(2)}, u32[]{:S(2)}) collective-permute-start(f32[32,2048]{1,0:T(8,128)S(1)} %apply_0.1.refs_0_.refs_3_), channel_id=1, source_target_pairs={{0,504},{8,16},{16,8},{24,32},{32,24},{40,48},{48,40},{56,64},{64,... | collective-permute-start | bytes 786440 | tf_op jit(solution)/shard_map/ppermute | solution.py:351
  30.4 7.9 %collective-permute-start.2 = (f32[32,2048]{1,0:T(8,128)S(1)}, f32[32,2048]{1,0:T(8,128)S(1)}, u32[]{:S(2)}, u32[]{:S(2)}) collective-permute-start(f32[32,2048]{1,0:T(8,128)S(1)} %apply_0.1.refs_0_.refs_3_), channel_id=1, source_target_pairs={{0,8},{8,0},{16,24},{24,16},{32,40},{40,32},{48,56},{56,48},{64,72... | collective-permute-start | bytes 786440 | tf_op jit(solution)/shard_map/ppermute | solution.py:350
  41.0 10.4 %collective-permute-start.5 = (f32[32,2048]{1,0:T(8,128)S(1)}, f32[32,2048]{1,0:T(8,128)S(1)}, u32[]{:S(2)}, u32[]{:S(2)}) collective-permute-start(f32[32,2048]{1,0:T(8,128)S(1)} %apply_1.1.refs_0_), channel_id=1, source_target_pairs={{0,504},{8,16},{16,8},{24,32},{32,24},{40,48},{48,40},{56,64},{64,... | collective-permute-start | bytes 786440 | tf_op jit(solution)/shard_map/ppermute | solution.py:351
  45.8 7.4 %collective-permute-start.4 = (f32[32,2048]{1,0:T(8,128)S(1)}, f32[32,2048]{1,0:T(8,128)S(1)}, u32[]{:S(2)}, u32[]{:S(2)}) collective-permute-start(f32[32,2048]{1,0:T(8,128)S(1)} %apply_1.1.refs_0_), channel_id=1, source_target_pairs={{0,8},{8,0},{16,24},{24,16},{32,40},{40,32},{48,56},{56,48},{64,72... | collective-permute-start | bytes 786440 | tf_op jit(solution)/shard_map/ppermute | solution.py:350

commit v5 on v4

--- a/solution.py
+++ b/solution.py
@@ -34,9 +34,10 @@
 
 
 def split_kernel(b_ref, w_ref):
-    hi, lo = split(b_ref[...])
-    w_ref[:, 0:64, :] = hi
-    w_ref[:, 64:128, :] = lo
+    for i in range(b_ref.shape[0]):
+        hi, lo = split(b_ref[i])
+        both = jnp.concatenate([hi.astype(F32), lo.astype(F32)], axis=0)
+        w_ref[i] = both.T.astype(BF)
 
 
 def split_blocks(blocks):
@@ -44,10 +45,10 @@
     step = 8
     return pl.pallas_call(
         split_kernel,
-        out_shape=pltpu.VMEM((n, 2 * a, m), BF),
+        out_shape=pltpu.VMEM((n, m, 2 * a), BF),
         grid=(n // step,),
         in_specs=[pl.BlockSpec((step, a, m), lambda i: (i, 0, 0))],
-        out_specs=pl.BlockSpec((step, 2 * a, m), lambda i: (i, 0, 0)),
+        out_specs=pl.BlockSpec((step, m, 2 * a), lambda i: (i, 0, 0)),
         compiler_params=PARAMS,
         name="split_blocks",
     )(blocks)
@@ -78,7 +79,7 @@
 
     center = (bounds_ref[0] + bounds_ref[1]) * 0.5
     half = (bounds_ref[1] - bounds_ref[0]) * 0.5
-    slots = w_ref.shape[2] // 64
+    slots = w_ref.shape[1] // 64
 
     def one(i):
         at = [slot_ref[i * slots + s] for s in range(slots)]
@@ -89,7 +90,7 @@
             ],
             axis=1,
         )
-        out = dot_nt(lhs, w_ref[i])
+        out = dot_nn(lhs, w_ref[i])
         acc = out[:width] + jnp.where(left, out[width:], 0.0)
         return acc + pltpu.roll(acc, 64, 1)
 
@@ -188,33 +189,42 @@
     here = [sub == k for k in range(8)]
     vregs = [m[8 * v : 8 * v + 8] for v in range(n // 8)]
     done = []
+
+    def update(some, v0, z):
+        sums = {}
+        for k in range(8):
+            for v in some:
+                t = lane_of(vregs[v], 8 * v0 + k) * z[k]
+                sums[v] = sums[v] + t if k else t
+        for v in some:
+            vregs[v] = vregs[v] - sums[v]
+
     for v0 in range(n // 8):
         head = vregs[v0]
-        cols = [
-            [lane_of(vregs[v], 8 * v0 + c) for c in range(8)]
-            for v in range(v0, n // 8)
-        ]
-        p = list(cols[0])
+        p = [lane_of(head, 8 * v0 + c) for c in range(8)]
         out = jnp.zeros((8, 128), F32)
-        for k in range(8):
-            pivot = row_of(p[k], k)
-            inv = 1.0 / pivot
-            row = row_of(head, k)
-            out = jnp.where(here[k], row * lax.rsqrt(pivot), out)
-            for c in range(k + 1, 8):
-                r = row_of(p[c], k) * inv
-                p[c] = jnp.where(here[k], r, p[c] - p[k] * r)
-            r = row * inv
-            head = jnp.where(here[k], r, head - p[k] * r)
+        for k in range(0, 8, 2):
+            a, b, d = row_of(p[k], k), row_of(p[k + 1], k), row_of(p[k + 1], k + 1)
+            det = a * d - b * b
+            inv = 1.0 / det
+
+            def eliminate(x):
+                s0, s1 = row_of(x, k), row_of(x, k + 1)
+                w0, w1 = d * s0 - b * s1, a * s1 - b * s0
+                y = x - (p[k] * w0 + p[k + 1] * w1) * inv
+                y = jnp.where(here[k], w0 * inv, y)
+                return jnp.where(here[k + 1], w1 * inv, y), s0, w1
+
+            for c in range(k + 2, 8):
+                p[c] = eliminate(p[c])[0]
+            head, s0, w1 = eliminate(head)
+            out = jnp.where(here[k], s0 * lax.rsqrt(a), out)
+            out = jnp.where(here[k + 1], w1 * lax.rsqrt(a * det), out)
         done.append(out)
-        if v0 + 1 == n // 8:
-            break
         z = [row_of(head, k) for k in range(8)]
-        for v in range(v0 + 1, n // 8):
-            t = [cols[v - v0][k] * z[k] for k in range(8)]
-            while len(t) > 1:
-                t = [t[i] + t[i + 1] for i in range(0, len(t), 2)]
-            vregs[v] = vregs[v] - t[0]
+        for some in ([v0 + 1], list(range(v0 + 2, n // 8))):
+            if some and some[0] < n // 8:
+                update(some, v0, z)
     return jnp.concatenate(done, axis=0)
 
 
@@ -246,12 +256,24 @@
     row, col = square()
     mixed = g_ref[128:256]
     turned = mixed.T
-    a_ref[:128, :128] = jnp.where(row >= col, mixed, turned)
-    a_ref[:128, 128:k] = g_ref[0:128]
+    diag = [
+        jnp.sum(jnp.where(row == col, mixed, 0.0), axis=0, keepdims=True),
+        g_ref[256:257],
+    ]
+    right = [jnp.broadcast_to(lax.rsqrt(d), (128, 128)) for d in diag]
+    left = [r.T for r in right]
+    size = [jnp.sqrt(d) for d in diag]
+    a_ref[:128, :128] = jnp.where(row >= col, mixed, turned) * left[0] * right[0]
+    a_ref[:128, 128:k] = g_ref[0:128] * left[0] * right[1]
     last = jnp.where(row < col, mixed, turned)
-    a_ref[128:, 128:k] = jnp.where(row == col, g_ref[256:257], last)
+    last = jnp.where(row == col, diag[1], last)
+    a_ref[128:, 128:k] = last * left[1] * right[1]
     for j in range(s_ref.shape[1]):
-        a_ref[:, k + j * 128 : k + (j + 1) * 128] = s_ref[:, j].reshape(k, 128)
+        at = k + j * 128
+        part = s_ref[:, j].reshape(k, 128)
+        a_ref[:128, at : at + 128] = part[:128] * left[0]
+        a_ref[128:, at : at + 128] = part[128:] * left[1]
+    size = jnp.concatenate(size, axis=1)
     lane = lax.broadcasted_iota(jnp.int32, (NB, 128), 1)
     sub = lax.broadcasted_iota(jnp.int32, (NB, 128), 0)
     eye = jnp.where(lane == sub + NB, 1.0, 0.0)
@@ -266,7 +288,7 @@
         x = dot_nn(six_lanes(twice), six_rows(a_ref[rows, at:]))
         col_id = at + lax.broadcasted_iota(jnp.int32, (NB, k - at), 1)
         row_id = first + lax.broadcasted_iota(jnp.int32, (NB, k - at), 0)
-        upper = jnp.where(col_id >= row_id, x[:, : k - at], 0.0)
+        upper = jnp.where(col_id >= row_id, x[:, : k - at] * size[:, at:], 0.0)
         if at > 0:
             upper = jnp.concatenate([jnp.zeros((NB, at), F32), upper], axis=1)
         factor_ref[rows, :] = upper

time: 121 us -> 117 us (0.967)
  Pallas kernels: 19.3 us -> 16.5 us
    pallas_call x3, Pallas kernels: 8.15 us -> 6.13 us  [apply_step(): pl.pallas_call(functools.partial(apply_kernel, stage), out_shape=pltpu.VM...]
    pallas_call x1, Pallas kernels: 10.2 us -> 8.81 us  [orthonormalize(): pl.pallas_call(solve_kernel, out_shape=(jax.ShapeDtypeStruct((k, n), F32)...]
  transfers between devices with their start and end apart: 6 -> 6, of which waited for: 6 -> 6; matrix products, arithmetic and copies ran while one was open for 1% -> 1% of each run, Pallas kernels for 0% -> 1%
where the time goes in v5:
time: 117 us
  blocking collectives  53.5 us (46%)
  starting transfers between devices  28.5 us (24%)
  Pallas kernels  16.5 us (14%)
  waiting for transfers between devices  14.5 us (12%)
  local copies, waits for them, and re-layouts  2.21 us (2%)
    all_to_all x3, blocking collectives, exchange(): return lax.all_to_all(x, axes, 0, 0, axis_index_groups=groups, tiled=True)  38.8 us
    ppermute x3, starting transfers between devices, sides(): lax.ppermute(field, 'row', outside)  22.7 us
    all_to_all x1, blocking collectives, local(): lax.all_to_all(filtered.reshape(bundles, tiles // bundles, width, lanes),...  14.6 us
    ppermute x3, waiting for transfers between devices, sides(): lax.ppermute(field, 'row', outside)  9.74 us
    pallas_call x1, Pallas kernels, orthonormalize(): pl.pallas_call(solve_kernel, out_shape=(jax.ShapeDtypeStruct((k, n), F32)...  8.81 us
    pallas_call x3, Pallas kernels, apply_step(): pl.pallas_call(functools.partial(apply_kernel, stage), out_shape=pltpu.VM...  6.13 us
    ppermute x3, starting transfers between devices, sides(): lax.ppermute(field, 'row', inside)  5.76 us
    ppermute x3, waiting for transfers between devices, sides(): lax.ppermute(field, 'row', inside)  4.81 us
  transfers between devices with their start and end apart: 6, of which 6 were waited for; matrix products, arithmetic and copies ran while one was open for 1% of the time, Pallas kernels for 1%

profile of v5, /device:TPU:1, one launch (start us, length us, event | category | flops | bytes accessed | tf_op | source)
XLA Modules:
  0.0 116.9 jit_solution(3840229870422494797)
XLA Ops:
  0.6 14.4 %collective-permute-start.1 = (f32[32,2048]{1,0:T(8,128)}, f32[32,2048]{1,0:T(8,128)S(1)}, u32[]{:S(2)}, u32[]{:S(2)}) collective-permute-start(f32[32,2048]{1,0:T(8,128)} %refs_3_.1), channel_id=1, source_target_pairs={{0,504},{8,16},{16,8},{24,32},{32,24},{40,48},{48,40},{56,64},{64,... | collective-permute-start | bytes 786440 | tf_op jit(solution)/shard_map/ppermute | solution.py:373
  15.0 1.9 %collective-permute-start = (f32[32,2048]{1,0:T(8,128)}, f32[32,2048]{1,0:T(8,128)S(1)}, u32[]{:S(2)}, u32[]{:S(2)}) collective-permute-start(f32[32,2048]{1,0:T(8,128)} %refs_3_.1), channel_id=1, source_target_pairs={{0,8},{8,0},{16,24},{24,16},{32,40},{40,32},{48,56},{56,48},{64,72... | collective-permute-start | bytes 786440 | tf_op jit(solution)/shard_map/ppermute | solution.py:372
  17.0 0.8 fusion.5
  18.0 1.9 %copy-done = f32[32,64,384]{2,1,0:T(8,128)S(1)} copy-done((f32[32,64,384]{2,1,0:T(8,128)S(1)}, f32[32,64,384]{2,1,0:T(8,128)}, u32[]{:S(2)}) %copy-start) | copy-done | bytes 3145752
  19.8 1.1 split_blocks.1.refs_3_.refs_4_
  21.0 0.2 collective-permute-done.1.refs_2_
  21.2 2.8 %collective-permute-done.refs_1_ = f32[32,2048]{1,0:T(8,128)S(1)} collective-permute-done((f32[32,2048]{1,0:T(8,128)}, f32[32,2048]{1,0:T(8,128)S(1)}, u32[]{:S(2)}, u32[]{:S(2)}) %collective-permute-start) | collective-permute-done | bytes 262176 | tf_op jit(solution)/shard_map/ppermute | solution.py:372
  24.1 2.0 %apply_0.1.refs_0_.refs_3_ = f32[32,2048]{1,0:T(8,128)S(1)} custom-call(s32[192]{0:T(256)S(1)} %reshape.35.slot_ref, f32[2]{0:T(128)S(1)} %copy-done.2, f32[32,2048]{1,0:T(8,128)S(1)} %copy-done.1, f32[32,2048]{1,0:T(8,128)S(1)} %collective-permute-done.refs_1_, f32[32,2048]{1,0:T(8,128)S(1)} %collective-permute-done.1.refs_2_, ...), custom_call_target="tpu_custom_call" | custom-call | tf_op jit(solution)/shard_map/apply_0/pallas_call | solution.py:118
  26.1 3.6 %collective-permute-start.3 = (f32[32,2048]{1,0:T(8,128)S(1)}, f32[32,2048]{1,0:T(8,128)S(1)}, u32[]{:S(2)}, u32[]{:S(2)}) collective-permute-start(f32[32,2048]{1,0:T(8,128)S(1)} %apply_0.1.refs_0_.refs_3_), channel_id=1, source_target_pairs={{0,504},{8,16},{16,8},{24,32},{32,24},{40,48},{48,40},{56,64},{64,... | collective-permute-start | bytes 786440 | tf_op jit(solution)/shard_map/ppermute | solution.py:373
  29.7 1.9 %collective-permute-start.2 = (f32[32,2048]{1,0:T(8,128)S(1)}, f32[32,2048]{1,0:T(8,128)S(1)}, u32[]{:S(2)}, u32[]{:S(2)}) collective-permute-start(f32[32,2048]{1,0:T(8,128)S(1)} %apply_0.1.refs_0_.refs_3_), channel_id=1, source_target_pairs={{0,8},{8,0},{16,24},{24,16},{32,40},{40,32},{48,56},{56,48},{64,72... | collective-permute-start | bytes 786440 | tf_op jit(solution)/shard_map/ppermute | solution.py:372
  31.6 5.7 %collective-permute-done.3.refs_2_ = f32[32,2048]{1,0:T(8,128)S(1)} collective-permute-done((f32[32,2048]{1,0:T(8,128)S(1)}, f32[32,2048]{1,0:T(8,128)S(1)}, u32[]{:S(2)}, u32[]{:S(2)}) %collective-permute-start.3) | collective-permute-done | bytes 262176 | tf_op jit(solution)/shard_map/ppermute | solution.py:373
  37.4 0.3 collective-permute-done.2.refs_1_
  37.6 2.1 %apply_1.1.refs_0_ = f32[32,2048]{1,0:T(8,128)S(1)} custom-call(s32[192]{0:T(256)S(1)} %reshape.35.slot_ref, f32[2]{0:T(128)S(1)} %copy-done.2, f32[32,2048]{1,0:T(8,128)S(1)} %apply_0.1.refs_0_.refs_3_, f32[32,2048]{1,0:T(8,128)S(1)} %collective-permute-done.2.refs_1_, f32[32,2048]{1,0:T(8,128)S(1)} %collective-permute-done.3.refs_2_, ...), custom_call_target="tpu_custom_call" | custom-call | tf_op jit(solution)/shard_map/apply_1/pallas_call | solution.py:118
  39.7 4.7 %collective-permute-start.5 = (f32[32,2048]{1,0:T(8,128)S(1)}, f32[32,2048]{1,0:T(8,128)S(1)}, u32[]{:S(2)}, u32[]{:S(2)}) collective-permute-start(f32[32,2048]{1,0:T(8,128)S(1)} %apply_1.1.refs_0_), channel_id=1, source_target_pairs={{0,504},{8,16},{16,8},{24,32},{32,24},{40,48},{48,40},{56,64},{64,... | collective-permute-start | bytes 786440 | tf_op jit(solution)/shard_map/ppermute | solution.py:373
  44.4 1.9 %collective-permute-start.4 = (f32[32,2048]{1,0:T(8,128)S(1)}, f32[32,2048]{1,0:T(8,128)S(1)}, u32[]{:S(2)}, u32[]{:S(2)}) collective-permute-start(f32[32,2048]{1,0:T(8,128)S(1)} %apply_1.1.refs_0_), channel_id=1, source_target_pairs={{0,8},{8,0},{16,24},{24,16},{32,40},{40,32},{48,56},{56,48},{64,72... | collective-permute-start | bytes 786440 | tf_op jit(solution)/shard_map/ppermute | solution.py:372
  46.4 3.8 %collective-permute-done.5.refs_2_ = f32[32,2048]{1,0:T(8,128)S(1)} collective-permute-done((f32[32,2048]{1,0:T(8,128)S(1)}, f32[32,2048]{1,0:T(8,128)S(1)}, u32[]{:S(2)}, u32[]{:S(2)}) %collective-permute-start.5) | collective-permute-done | bytes 262176 | tf_op jit(solution)/shard_map/ppermute | solution.py:373
  50.1 1.7 %collective-permute-done.4.refs_1_ = f32[32,2048]{1,0:T(8,128)S(1)} collective-permute-done((f32[32,2048]{1,0:T(8,128)S(1)}, f32[32,2048]{1,0:T(8,128)S(1)}, u32[]{:S(2)}, u32[]{:S(2)}) %collective-permute-start.4) | collective-permute-done | bytes 262176 | tf_op jit(solution)/shard_map/ppermute | solution.py:372
  51.8 2.1 %apply_2.1 = f32[16,32,128]{2,1,0:T(8,128)S(1)} custom-call(s32[192]{0:T(256)S(1)} %reshape.35.slot_ref, f32[2]{0:T(128)S(1)} %copy-done.2, f32[32,2048]{1,0:T(8,128)S(1)} %apply_1.1.refs_0_, f32[32,2048]{1,0:T(8,128)S(1)} %collective-permute-done.4.refs_1_, f32[32,2048]{1,0:T(8,128)S(1)} %collective-permute-done.5.refs_2_, ...), custom_call_target="tpu_custom_call" | custom-call | tf_op jit(solution)/shard_map/apply_2/pallas_call | solution.py:118
  53.9 14.6 %all_to_all.20.s_ref = f32[8,2,32,128]{3,2,1,0:T(8,128)S(1)} all-to-all(f32[8,2,32,128]{3,2,1,0:T(8,128)S(1)} %bitcast.3), channel_id=1, replica_groups=mesh['row'=64,'bundle'=8] {'bundle'}, dimensions={0} | all-to-all | bytes 524288 | tf_op jit(solution)/shard_map/all_to_all | solution.py:390
  68.5 0.4 gram.1
  69.0 12.7 %all_to_all.21 = f32[32,1,1280]{2,1,0:T(1,128)S(1)} all-to-all(f32[32,1,1280]{2,1,0:T(1,128)S(1)} %bitcast.5), channel_id=1, replica_groups={{0,2,4,6,8,10,12,14,16,18,20,22,24,26,28,30,32,34,36,38,40,42,44,46,48,..., dimensions={0} | all-to-all | bytes 327680 | tf_op jit(solution)/shard_map/all_to_all | solution.py:345
  81.8 13.0 %all_to_all.22 = f32[16,1,1280]{2,1,0:T(1,128)S(1)} all-to-all(f32[16,1,1280]{2,1,0:T(1,128)S(1)} %broadcast_in_dim.4), channel_id=1, replica_groups={{0,1,64,65,128,129,192,193,256,257,320,321,384,385,448,449},{2,3,66,67,..., dimensions={0} | all-to-all | bytes 163840 | tf_op jit(solution)/shard_map/all_to_all | solution.py:345
  94.9 13.2 %all_to_all.23 = f32[32,1,1280]{2,1,0:T(1,128)S(1)} all-to-all(f32[32,1,1280]{2,1,0:T(1,128)S(1)} %broadcast_in_dim.5), channel_id=1, replica_groups={{0,2,4,6,8,10,12,14,16,18,20,22,24,26,28,30,32,34,36,38,40,42,44,46,48,..., dimensions={0} | all-to-all | bytes 327680 | tf_op jit(solution)/shard_map/all_to_all | solution.py:345
  108.1 8.8 %orthonormalize.1 = (f32[256,256]{1,0:T(8,128)}, f32[256,256]{1,0:T(8,128)}) custom-call(f32[320,128]{1,0:T(8,128)S(1)} %bitcast.4, f32[8,2,32,128]{3,2,1,0:T(8,128)S(1)} %all_to_all.20.s_ref), custom_call_target="tpu_custom_call" | custom-call | tf_op jit(solution)/shard_map/orthonormalize/pallas_call | solution.py:309
  (12 shorter events, 0.5 us)
Async XLA Ops:
  0.6 20.6 %collective-permute-start.1 = (f32[32,2048]{1,0:T(8,128)}, f32[32,2048]{1,0:T(8,128)S(1)}, u32[]{:S(2)}, u32[]{:S(2)}) collective-permute-start(f32[32,2048]{1,0:T(8,128)} %refs_3_.1), channel_id=1, source_target_pairs={{0,504},{8,16},{16,8},{24,32},{32,24},{40,48},{48,40},{56,64},{64,... | collective-permute-start | bytes 786440 | tf_op jit(solution)/shard_map/ppermute | solution.py:373
  15.0 9.0 %collective-permute-start = (f32[32,2048]{1,0:T(8,128)}, f32[32,2048]{1,0:T(8,128)S(1)}, u32[]{:S(2)}, u32[]{:S(2)}) collective-permute-start(f32[32,2048]{1,0:T(8,128)} %refs_3_.1), channel_id=1, source_target_pairs={{0,8},{8,0},{16,24},{24,16},{32,40},{40,32},{48,56},{56,48},{64,72... | collective-permute-start | bytes 786440 | tf_op jit(solution)/shard_map/ppermute | solution.py:372
  17.9 1.9 %copy-start = (f32[32,64,384]{2,1,0:T(8,128)S(1)}, f32[32,64,384]{2,1,0:T(8,128)}, u32[]{:S(2)}) copy-start(f32[32,64,384]{2,1,0:T(8,128)} %b_ref.1) | copy-start | bytes 9437188
  19.8 4.2 %copy-start.1 = (f32[32,2048]{1,0:T(8,128)S(1)}, f32[32,2048]{1,0:T(8,128)}, u32[]{:S(2)}) copy-start(f32[32,2048]{1,0:T(8,128)} %refs_3_.1) | copy-start | bytes 786436
  19.8 4.2 %copy-start.2 = (f32[2]{0:T(128)S(1)}, f32[2]{0:T(128)}, u32[]{:S(2)}) copy-start(f32[2]{0:T(128)} %bounds_ref.5) | copy-start | bytes 28
  26.1 11.3 %collective-permute-start.3 = (f32[32,2048]{1,0:T(8,128)S(1)}, f32[32,2048]{1,0:T(8,128)S(1)}, u32[]{:S(2)}, u32[]{:S(2)}) collective-permute-start(f32[32,2048]{1,0:T(8,128)S(1)} %apply_0.1.refs_0_.refs_3_), channel_id=1, source_target_pairs={{0,504},{8,16},{16,8},{24,32},{32,24},{40,48},{48,40},{56,64},{64,... | collective-permute-start | bytes 786440 | tf_op jit(solution)/shard_map/ppermute | solution.py:373
  29.7 7.9 %collective-permute-start.2 = (f32[32,2048]{1,0:T(8,128)S(1)}, f32[32,2048]{1,0:T(8,128)S(1)}, u32[]{:S(2)}, u32[]{:S(2)}) collective-permute-start(f32[32,2048]{1,0:T(8,128)S(1)} %apply_0.1.refs_0_.refs_3_), channel_id=1, source_target_pairs={{0,8},{8,0},{16,24},{24,16},{32,40},{40,32},{48,56},{56,48},{64,72... | collective-permute-start | bytes 786440 | tf_op jit(solution)/shard_map/ppermute | solution.py:372
  39.7 10.4 %collective-permute-start.5 = (f32[32,2048]{1,0:T(8,128)S(1)}, f32[32,2048]{1,0:T(8,128)S(1)}, u32[]{:S(2)}, u32[]{:S(2)}) collective-permute-start(f32[32,2048]{1,0:T(8,128)S(1)} %apply_1.1.refs_0_), channel_id=1, source_target_pairs={{0,504},{8,16},{16,8},{24,32},{32,24},{40,48},{48,40},{56,64},{64,... | collective-permute-start | bytes 786440 | tf_op jit(solution)/shard_map/ppermute | solution.py:373
  44.4 7.4 %collective-permute-start.4 = (f32[32,2048]{1,0:T(8,128)S(1)}, f32[32,2048]{1,0:T(8,128)S(1)}, u32[]{:S(2)}, u32[]{:S(2)}) collective-permute-start(f32[32,2048]{1,0:T(8,128)S(1)} %apply_1.1.refs_0_), channel_id=1, source_target_pairs={{0,8},{8,0},{16,24},{24,16},{32,40},{40,32},{48,56},{56,48},{64,72... | collective-permute-start | bytes 786440 | tf_op jit(solution)/shard_map/ppermute | solution.py:372

commit v6 on v5

--- a/solution.py
+++ b/solution.py
@@ -15,6 +15,7 @@
 NB = 64
 PACKED = 320
 BUILD_UNROLL = 8
+AHEAD = 8
 PAIR_UNROLL = 8
 PARAMS = pltpu.CompilerParams(vmem_limit_bytes=20 * 1024 * 1024)
 
@@ -199,28 +200,43 @@
         for v in some:
             vregs[v] = vregs[v] - sums[v]
 
+    early = []
     for v0 in range(n // 8):
         head = vregs[v0]
-        p = [lane_of(head, 8 * v0 + c) for c in range(8)]
+        p = early + [lane_of(head, 8 * v0 + c) for c in range(len(early), 8)]
+        more = AHEAD if v0 + 1 < n // 8 else 0
+        p += [lane_of(head, 8 * v0 + 8 + c) for c in range(more)]
         out = jnp.zeros((8, 128), F32)
         for k in range(0, 8, 2):
             a, b, d = row_of(p[k], k), row_of(p[k + 1], k), row_of(p[k + 1], k + 1)
             det = a * d - b * b
             inv = 1.0 / det
 
+            both = here[k] | here[k + 1]
+            m0 = jnp.where(both, jnp.where(here[k], -1.0, 0.0), p[k])
+            m1 = jnp.where(both, jnp.where(here[k + 1], -1.0, 0.0), p[k + 1])
+
             def eliminate(x):
                 s0, s1 = row_of(x, k), row_of(x, k + 1)
                 w0, w1 = d * s0 - b * s1, a * s1 - b * s0
-                y = x - (p[k] * w0 + p[k + 1] * w1) * inv
-                y = jnp.where(here[k], w0 * inv, y)
-                return jnp.where(here[k + 1], w1 * inv, y), s0, w1
-
-            for c in range(k + 2, 8):
+                y = jnp.where(both, 0.0, x) - (m0 * w0 + m1 * w1) * inv
+                return y, s0, w1
+
+            for c in range(k + 2, 8 + more):
                 p[c] = eliminate(p[c])[0]
             head, s0, w1 = eliminate(head)
             out = jnp.where(here[k], s0 * lax.rsqrt(a), out)
             out = jnp.where(here[k + 1], w1 * lax.rsqrt(a * det), out)
         done.append(out)
+        early = []
+        for c in range(more):
+            t = [
+                lane_of(vregs[v0 + 1], 8 * v0 + k) * row_of(p[8 + c], k)
+                for k in range(8)
+            ]
+            while len(t) > 1:
+                t = [t[i] + t[i + 1] for i in range(0, len(t), 2)]
+            early.append(lane_of(vregs[v0 + 1], 8 * v0 + 8 + c) - t[0])
         z = [row_of(head, k) for k in range(8)]
         for some in ([v0 + 1], list(range(v0 + 2, n // 8))):
             if some and some[0] < n // 8:
@@ -251,8 +267,11 @@
     return lax.dot_general(a, b, (((1,), (0,)), ((), ())), preferred_element_type=F32)
 
 
-def solve_kernel(g_ref, s_ref, basis_ref, factor_ref, a_ref):
+def solve_kernel(
+    g_ref, s_ref, basis_out, factor_out, a_ref, basis_ref, factor_ref, sems
+):
     k = factor_ref.shape[0]
+    copies = []
     row, col = square()
     mixed = g_ref[128:256]
     turned = mixed.T
@@ -277,14 +296,8 @@
     lane = lax.broadcasted_iota(jnp.int32, (NB, 128), 1)
     sub = lax.broadcasted_iota(jnp.int32, (NB, 128), 0)
     eye = jnp.where(lane == sub + NB, 1.0, 0.0)
-    for first in range(0, k, NB):
-        rows = slice(first, first + NB)
-        at = first // 128 * 128
-        tile = a_ref[rows, at : at + 128]
-        if first > at:
-            tile = pltpu.roll(tile, NB, 1)
-        u = factor_block(jnp.where(lane < NB, tile, eye))
-        twice = jnp.where(lane < NB, pltpu.roll(u, NB, 1), u)
+    def rest(first, twice):
+        rows, at, after = slice(first, first + NB), first // 128 * 128, first + NB
         x = dot_nn(six_lanes(twice), six_rows(a_ref[rows, at:]))
         col_id = at + lax.broadcasted_iota(jnp.int32, (NB, k - at), 1)
         row_id = first + lax.broadcasted_iota(jnp.int32, (NB, k - at), 0)
@@ -293,14 +306,51 @@
             upper = jnp.concatenate([jnp.zeros((NB, at), F32), upper], axis=1)
         factor_ref[rows, :] = upper
         basis_ref[rows, :] = x[:, k - at :]
-        after = first + NB
-        if after < k:
-            start = after // 128 * 128
-            turned = x[:, start - at : k - at]
-            turned = jnp.concatenate([turned, turned], axis=0).T[after - start :]
-            a_ref[after:, start:] -= dot_nn(
-                six_lanes(turned), six_rows(x[:, start - at :])
+        for i, (src, dst) in enumerate(
+            ((basis_ref, basis_out), (factor_ref, factor_out))
+        ):
+            copy = pltpu.make_async_copy(
+                src.at[rows, :], dst.at[rows, :], sems.at[i, first // NB]
             )
+            copy.start()
+            copies.append(copy)
+        if after == k:
+            return
+        start = after // 128 * 128
+        right = six_rows(x[:, start - at :])
+        turned = x[:, start - at : k - at]
+        turned = jnp.concatenate([turned, turned], axis=0).T[after - start :]
+        left = six_lanes(turned)
+        a_ref[after : after + NB, start + 128 :] -= dot_nn(left[:NB], right[:, 128:])
+        if after + NB < k:
+            a_ref[after + NB :, start:] -= dot_nn(left[NB:], right)
+
+    def ahead(first, twice):
+        rows, after = slice(first, first + NB), first + NB
+        start = after // 128 * 128
+        x = dot_nn(six_lanes(twice), six_rows(a_ref[rows, start : start + 128]))
+        turned = jnp.concatenate([x, x], axis=0).T
+        turned = turned[after - start : after - start + NB]
+        return a_ref[after : after + NB, start : start + 128] - dot_nn(
+            six_lanes(turned), six_rows(x)
+        )
+
+    for first in range(0, k, NB):
+        at = first // 128 * 128
+        if first == 0:
+            tile = a_ref[0:NB, 0:128]
+        elif first > at:
+            tile = pltpu.roll(tile, NB, 1)
+        u = factor_block(jnp.where(lane < NB, tile, eye))
+        twice = jnp.where(lane < NB, pltpu.roll(u, NB, 1), u)
+        if first + NB < k:
+            tile = ahead(first, twice)
+            rest(first, twice)
+            nxt = first + NB
+            a_ref[nxt : nxt + NB, nxt // 128 * 128 : nxt // 128 * 128 + 128] = tile
+    rest(k - NB, twice)
+    for copy in copies:
+        copy.wait()
 
 
 def orthonormalize(g, s):
@@ -313,8 +363,13 @@
             jax.ShapeDtypeStruct((k, k), F32),
         ),
         in_specs=[VMEM, VMEM],
-        out_specs=(VMEM, VMEM),
-        scratch_shapes=[pltpu.VMEM((k, k + n), F32)],
+        out_specs=(pl.BlockSpec(memory_space=pl.ANY),) * 2,
+        scratch_shapes=[
+            pltpu.VMEM((k, k + n), F32),
+            pltpu.VMEM((k, n), F32),
+            pltpu.VMEM((k, k), F32),
+            pltpu.SemaphoreType.DMA((2, k // NB)),
+        ],
         compiler_params=PARAMS,
         name="orthonormalize",
     )(near(g), near(s))

time: 117 us -> 116 us (level)
  Pallas kernels: 16.5 us -> 14.7 us
    pallas_call x1, Pallas kernels: 8.81 us -> 7.05 us  [orthonormalize(): pl.pallas_call(solve_kernel, out_shape=(jax.ShapeDtypeStruct((k, n), F32)...]
where the time goes in v6:
time: 116 us; the launch traced here: 115 us
  blocking collectives  53.5 us (46%)
  starting transfers between devices  28.5 us (25%)
  Pallas kernels  14.7 us (13%)
  waiting for transfers between devices  14.5 us (12%)
  local copies, waits for them, and re-layouts  2.21 us (2%)
    all_to_all x3, blocking collectives, exchange(): return lax.all_to_all(x, axes, 0, 0, axis_index_groups=groups, tiled=True)  38.8 us
    ppermute x3, starting transfers between devices, sides(): lax.ppermute(field, 'row', outside)  22.7 us
    all_to_all x1, blocking collectives, local(): lax.all_to_all(filtered.reshape(bundles, tiles // bundles, width, lanes),...  14.6 us
    ppermute x3, waiting for transfers between devices, sides(): lax.ppermute(field, 'row', outside)  9.74 us
    pallas_call x1, Pallas kernels, orthonormalize(): pl.pallas_call(solve_kernel, out_shape=(jax.ShapeDtypeStruct((k, n), F32)...  7.05 us
    pallas_call x3, Pallas kernels, apply_step(): pl.pallas_call(functools.partial(apply_kernel, stage), out_shape=pltpu.VM...  6.13 us
    ppermute x3, starting transfers between devices, sides(): lax.ppermute(field, 'row', inside)  5.76 us
    ppermute x3, waiting for transfers between devices, sides(): lax.ppermute(field, 'row', inside)  4.81 us
  transfers between devices with their start and end apart: 6, of which 6 were waited for; matrix products, arithmetic and copies ran while one was open for 1% of the time, Pallas kernels for 1%

profile of v6, /device:TPU:1, one launch (start us, length us, event | category | flops | bytes accessed | tf_op | source)
XLA Modules:
  0.0 115.2 jit_solution(7329935141774121790)
XLA Ops:
  0.6 14.4 %collective-permute-start.1 = (f32[32,2048]{1,0:T(8,128)}, f32[32,2048]{1,0:T(8,128)S(1)}, u32[]{:S(2)}, u32[]{:S(2)}) collective-permute-start(f32[32,2048]{1,0:T(8,128)} %refs_3_.1), channel_id=1, source_target_pairs={{0,504},{8,16},{16,8},{24,32},{32,24},{40,48},{48,40},{56,64},{64,... | collective-permute-start | bytes 786440 | tf_op jit(solution)/shard_map/ppermute | solution.py:428
  15.0 1.9 %collective-permute-start = (f32[32,2048]{1,0:T(8,128)}, f32[32,2048]{1,0:T(8,128)S(1)}, u32[]{:S(2)}, u32[]{:S(2)}) collective-permute-start(f32[32,2048]{1,0:T(8,128)} %refs_3_.1), channel_id=1, source_target_pairs={{0,8},{8,0},{16,24},{24,16},{32,40},{40,32},{48,56},{56,48},{64,72... | collective-permute-start | bytes 786440 | tf_op jit(solution)/shard_map/ppermute | solution.py:427
  17.0 0.8 fusion.5
  18.0 1.9 %copy-done = f32[32,64,384]{2,1,0:T(8,128)S(1)} copy-done((f32[32,64,384]{2,1,0:T(8,128)S(1)}, f32[32,64,384]{2,1,0:T(8,128)}, u32[]{:S(2)}) %copy-start) | copy-done | bytes 3145752
  19.8 1.1 split_blocks.1.refs_3_.refs_4_
  21.0 0.2 collective-permute-done.1.refs_2_
  21.2 2.8 %collective-permute-done.refs_1_ = f32[32,2048]{1,0:T(8,128)S(1)} collective-permute-done((f32[32,2048]{1,0:T(8,128)}, f32[32,2048]{1,0:T(8,128)S(1)}, u32[]{:S(2)}, u32[]{:S(2)}) %collective-permute-start) | collective-permute-done | bytes 262176 | tf_op jit(solution)/shard_map/ppermute | solution.py:427
  24.1 2.0 %apply_0.1.refs_0_.refs_3_ = f32[32,2048]{1,0:T(8,128)S(1)} custom-call(s32[192]{0:T(256)S(1)} %reshape.35.slot_ref, f32[2]{0:T(128)S(1)} %copy-done.2, f32[32,2048]{1,0:T(8,128)S(1)} %copy-done.1, f32[32,2048]{1,0:T(8,128)S(1)} %collective-permute-done.refs_1_, f32[32,2048]{1,0:T(8,128)S(1)} %collective-permute-done.1.refs_2_, ...), custom_call_target="tpu_custom_call" | custom-call | tf_op jit(solution)/shard_map/apply_0/pallas_call | solution.py:119
  26.1 3.6 %collective-permute-start.3 = (f32[32,2048]{1,0:T(8,128)S(1)}, f32[32,2048]{1,0:T(8,128)S(1)}, u32[]{:S(2)}, u32[]{:S(2)}) collective-permute-start(f32[32,2048]{1,0:T(8,128)S(1)} %apply_0.1.refs_0_.refs_3_), channel_id=1, source_target_pairs={{0,504},{8,16},{16,8},{24,32},{32,24},{40,48},{48,40},{56,64},{64,... | collective-permute-start | bytes 786440 | tf_op jit(solution)/shard_map/ppermute | solution.py:428
  29.7 1.9 %collective-permute-start.2 = (f32[32,2048]{1,0:T(8,128)S(1)}, f32[32,2048]{1,0:T(8,128)S(1)}, u32[]{:S(2)}, u32[]{:S(2)}) collective-permute-start(f32[32,2048]{1,0:T(8,128)S(1)} %apply_0.1.refs_0_.refs_3_), channel_id=1, source_target_pairs={{0,8},{8,0},{16,24},{24,16},{32,40},{40,32},{48,56},{56,48},{64,72... | collective-permute-start | bytes 786440 | tf_op jit(solution)/shard_map/ppermute | solution.py:427
  31.6 5.7 %collective-permute-done.3.refs_2_ = f32[32,2048]{1,0:T(8,128)S(1)} collective-permute-done((f32[32,2048]{1,0:T(8,128)S(1)}, f32[32,2048]{1,0:T(8,128)S(1)}, u32[]{:S(2)}, u32[]{:S(2)}) %collective-permute-start.3) | collective-permute-done | bytes 262176 | tf_op jit(solution)/shard_map/ppermute | solution.py:428
  37.4 0.3 collective-permute-done.2.refs_1_
  37.6 2.1 %apply_1.1.refs_0_ = f32[32,2048]{1,0:T(8,128)S(1)} custom-call(s32[192]{0:T(256)S(1)} %reshape.35.slot_ref, f32[2]{0:T(128)S(1)} %copy-done.2, f32[32,2048]{1,0:T(8,128)S(1)} %apply_0.1.refs_0_.refs_3_, f32[32,2048]{1,0:T(8,128)S(1)} %collective-permute-done.2.refs_1_, f32[32,2048]{1,0:T(8,128)S(1)} %collective-permute-done.3.refs_2_, ...), custom_call_target="tpu_custom_call" | custom-call | tf_op jit(solution)/shard_map/apply_1/pallas_call | solution.py:119
  39.7 4.7 %collective-permute-start.5 = (f32[32,2048]{1,0:T(8,128)S(1)}, f32[32,2048]{1,0:T(8,128)S(1)}, u32[]{:S(2)}, u32[]{:S(2)}) collective-permute-start(f32[32,2048]{1,0:T(8,128)S(1)} %apply_1.1.refs_0_), channel_id=1, source_target_pairs={{0,504},{8,16},{16,8},{24,32},{32,24},{40,48},{48,40},{56,64},{64,... | collective-permute-start | bytes 786440 | tf_op jit(solution)/shard_map/ppermute | solution.py:428
  44.4 1.9 %collective-permute-start.4 = (f32[32,2048]{1,0:T(8,128)S(1)}, f32[32,2048]{1,0:T(8,128)S(1)}, u32[]{:S(2)}, u32[]{:S(2)}) collective-permute-start(f32[32,2048]{1,0:T(8,128)S(1)} %apply_1.1.refs_0_), channel_id=1, source_target_pairs={{0,8},{8,0},{16,24},{24,16},{32,40},{40,32},{48,56},{56,48},{64,72... | collective-permute-start | bytes 786440 | tf_op jit(solution)/shard_map/ppermute | solution.py:427
  46.4 3.8 %collective-permute-done.5.refs_2_ = f32[32,2048]{1,0:T(8,128)S(1)} collective-permute-done((f32[32,2048]{1,0:T(8,128)S(1)}, f32[32,2048]{1,0:T(8,128)S(1)}, u32[]{:S(2)}, u32[]{:S(2)}) %collective-permute-start.5) | collective-permute-done | bytes 262176 | tf_op jit(solution)/shard_map/ppermute | solution.py:428
  50.1 1.7 %collective-permute-done.4.refs_1_ = f32[32,2048]{1,0:T(8,128)S(1)} collective-permute-done((f32[32,2048]{1,0:T(8,128)S(1)}, f32[32,2048]{1,0:T(8,128)S(1)}, u32[]{:S(2)}, u32[]{:S(2)}) %collective-permute-start.4) | collective-permute-done | bytes 262176 | tf_op jit(solution)/shard_map/ppermute | solution.py:427
  51.8 2.1 %apply_2.1 = f32[16,32,128]{2,1,0:T(8,128)S(1)} custom-call(s32[192]{0:T(256)S(1)} %reshape.35.slot_ref, f32[2]{0:T(128)S(1)} %copy-done.2, f32[32,2048]{1,0:T(8,128)S(1)} %apply_1.1.refs_0_, f32[32,2048]{1,0:T(8,128)S(1)} %collective-permute-done.4.refs_1_, f32[32,2048]{1,0:T(8,128)S(1)} %collective-permute-done.5.refs_2_, ...), custom_call_target="tpu_custom_call" | custom-call | tf_op jit(solution)/shard_map/apply_2/pallas_call | solution.py:119
  53.9 14.6 %all_to_all.20.s_ref = f32[8,2,32,128]{3,2,1,0:T(8,128)S(1)} all-to-all(f32[8,2,32,128]{3,2,1,0:T(8,128)S(1)} %bitcast.3), channel_id=1, replica_groups=mesh['row'=64,'bundle'=8] {'bundle'}, dimensions={0} | all-to-all | bytes 524288 | tf_op jit(solution)/shard_map/all_to_all | solution.py:445
  68.5 0.4 gram.1
  69.0 12.7 %all_to_all.21 = f32[32,1,1280]{2,1,0:T(1,128)S(1)} all-to-all(f32[32,1,1280]{2,1,0:T(1,128)S(1)} %bitcast.5), channel_id=1, replica_groups={{0,2,4,6,8,10,12,14,16,18,20,22,24,26,28,30,32,34,36,38,40,42,44,46,48,..., dimensions={0} | all-to-all | bytes 327680 | tf_op jit(solution)/shard_map/all_to_all | solution.py:400
  81.8 13.0 %all_to_all.22 = f32[16,1,1280]{2,1,0:T(1,128)S(1)} all-to-all(f32[16,1,1280]{2,1,0:T(1,128)S(1)} %broadcast_in_dim.4), channel_id=1, replica_groups={{0,1,64,65,128,129,192,193,256,257,320,321,384,385,448,449},{2,3,66,67,..., dimensions={0} | all-to-all | bytes 163840 | tf_op jit(solution)/shard_map/all_to_all | solution.py:400
  94.9 13.2 %all_to_all.23 = f32[32,1,1280]{2,1,0:T(1,128)S(1)} all-to-all(f32[32,1,1280]{2,1,0:T(1,128)S(1)} %broadcast_in_dim.5), channel_id=1, replica_groups={{0,2,4,6,8,10,12,14,16,18,20,22,24,26,28,30,32,34,36,38,40,42,44,46,48,..., dimensions={0} | all-to-all | bytes 327680 | tf_op jit(solution)/shard_map/all_to_all | solution.py:400
  108.1 7.1 %orthonormalize.1 = (f32[256,256]{1,0:T(8,128)}, f32[256,256]{1,0:T(8,128)}) custom-call(f32[320,128]{1,0:T(8,128)S(1)} %bitcast.4, f32[8,2,32,128]{3,2,1,0:T(8,128)S(1)} %all_to_all.20.s_ref), custom_call_target="tpu_custom_call" | custom-call | tf_op jit(solution)/shard_map/orthonormalize/pallas_call | solution.py:359
  (12 shorter events, 0.5 us)
Async XLA Ops:
  0.6 20.6 %collective-permute-start.1 = (f32[32,2048]{1,0:T(8,128)}, f32[32,2048]{1,0:T(8,128)S(1)}, u32[]{:S(2)}, u32[]{:S(2)}) collective-permute-start(f32[32,2048]{1,0:T(8,128)} %refs_3_.1), channel_id=1, source_target_pairs={{0,504},{8,16},{16,8},{24,32},{32,24},{40,48},{48,40},{56,64},{64,... | collective-permute-start | bytes 786440 | tf_op jit(solution)/shard_map/ppermute | solution.py:428
  15.0 9.0 %collective-permute-start = (f32[32,2048]{1,0:T(8,128)}, f32[32,2048]{1,0:T(8,128)S(1)}, u32[]{:S(2)}, u32[]{:S(2)}) collective-permute-start(f32[32,2048]{1,0:T(8,128)} %refs_3_.1), channel_id=1, source_target_pairs={{0,8},{8,0},{16,24},{24,16},{32,40},{40,32},{48,56},{56,48},{64,72... | collective-permute-start | bytes 786440 | tf_op jit(solution)/shard_map/ppermute | solution.py:427
  17.9 1.9 %copy-start = (f32[32,64,384]{2,1,0:T(8,128)S(1)}, f32[32,64,384]{2,1,0:T(8,128)}, u32[]{:S(2)}) copy-start(f32[32,64,384]{2,1,0:T(8,128)} %b_ref.1) | copy-start | bytes 9437188
  19.8 4.2 %copy-start.1 = (f32[32,2048]{1,0:T(8,128)S(1)}, f32[32,2048]{1,0:T(8,128)}, u32[]{:S(2)}) copy-start(f32[32,2048]{1,0:T(8,128)} %refs_3_.1) | copy-start | bytes 786436
  19.8 4.2 %copy-start.2 = (f32[2]{0:T(128)S(1)}, f32[2]{0:T(128)}, u32[]{:S(2)}) copy-start(f32[2]{0:T(128)} %bounds_ref.5) | copy-start | bytes 28
  26.1 11.3 %collective-permute-start.3 = (f32[32,2048]{1,0:T(8,128)S(1)}, f32[32,2048]{1,0:T(8,128)S(1)}, u32[]{:S(2)}, u32[]{:S(2)}) collective-permute-start(f32[32,2048]{1,0:T(8,128)S(1)} %apply_0.1.refs_0_.refs_3_), channel_id=1, source_target_pairs={{0,504},{8,16},{16,8},{24,32},{32,24},{40,48},{48,40},{56,64},{64,... | collective-permute-start | bytes 786440 | tf_op jit(solution)/shard_map/ppermute | solution.py:428
  29.7 7.9 %collective-permute-start.2 = (f32[32,2048]{1,0:T(8,128)S(1)}, f32[32,2048]{1,0:T(8,128)S(1)}, u32[]{:S(2)}, u32[]{:S(2)}) collective-permute-start(f32[32,2048]{1,0:T(8,128)S(1)} %apply_0.1.refs_0_.refs_3_), channel_id=1, source_target_pairs={{0,8},{8,0},{16,24},{24,16},{32,40},{40,32},{48,56},{56,48},{64,72... | collective-permute-start | bytes 786440 | tf_op jit(solution)/shard_map/ppermute | solution.py:427
  39.7 10.4 %collective-permute-start.5 = (f32[32,2048]{1,0:T(8,128)S(1)}, f32[32,2048]{1,0:T(8,128)S(1)}, u32[]{:S(2)}, u32[]{:S(2)}) collective-permute-start(f32[32,2048]{1,0:T(8,128)S(1)} %apply_1.1.refs_0_), channel_id=1, source_target_pairs={{0,504},{8,16},{16,8},{24,32},{32,24},{40,48},{48,40},{56,64},{64,... | collective-permute-start | bytes 786440 | tf_op jit(solution)/shard_map/ppermute | solution.py:428
  44.4 7.4 %collective-permute-start.4 = (f32[32,2048]{1,0:T(8,128)S(1)}, f32[32,2048]{1,0:T(8,128)S(1)}, u32[]{:S(2)}, u32[]{:S(2)}) collective-permute-start(f32[32,2048]{1,0:T(8,128)S(1)} %apply_1.1.refs_0_), channel_id=1, source_target_pairs={{0,8},{8,0},{16,24},{24,16},{32,40},{40,32},{48,56},{56,48},{64,72... | collective-permute-start | bytes 786440 | tf_op jit(solution)/shard_map/ppermute | solution.py:427

commit v7 on v6

--- a/solution.py
+++ b/solution.py
@@ -14,9 +14,7 @@
 SMEM = pl.BlockSpec(memory_space=pltpu.SMEM)
 NB = 64
 PACKED = 320
-BUILD_UNROLL = 8
 AHEAD = 8
-PAIR_UNROLL = 8
 PARAMS = pltpu.CompilerParams(vmem_limit_bytes=20 * 1024 * 1024)
 
 
@@ -66,17 +64,17 @@
     left = lax.broadcasted_iota(jnp.int32, (width, 128), 1) < 64
     left2 = lax.broadcasted_iota(jnp.int32, (2 * width, 128), 1) < 64
 
-    def build(t, carry):
+    def build(t):
         for part, ref in enumerate((inner_ref, f_ref, outer_ref)):
-            x = ref[:, pl.ds(pl.multiple_of(t * 128, 128), 128)]
+            x = ref[:, t * 128 : (t + 1) * 128]
             for v, y in enumerate((x, pltpu.roll(x, 64, 1))):
                 hi, lo = split(y)
                 at = (3 * v + part) * tiles + t
                 e_ref[at, 0:width] = hi
                 e_ref[at, width : 2 * width] = lo
-        return carry
-
-    lax.fori_loop(0, tiles, build, 0, unroll=BUILD_UNROLL)
+
+    for t in range(tiles):
+        build(t)
 
     center = (bounds_ref[0] + bounds_ref[1]) * 0.5
     half = (bounds_ref[1] - bounds_ref[0]) * 0.5
@@ -95,9 +93,9 @@
         acc = out[:width] + jnp.where(left, out[width:], 0.0)
         return acc + pltpu.roll(acc, 64, 1)
 
-    def pair(g, carry):
+    def pair(g):
         y = jnp.where(left, one(2 * g), one(2 * g + 1))
-        lanes = pl.ds(pl.multiple_of(g * 128, 128), 128)
+        lanes = slice(g * 128, (g + 1) * 128)
         f = f_ref[:, lanes]
         r = (y - center * f) / half
         if stage > 0:
@@ -106,9 +104,9 @@
             out_ref[:, lanes] = r
         else:
             out_ref[g] = r
-        return carry
-
-    lax.fori_loop(0, tiles, pair, 0, unroll=PAIR_UNROLL)
+
+    for g in range(tiles):
+        pair(g)
 
 
 def apply_step(stage, slot_table, bounds, f, inner, outer, prev, w):

time: 116 us -> 115 us (level)
  no operation moved by 1% of the time
where the time goes in v7:
time: 115 us; the launch traced here: 114 us
  blocking collectives  53.5 us (47%)
  starting transfers between devices  28.5 us (25%)
  waiting for transfers between devices  14.6 us (13%)
  Pallas kernels  13.8 us (12%)
  local copies, waits for them, and re-layouts  2.21 us (2%)
    all_to_all x3, blocking collectives, exchange(): return lax.all_to_all(x, axes, 0, 0, axis_index_groups=groups, tiled=True)  38.8 us
    ppermute x3, starting transfers between devices, sides(): lax.ppermute(field, 'row', outside)  22.7 us
    all_to_all x1, blocking collectives, local(): lax.all_to_all(filtered.reshape(bundles, tiles // bundles, width, lanes),...  14.7 us
    ppermute x3, waiting for transfers between devices, sides(): lax.ppermute(field, 'row', outside)  9.75 us
    pallas_call x1, Pallas kernels, orthonormalize(): pl.pallas_call(solve_kernel, out_shape=(jax.ShapeDtypeStruct((k, n), F32)...  7.05 us
    ppermute x3, starting transfers between devices, sides(): lax.ppermute(field, 'row', inside)  5.76 us
    pallas_call x3, Pallas kernels, apply_step(): pl.pallas_call(functools.partial(apply_kernel, stage), out_shape=pltpu.VM...  5.14 us
    ppermute x3, waiting for transfers between devices, sides(): lax.ppermute(field, 'row', inside)  4.8 us
  transfers between devices with their start and end apart: 6, of which 6 were waited for; matrix products, arithmetic and copies ran while one was open for 1% of the time, Pallas kernels for 1%

profile of v7, /device:TPU:1, one launch (start us, length us, event | category | flops | bytes accessed | tf_op | source)
XLA Modules:
  0.0 114.2 jit_solution(15692377109573130735)
XLA Ops:
  0.6 14.4 %collective-permute-start.1 = (f32[32,2048]{1,0:T(8,128)}, f32[32,2048]{1,0:T(8,128)S(1)}, u32[]{:S(2)}, u32[]{:S(2)}) collective-permute-start(f32[32,2048]{1,0:T(8,128)} %refs_3_.1), channel_id=1, source_target_pairs={{0,504},{8,16},{16,8},{24,32},{32,24},{40,48},{48,40},{56,64},{64,... | collective-permute-start | bytes 786440 | tf_op jit(solution)/shard_map/ppermute | solution.py:426
  15.0 1.9 %collective-permute-start = (f32[32,2048]{1,0:T(8,128)}, f32[32,2048]{1,0:T(8,128)S(1)}, u32[]{:S(2)}, u32[]{:S(2)}) collective-permute-start(f32[32,2048]{1,0:T(8,128)} %refs_3_.1), channel_id=1, source_target_pairs={{0,8},{8,0},{16,24},{24,16},{32,40},{40,32},{48,56},{56,48},{64,72... | collective-permute-start | bytes 786440 | tf_op jit(solution)/shard_map/ppermute | solution.py:425
  17.0 0.8 fusion.5
  18.0 1.9 %copy-done = f32[32,64,384]{2,1,0:T(8,128)S(1)} copy-done((f32[32,64,384]{2,1,0:T(8,128)S(1)}, f32[32,64,384]{2,1,0:T(8,128)}, u32[]{:S(2)}) %copy-start) | copy-done | bytes 3145752
  19.8 1.1 split_blocks.1.refs_3_.refs_4_
  21.0 0.2 collective-permute-done.1.refs_2_
  21.2 2.8 %collective-permute-done.refs_1_ = f32[32,2048]{1,0:T(8,128)S(1)} collective-permute-done((f32[32,2048]{1,0:T(8,128)}, f32[32,2048]{1,0:T(8,128)S(1)}, u32[]{:S(2)}, u32[]{:S(2)}) %collective-permute-start) | collective-permute-done | bytes 262176 | tf_op jit(solution)/shard_map/ppermute | solution.py:425
  24.1 1.7 %apply_0.1.refs_0_.refs_3_ = f32[32,2048]{1,0:T(8,128)S(1)} custom-call(s32[192]{0:T(256)S(1)} %reshape.35.slot_ref, f32[2]{0:T(128)S(1)} %copy-done.2, f32[32,2048]{1,0:T(8,128)S(1)} %copy-done.1, f32[32,2048]{1,0:T(8,128)S(1)} %collective-permute-done.refs_1_, f32[32,2048]{1,0:T(8,128)S(1)} %collective-permute-done.1.refs_2_, ...), custom_call_target="tpu_custom_call" | custom-call | tf_op jit(solution)/shard_map/apply_0/pallas_call | solution.py:117
  25.8 3.6 %collective-permute-start.3 = (f32[32,2048]{1,0:T(8,128)S(1)}, f32[32,2048]{1,0:T(8,128)S(1)}, u32[]{:S(2)}, u32[]{:S(2)}) collective-permute-start(f32[32,2048]{1,0:T(8,128)S(1)} %apply_0.1.refs_0_.refs_3_), channel_id=1, source_target_pairs={{0,504},{8,16},{16,8},{24,32},{32,24},{40,48},{48,40},{56,64},{64,... | collective-permute-start | bytes 786440 | tf_op jit(solution)/shard_map/ppermute | solution.py:426
  29.4 1.9 %collective-permute-start.2 = (f32[32,2048]{1,0:T(8,128)S(1)}, f32[32,2048]{1,0:T(8,128)S(1)}, u32[]{:S(2)}, u32[]{:S(2)}) collective-permute-start(f32[32,2048]{1,0:T(8,128)S(1)} %apply_0.1.refs_0_.refs_3_), channel_id=1, source_target_pairs={{0,8},{8,0},{16,24},{24,16},{32,40},{40,32},{48,56},{56,48},{64,72... | collective-permute-start | bytes 786440 | tf_op jit(solution)/shard_map/ppermute | solution.py:425
  31.3 5.7 %collective-permute-done.3.refs_2_ = f32[32,2048]{1,0:T(8,128)S(1)} collective-permute-done((f32[32,2048]{1,0:T(8,128)S(1)}, f32[32,2048]{1,0:T(8,128)S(1)}, u32[]{:S(2)}, u32[]{:S(2)}) %collective-permute-start.3) | collective-permute-done | bytes 262176 | tf_op jit(solution)/shard_map/ppermute | solution.py:426
  37.0 0.3 collective-permute-done.2.refs_1_
  37.3 1.7 %apply_1.1.refs_0_ = f32[32,2048]{1,0:T(8,128)S(1)} custom-call(s32[192]{0:T(256)S(1)} %reshape.35.slot_ref, f32[2]{0:T(128)S(1)} %copy-done.2, f32[32,2048]{1,0:T(8,128)S(1)} %apply_0.1.refs_0_.refs_3_, f32[32,2048]{1,0:T(8,128)S(1)} %collective-permute-done.2.refs_1_, f32[32,2048]{1,0:T(8,128)S(1)} %collective-permute-done.3.refs_2_, ...), custom_call_target="tpu_custom_call" | custom-call | tf_op jit(solution)/shard_map/apply_1/pallas_call | solution.py:117
  39.0 4.7 %collective-permute-start.5 = (f32[32,2048]{1,0:T(8,128)S(1)}, f32[32,2048]{1,0:T(8,128)S(1)}, u32[]{:S(2)}, u32[]{:S(2)}) collective-permute-start(f32[32,2048]{1,0:T(8,128)S(1)} %apply_1.1.refs_0_), channel_id=1, source_target_pairs={{0,504},{8,16},{16,8},{24,32},{32,24},{40,48},{48,40},{56,64},{64,... | collective-permute-start | bytes 786440 | tf_op jit(solution)/shard_map/ppermute | solution.py:426
  43.8 1.9 %collective-permute-start.4 = (f32[32,2048]{1,0:T(8,128)S(1)}, f32[32,2048]{1,0:T(8,128)S(1)}, u32[]{:S(2)}, u32[]{:S(2)}) collective-permute-start(f32[32,2048]{1,0:T(8,128)S(1)} %apply_1.1.refs_0_), channel_id=1, source_target_pairs={{0,8},{8,0},{16,24},{24,16},{32,40},{40,32},{48,56},{56,48},{64,72... | collective-permute-start | bytes 786440 | tf_op jit(solution)/shard_map/ppermute | solution.py:425
  45.7 3.8 %collective-permute-done.5.refs_2_ = f32[32,2048]{1,0:T(8,128)S(1)} collective-permute-done((f32[32,2048]{1,0:T(8,128)S(1)}, f32[32,2048]{1,0:T(8,128)S(1)}, u32[]{:S(2)}, u32[]{:S(2)}) %collective-permute-start.5) | collective-permute-done | bytes 262176 | tf_op jit(solution)/shard_map/ppermute | solution.py:426
  49.5 1.7 %collective-permute-done.4.refs_1_ = f32[32,2048]{1,0:T(8,128)S(1)} collective-permute-done((f32[32,2048]{1,0:T(8,128)S(1)}, f32[32,2048]{1,0:T(8,128)S(1)}, u32[]{:S(2)}, u32[]{:S(2)}) %collective-permute-start.4) | collective-permute-done | bytes 262176 | tf_op jit(solution)/shard_map/ppermute | solution.py:425
  51.2 1.7 %apply_2.1 = f32[16,32,128]{2,1,0:T(8,128)S(1)} custom-call(s32[192]{0:T(256)S(1)} %reshape.35.slot_ref, f32[2]{0:T(128)S(1)} %copy-done.2, f32[32,2048]{1,0:T(8,128)S(1)} %apply_1.1.refs_0_, f32[32,2048]{1,0:T(8,128)S(1)} %collective-permute-done.4.refs_1_, f32[32,2048]{1,0:T(8,128)S(1)} %collective-permute-done.5.refs_2_, ...), custom_call_target="tpu_custom_call" | custom-call | tf_op jit(solution)/shard_map/apply_2/pallas_call | solution.py:117
  52.9 14.7 %all_to_all.20.s_ref = f32[8,2,32,128]{3,2,1,0:T(8,128)S(1)} all-to-all(f32[8,2,32,128]{3,2,1,0:T(8,128)S(1)} %bitcast.3), channel_id=1, replica_groups=mesh['row'=64,'bundle'=8] {'bundle'}, dimensions={0} | all-to-all | bytes 524288 | tf_op jit(solution)/shard_map/all_to_all | solution.py:443
  67.6 0.4 gram.1
  68.0 12.7 %all_to_all.21 = f32[32,1,1280]{2,1,0:T(1,128)S(1)} all-to-all(f32[32,1,1280]{2,1,0:T(1,128)S(1)} %bitcast.5), channel_id=1, replica_groups={{0,2,4,6,8,10,12,14,16,18,20,22,24,26,28,30,32,34,36,38,40,42,44,46,48,..., dimensions={0} | all-to-all | bytes 327680 | tf_op jit(solution)/shard_map/all_to_all | solution.py:398
  80.8 13.0 %all_to_all.22 = f32[16,1,1280]{2,1,0:T(1,128)S(1)} all-to-all(f32[16,1,1280]{2,1,0:T(1,128)S(1)} %broadcast_in_dim.4), channel_id=1, replica_groups={{0,1,64,65,128,129,192,193,256,257,320,321,384,385,448,449},{2,3,66,67,..., dimensions={0} | all-to-all | bytes 163840 | tf_op jit(solution)/shard_map/all_to_all | solution.py:398
  93.9 13.2 %all_to_all.23 = f32[32,1,1280]{2,1,0:T(1,128)S(1)} all-to-all(f32[32,1,1280]{2,1,0:T(1,128)S(1)} %broadcast_in_dim.5), channel_id=1, replica_groups={{0,2,4,6,8,10,12,14,16,18,20,22,24,26,28,30,32,34,36,38,40,42,44,46,48,..., dimensions={0} | all-to-all | bytes 327680 | tf_op jit(solution)/shard_map/all_to_all | solution.py:398
  107.1 7.1 %orthonormalize.1 = (f32[256,256]{1,0:T(8,128)}, f32[256,256]{1,0:T(8,128)}) custom-call(f32[320,128]{1,0:T(8,128)S(1)} %bitcast.4, f32[8,2,32,128]{3,2,1,0:T(8,128)S(1)} %all_to_all.20.s_ref), custom_call_target="tpu_custom_call" | custom-call | tf_op jit(solution)/shard_map/orthonormalize/pallas_call | solution.py:357
  (12 shorter events, 0.5 us)
Async XLA Ops:
  0.6 20.6 %collective-permute-start.1 = (f32[32,2048]{1,0:T(8,128)}, f32[32,2048]{1,0:T(8,128)S(1)}, u32[]{:S(2)}, u32[]{:S(2)}) collective-permute-start(f32[32,2048]{1,0:T(8,128)} %refs_3_.1), channel_id=1, source_target_pairs={{0,504},{8,16},{16,8},{24,32},{32,24},{40,48},{48,40},{56,64},{64,... | collective-permute-start | bytes 786440 | tf_op jit(solution)/shard_map/ppermute | solution.py:426
  15.0 9.0 %collective-permute-start = (f32[32,2048]{1,0:T(8,128)}, f32[32,2048]{1,0:T(8,128)S(1)}, u32[]{:S(2)}, u32[]{:S(2)}) collective-permute-start(f32[32,2048]{1,0:T(8,128)} %refs_3_.1), channel_id=1, source_target_pairs={{0,8},{8,0},{16,24},{24,16},{32,40},{40,32},{48,56},{56,48},{64,72... | collective-permute-start | bytes 786440 | tf_op jit(solution)/shard_map/ppermute | solution.py:425
  17.9 1.9 %copy-start = (f32[32,64,384]{2,1,0:T(8,128)S(1)}, f32[32,64,384]{2,1,0:T(8,128)}, u32[]{:S(2)}) copy-start(f32[32,64,384]{2,1,0:T(8,128)} %b_ref.1) | copy-start | bytes 9437188
  19.8 4.2 %copy-start.1 = (f32[32,2048]{1,0:T(8,128)S(1)}, f32[32,2048]{1,0:T(8,128)}, u32[]{:S(2)}) copy-start(f32[32,2048]{1,0:T(8,128)} %refs_3_.1) | copy-start | bytes 786436
  19.8 4.2 %copy-start.2 = (f32[2]{0:T(128)S(1)}, f32[2]{0:T(128)}, u32[]{:S(2)}) copy-start(f32[2]{0:T(128)} %bounds_ref.5) | copy-start | bytes 28
  25.8 11.3 %collective-permute-start.3 = (f32[32,2048]{1,0:T(8,128)S(1)}, f32[32,2048]{1,0:T(8,128)S(1)}, u32[]{:S(2)}, u32[]{:S(2)}) collective-permute-start(f32[32,2048]{1,0:T(8,128)S(1)} %apply_0.1.refs_0_.refs_3_), channel_id=1, source_target_pairs={{0,504},{8,16},{16,8},{24,32},{32,24},{40,48},{48,40},{56,64},{64,... | collective-permute-start | bytes 786440 | tf_op jit(solution)/shard_map/ppermute | solution.py:426
  29.4 7.9 %collective-permute-start.2 = (f32[32,2048]{1,0:T(8,128)S(1)}, f32[32,2048]{1,0:T(8,128)S(1)}, u32[]{:S(2)}, u32[]{:S(2)}) collective-permute-start(f32[32,2048]{1,0:T(8,128)S(1)} %apply_0.1.refs_0_.refs_3_), channel_id=1, source_target_pairs={{0,8},{8,0},{16,24},{24,16},{32,40},{40,32},{48,56},{56,48},{64,72... | collective-permute-start | bytes 786440 | tf_op jit(solution)/shard_map/ppermute | solution.py:425
  39.0 10.4 %collective-permute-start.5 = (f32[32,2048]{1,0:T(8,128)S(1)}, f32[32,2048]{1,0:T(8,128)S(1)}, u32[]{:S(2)}, u32[]{:S(2)}) collective-permute-start(f32[32,2048]{1,0:T(8,128)S(1)} %apply_1.1.refs_0_), channel_id=1, source_target_pairs={{0,504},{8,16},{16,8},{24,32},{32,24},{40,48},{48,40},{56,64},{64,... | collective-permute-start | bytes 786440 | tf_op jit(solution)/shard_map/ppermute | solution.py:426
  43.8 7.4 %collective-permute-start.4 = (f32[32,2048]{1,0:T(8,128)S(1)}, f32[32,2048]{1,0:T(8,128)S(1)}, u32[]{:S(2)}, u32[]{:S(2)}) collective-permute-start(f32[32,2048]{1,0:T(8,128)S(1)} %apply_1.1.refs_0_), channel_id=1, source_target_pairs={{0,8},{8,0},{16,24},{24,16},{32,40},{40,32},{48,56},{56,48},{64,72... | collective-permute-start | bytes 786440 | tf_op jit(solution)/shard_map/ppermute | solution.py:425

commit v8 on v7

--- a/solution.py
+++ b/solution.py
@@ -182,7 +182,8 @@
     return jnp.broadcast_to(x[:, c : c + 1], (8, 128))
 
 
-def factor_block(m):
+def factor_block(m, aside=()):
+    aside = list(aside)
     n = m.shape[0]
     sub = lax.broadcasted_iota(jnp.int32, (8, 128), 0)
     here = [sub == k for k in range(8)]
@@ -214,18 +215,22 @@
             m0 = jnp.where(both, jnp.where(here[k], -1.0, 0.0), p[k])
             m1 = jnp.where(both, jnp.where(here[k + 1], -1.0, 0.0), p[k + 1])
 
+            n0, n1 = m0 * d - m1 * b, m1 * a - m0 * b
+
             def eliminate(x):
                 s0, s1 = row_of(x, k), row_of(x, k + 1)
-                w0, w1 = d * s0 - b * s1, a * s1 - b * s0
-                y = jnp.where(both, 0.0, x) - (m0 * w0 + m1 * w1) * inv
-                return y, s0, w1
+                return jnp.where(both, 0.0, x) - (s0 * n0 + s1 * n1) * inv
 
             for c in range(k + 2, 8 + more):
-                p[c] = eliminate(p[c])[0]
-            head, s0, w1 = eliminate(head)
+                p[c] = eliminate(p[c])
+            s0 = row_of(head, k)
+            w1 = a * row_of(head, k + 1) - b * s0
+            head = eliminate(head)
             out = jnp.where(here[k], s0 * lax.rsqrt(a), out)
             out = jnp.where(here[k + 1], w1 * lax.rsqrt(a * det), out)
         done.append(out)
+        for _ in range(-(-len(aside) // max(1, n // 8 - 1 - v0))):
+            aside.pop(0)()
         early = []
         for c in range(more):
             t = [
@@ -294,34 +299,61 @@
     lane = lax.broadcasted_iota(jnp.int32, (NB, 128), 1)
     sub = lax.broadcasted_iota(jnp.int32, (NB, 128), 0)
     eye = jnp.where(lane == sub + NB, 1.0, 0.0)
+    def send(i, src, dst, rows, first):
+        copy = pltpu.make_async_copy(
+            src.at[rows, :], dst.at[rows, :], sems.at[i, first // NB]
+        )
+        copy.start()
+        copies.append(copy)
+
     def rest(first, twice):
         rows, at, after = slice(first, first + NB), first // 128 * 128, first + NB
-        x = dot_nn(six_lanes(twice), six_rows(a_ref[rows, at:]))
-        col_id = at + lax.broadcasted_iota(jnp.int32, (NB, k - at), 1)
-        row_id = first + lax.broadcasted_iota(jnp.int32, (NB, k - at), 0)
-        upper = jnp.where(col_id >= row_id, x[:, : k - at] * size[:, at:], 0.0)
-        if at > 0:
-            upper = jnp.concatenate([jnp.zeros((NB, at), F32), upper], axis=1)
-        factor_ref[rows, :] = upper
-        basis_ref[rows, :] = x[:, k - at :]
-        for i, (src, dst) in enumerate(
-            ((basis_ref, basis_out), (factor_ref, factor_out))
-        ):
-            copy = pltpu.make_async_copy(
-                src.at[rows, :], dst.at[rows, :], sems.at[i, first // NB]
+        start = after // 128 * 128
+        held = {}
+
+        def begin():
+            held["left"] = six_lanes(twice)
+
+        def solve(c):
+            x = dot_nn(held["left"], six_rows(a_ref[rows, c : c + 128]))
+            held[c] = x
+            if c >= k:
+                basis_ref[rows, c - k : c - k + 128] = x
+            else:
+                col_id = c + lax.broadcasted_iota(jnp.int32, (NB, 128), 1)
+                row_id = first + lax.broadcasted_iota(jnp.int32, (NB, 128), 0)
+                factor_ref[rows, c : c + 128] = jnp.where(
+                    col_id >= row_id, x * size[:, c : c + 128], 0.0
+                )
+
+        def leave():
+            if at > 0:
+                factor_ref[rows, :at] = jnp.zeros((NB, at), F32)
+            send(0, basis_ref, basis_out, rows, first)
+            send(1, factor_ref, factor_out, rows, first)
+
+        def turn(c):
+            x = jnp.concatenate([held[c], held[c]], axis=0).T
+            held["turned", c] = six_lanes(x[max(after - c, 0) :])
+
+        def update(c):
+            left = jnp.concatenate(
+                [held["turned", t] for t in range(start, k, 128)], axis=0
             )
-            copy.start()
-            copies.append(copy)
-        if after == k:
-            return
-        start = after // 128 * 128
-        right = six_rows(x[:, start - at :])
-        turned = x[:, start - at : k - at]
-        turned = jnp.concatenate([turned, turned], axis=0).T[after - start :]
-        left = six_lanes(turned)
-        a_ref[after : after + NB, start + 128 :] -= dot_nn(left[:NB], right[:, 128:])
-        if after + NB < k:
-            a_ref[after + NB :, start:] -= dot_nn(left[NB:], right)
+            low = after + NB if c == start else after
+            if low < k:
+                a_ref[low:, c : c + 128] -= dot_nn(
+                    left[low - after :], six_rows(held[c])
+                )
+
+        total = a_ref.shape[1]
+        pieces = [begin]
+        pieces += [functools.partial(solve, c) for c in range(at, total, 128)]
+        pieces.append(leave)
+        if after < k:
+            pieces += [functools.partial(turn, c) for c in range(start, k, 128)]
+            pieces += [functools.partial(update, c) for c in range(start, total, 128)]
+        return pieces
 
     def ahead(first, twice):
         rows, after = slice(first, first + NB), first + NB
@@ -333,20 +365,26 @@
             six_lanes(turned), six_rows(x)
         )
 
+    def keep(nxt, tile):
+        at = nxt // 128 * 128
+        a_ref[nxt : nxt + NB, at : at + 128] = tile
+
+    aside = []
     for first in range(0, k, NB):
         at = first // 128 * 128
         if first == 0:
             tile = a_ref[0:NB, 0:128]
         elif first > at:
             tile = pltpu.roll(tile, NB, 1)
-        u = factor_block(jnp.where(lane < NB, tile, eye))
+        u = factor_block(jnp.where(lane < NB, tile, eye), aside)
         twice = jnp.where(lane < NB, pltpu.roll(u, NB, 1), u)
         if first + NB < k:
             tile = ahead(first, twice)
-            rest(first, twice)
             nxt = first + NB
-            a_ref[nxt : nxt + NB, nxt // 128 * 128 : nxt // 128 * 128 + 128] = tile
-    rest(k - NB, twice)
+            aside = rest(first, twice)
+            aside.append(functools.partial(keep, nxt, tile))
+    for piece in rest(k - NB, twice):
+        piece()
     for copy in copies:
         copy.wait()
 

time: 115 us -> 114 us (level)
  no operation moved by 1% of the time
where the time goes in v8:
time: 114 us; the launch traced here: 113 us
  blocking collectives  53.5 us (47%)
  starting transfers between devices  28.5 us (25%)
  waiting for transfers between devices  14.6 us (13%)
  Pallas kernels  12.9 us (11%)
  local copies, waits for them, and re-layouts  2.21 us (2%)
    all_to_all x3, blocking collectives, exchange(): return lax.all_to_all(x, axes, 0, 0, axis_index_groups=groups, tiled=True)  38.8 us
    ppermute x3, starting transfers between devices, sides(): lax.ppermute(field, 'row', outside)  22.7 us
    all_to_all x1, blocking collectives, local(): lax.all_to_all(filtered.reshape(bundles, tiles // bundles, width, lanes),...  14.7 us
    ppermute x3, waiting for transfers between devices, sides(): lax.ppermute(field, 'row', outside)  9.75 us
    pallas_call x1, Pallas kernels, orthonormalize(): pl.pallas_call(solve_kernel, out_shape=(jax.ShapeDtypeStruct((k, n), F32)...  6.17 us
    ppermute x3, starting transfers between devices, sides(): lax.ppermute(field, 'row', inside)  5.76 us
    pallas_call x3, Pallas kernels, apply_step(): pl.pallas_call(functools.partial(apply_kernel, stage), out_shape=pltpu.VM...  5.14 us
    ppermute x3, waiting for transfers between devices, sides(): lax.ppermute(field, 'row', inside)  4.8 us
  transfers between devices with their start and end apart: 6, of which 6 were waited for; matrix products, arithmetic and copies ran while one was open for 1% of the time, Pallas kernels for 1%

profile of v8, /device:TPU:1, one launch (start us, length us, event | category | flops | bytes accessed | tf_op | source)
XLA Modules:
  0.0 113.3 jit_solution(17263705991609999093)
XLA Ops:
  0.6 14.4 %collective-permute-start.1 = (f32[32,2048]{1,0:T(8,128)}, f32[32,2048]{1,0:T(8,128)S(1)}, u32[]{:S(2)}, u32[]{:S(2)}) collective-permute-start(f32[32,2048]{1,0:T(8,128)} %refs_3_.1), channel_id=1, source_target_pairs={{0,504},{8,16},{16,8},{24,32},{32,24},{40,48},{48,40},{56,64},{64,... | collective-permute-start | bytes 786440 | tf_op jit(solution)/shard_map/ppermute | solution.py:464
  15.0 1.9 %collective-permute-start = (f32[32,2048]{1,0:T(8,128)}, f32[32,2048]{1,0:T(8,128)S(1)}, u32[]{:S(2)}, u32[]{:S(2)}) collective-permute-start(f32[32,2048]{1,0:T(8,128)} %refs_3_.1), channel_id=1, source_target_pairs={{0,8},{8,0},{16,24},{24,16},{32,40},{40,32},{48,56},{56,48},{64,72... | collective-permute-start | bytes 786440 | tf_op jit(solution)/shard_map/ppermute | solution.py:463
  17.0 0.8 fusion.5
  18.0 1.9 %copy-done = f32[32,64,384]{2,1,0:T(8,128)S(1)} copy-done((f32[32,64,384]{2,1,0:T(8,128)S(1)}, f32[32,64,384]{2,1,0:T(8,128)}, u32[]{:S(2)}) %copy-start) | copy-done | bytes 3145752
  19.8 1.1 %split_blocks.1.refs_3_.refs_4_ = bf16[32,384,128]{2,1,0:T(8,128)(2,1)S(1)} custom-call(f32[32,64,384]{2,1,0:T(8,128)S(1)} %copy-done), custom_call_target="tpu_custom_call" | custom-call | tf_op jit(solution)/shard_map/split_blocks/pallas_call | solution.py:45
  21.0 0.2 collective-permute-done.1.refs_2_
  21.2 2.8 %collective-permute-done.refs_1_ = f32[32,2048]{1,0:T(8,128)S(1)} collective-permute-done((f32[32,2048]{1,0:T(8,128)}, f32[32,2048]{1,0:T(8,128)S(1)}, u32[]{:S(2)}, u32[]{:S(2)}) %collective-permute-start) | collective-permute-done | bytes 262176 | tf_op jit(solution)/shard_map/ppermute | solution.py:463
  24.1 1.7 %apply_0.1.refs_0_.refs_3_ = f32[32,2048]{1,0:T(8,128)S(1)} custom-call(s32[192]{0:T(256)S(1)} %reshape.35.slot_ref, f32[2]{0:T(128)S(1)} %copy-done.2, f32[32,2048]{1,0:T(8,128)S(1)} %copy-done.1, f32[32,2048]{1,0:T(8,128)S(1)} %collective-permute-done.refs_1_, f32[32,2048]{1,0:T(8,128)S(1)} %collective-permute-done.1.refs_2_, ...), custom_call_target="tpu_custom_call" | custom-call | tf_op jit(solution)/shard_map/apply_0/pallas_call | solution.py:117
  25.8 3.6 %collective-permute-start.3 = (f32[32,2048]{1,0:T(8,128)S(1)}, f32[32,2048]{1,0:T(8,128)S(1)}, u32[]{:S(2)}, u32[]{:S(2)}) collective-permute-start(f32[32,2048]{1,0:T(8,128)S(1)} %apply_0.1.refs_0_.refs_3_), channel_id=1, source_target_pairs={{0,504},{8,16},{16,8},{24,32},{32,24},{40,48},{48,40},{56,64},{64,... | collective-permute-start | bytes 786440 | tf_op jit(solution)/shard_map/ppermute | solution.py:464
  29.4 1.9 %collective-permute-start.2 = (f32[32,2048]{1,0:T(8,128)S(1)}, f32[32,2048]{1,0:T(8,128)S(1)}, u32[]{:S(2)}, u32[]{:S(2)}) collective-permute-start(f32[32,2048]{1,0:T(8,128)S(1)} %apply_0.1.refs_0_.refs_3_), channel_id=1, source_target_pairs={{0,8},{8,0},{16,24},{24,16},{32,40},{40,32},{48,56},{56,48},{64,72... | collective-permute-start | bytes 786440 | tf_op jit(solution)/shard_map/ppermute | solution.py:463
  31.3 5.7 %collective-permute-done.3.refs_2_ = f32[32,2048]{1,0:T(8,128)S(1)} collective-permute-done((f32[32,2048]{1,0:T(8,128)S(1)}, f32[32,2048]{1,0:T(8,128)S(1)}, u32[]{:S(2)}, u32[]{:S(2)}) %collective-permute-start.3) | collective-permute-done | bytes 262176 | tf_op jit(solution)/shard_map/ppermute | solution.py:464
  37.0 0.3 collective-permute-done.2.refs_1_
  37.3 1.7 %apply_1.1.refs_0_ = f32[32,2048]{1,0:T(8,128)S(1)} custom-call(s32[192]{0:T(256)S(1)} %reshape.35.slot_ref, f32[2]{0:T(128)S(1)} %copy-done.2, f32[32,2048]{1,0:T(8,128)S(1)} %apply_0.1.refs_0_.refs_3_, f32[32,2048]{1,0:T(8,128)S(1)} %collective-permute-done.2.refs_1_, f32[32,2048]{1,0:T(8,128)S(1)} %collective-permute-done.3.refs_2_, ...), custom_call_target="tpu_custom_call" | custom-call | tf_op jit(solution)/shard_map/apply_1/pallas_call | solution.py:117
  39.0 4.7 %collective-permute-start.5 = (f32[32,2048]{1,0:T(8,128)S(1)}, f32[32,2048]{1,0:T(8,128)S(1)}, u32[]{:S(2)}, u32[]{:S(2)}) collective-permute-start(f32[32,2048]{1,0:T(8,128)S(1)} %apply_1.1.refs_0_), channel_id=1, source_target_pairs={{0,504},{8,16},{16,8},{24,32},{32,24},{40,48},{48,40},{56,64},{64,... | collective-permute-start | bytes 786440 | tf_op jit(solution)/shard_map/ppermute | solution.py:464
  43.8 1.9 %collective-permute-start.4 = (f32[32,2048]{1,0:T(8,128)S(1)}, f32[32,2048]{1,0:T(8,128)S(1)}, u32[]{:S(2)}, u32[]{:S(2)}) collective-permute-start(f32[32,2048]{1,0:T(8,128)S(1)} %apply_1.1.refs_0_), channel_id=1, source_target_pairs={{0,8},{8,0},{16,24},{24,16},{32,40},{40,32},{48,56},{56,48},{64,72... | collective-permute-start | bytes 786440 | tf_op jit(solution)/shard_map/ppermute | solution.py:463
  45.7 3.8 %collective-permute-done.5.refs_2_ = f32[32,2048]{1,0:T(8,128)S(1)} collective-permute-done((f32[32,2048]{1,0:T(8,128)S(1)}, f32[32,2048]{1,0:T(8,128)S(1)}, u32[]{:S(2)}, u32[]{:S(2)}) %collective-permute-start.5) | collective-permute-done | bytes 262176 | tf_op jit(solution)/shard_map/ppermute | solution.py:464
  49.5 1.7 %collective-permute-done.4.refs_1_ = f32[32,2048]{1,0:T(8,128)S(1)} collective-permute-done((f32[32,2048]{1,0:T(8,128)S(1)}, f32[32,2048]{1,0:T(8,128)S(1)}, u32[]{:S(2)}, u32[]{:S(2)}) %collective-permute-start.4) | collective-permute-done | bytes 262176 | tf_op jit(solution)/shard_map/ppermute | solution.py:463
  51.2 1.7 %apply_2.1 = f32[16,32,128]{2,1,0:T(8,128)S(1)} custom-call(s32[192]{0:T(256)S(1)} %reshape.35.slot_ref, f32[2]{0:T(128)S(1)} %copy-done.2, f32[32,2048]{1,0:T(8,128)S(1)} %apply_1.1.refs_0_, f32[32,2048]{1,0:T(8,128)S(1)} %collective-permute-done.4.refs_1_, f32[32,2048]{1,0:T(8,128)S(1)} %collective-permute-done.5.refs_2_, ...), custom_call_target="tpu_custom_call" | custom-call | tf_op jit(solution)/shard_map/apply_2/pallas_call | solution.py:117
  52.9 14.7 %all_to_all.20.s_ref = f32[8,2,32,128]{3,2,1,0:T(8,128)S(1)} all-to-all(f32[8,2,32,128]{3,2,1,0:T(8,128)S(1)} %bitcast.3), channel_id=1, replica_groups=mesh['row'=64,'bundle'=8] {'bundle'}, dimensions={0} | all-to-all | bytes 524288 | tf_op jit(solution)/shard_map/all_to_all | solution.py:481
  67.6 0.4 gram.1
  68.0 12.7 %all_to_all.21 = f32[32,1,1280]{2,1,0:T(1,128)S(1)} all-to-all(f32[32,1,1280]{2,1,0:T(1,128)S(1)} %bitcast.5), channel_id=1, replica_groups={{0,2,4,6,8,10,12,14,16,18,20,22,24,26,28,30,32,34,36,38,40,42,44,46,48,..., dimensions={0} | all-to-all | bytes 327680 | tf_op jit(solution)/shard_map/all_to_all | solution.py:436
  80.8 13.0 %all_to_all.22 = f32[16,1,1280]{2,1,0:T(1,128)S(1)} all-to-all(f32[16,1,1280]{2,1,0:T(1,128)S(1)} %broadcast_in_dim.4), channel_id=1, replica_groups={{0,1,64,65,128,129,192,193,256,257,320,321,384,385,448,449},{2,3,66,67,..., dimensions={0} | all-to-all | bytes 163840 | tf_op jit(solution)/shard_map/all_to_all | solution.py:436
  93.9 13.2 %all_to_all.23 = f32[32,1,1280]{2,1,0:T(1,128)S(1)} all-to-all(f32[32,1,1280]{2,1,0:T(1,128)S(1)} %broadcast_in_dim.5), channel_id=1, replica_groups={{0,2,4,6,8,10,12,14,16,18,20,22,24,26,28,30,32,34,36,38,40,42,44,46,48,..., dimensions={0} | all-to-all | bytes 327680 | tf_op jit(solution)/shard_map/all_to_all | solution.py:436
  107.1 6.2 %orthonormalize.1 = (f32[256,256]{1,0:T(8,128)}, f32[256,256]{1,0:T(8,128)}) custom-call(f32[320,128]{1,0:T(8,128)S(1)} %bitcast.4, f32[8,2,32,128]{3,2,1,0:T(8,128)S(1)} %all_to_all.20.s_ref), custom_call_target="tpu_custom_call" | custom-call | tf_op jit(solution)/shard_map/orthonormalize/pallas_call | solution.py:395
  (12 shorter events, 0.5 us)
Async XLA Ops:
  0.6 20.6 %collective-permute-start.1 = (f32[32,2048]{1,0:T(8,128)}, f32[32,2048]{1,0:T(8,128)S(1)}, u32[]{:S(2)}, u32[]{:S(2)}) collective-permute-start(f32[32,2048]{1,0:T(8,128)} %refs_3_.1), channel_id=1, source_target_pairs={{0,504},{8,16},{16,8},{24,32},{32,24},{40,48},{48,40},{56,64},{64,... | collective-permute-start | bytes 786440 | tf_op jit(solution)/shard_map/ppermute | solution.py:464
  15.0 9.0 %collective-permute-start = (f32[32,2048]{1,0:T(8,128)}, f32[32,2048]{1,0:T(8,128)S(1)}, u32[]{:S(2)}, u32[]{:S(2)}) collective-permute-start(f32[32,2048]{1,0:T(8,128)} %refs_3_.1), channel_id=1, source_target_pairs={{0,8},{8,0},{16,24},{24,16},{32,40},{40,32},{48,56},{56,48},{64,72... | collective-permute-start | bytes 786440 | tf_op jit(solution)/shard_map/ppermute | solution.py:463
  17.9 1.9 %copy-start = (f32[32,64,384]{2,1,0:T(8,128)S(1)}, f32[32,64,384]{2,1,0:T(8,128)}, u32[]{:S(2)}) copy-start(f32[32,64,384]{2,1,0:T(8,128)} %b_ref.1) | copy-start | bytes 9437188
  19.8 4.2 %copy-start.1 = (f32[32,2048]{1,0:T(8,128)S(1)}, f32[32,2048]{1,0:T(8,128)}, u32[]{:S(2)}) copy-start(f32[32,2048]{1,0:T(8,128)} %refs_3_.1) | copy-start | bytes 786436
  19.8 4.2 %copy-start.2 = (f32[2]{0:T(128)S(1)}, f32[2]{0:T(128)}, u32[]{:S(2)}) copy-start(f32[2]{0:T(128)} %bounds_ref.5) | copy-start | bytes 28
  25.8 11.3 %collective-permute-start.3 = (f32[32,2048]{1,0:T(8,128)S(1)}, f32[32,2048]{1,0:T(8,128)S(1)}, u32[]{:S(2)}, u32[]{:S(2)}) collective-permute-start(f32[32,2048]{1,0:T(8,128)S(1)} %apply_0.1.refs_0_.refs_3_), channel_id=1, source_target_pairs={{0,504},{8,16},{16,8},{24,32},{32,24},{40,48},{48,40},{56,64},{64,... | collective-permute-start | bytes 786440 | tf_op jit(solution)/shard_map/ppermute | solution.py:464
  29.4 7.9 %collective-permute-start.2 = (f32[32,2048]{1,0:T(8,128)S(1)}, f32[32,2048]{1,0:T(8,128)S(1)}, u32[]{:S(2)}, u32[]{:S(2)}) collective-permute-start(f32[32,2048]{1,0:T(8,128)S(1)} %apply_0.1.refs_0_.refs_3_), channel_id=1, source_target_pairs={{0,8},{8,0},{16,24},{24,16},{32,40},{40,32},{48,56},{56,48},{64,72... | collective-permute-start | bytes 786440 | tf_op jit(solution)/shard_map/ppermute | solution.py:463
  39.0 10.4 %collective-permute-start.5 = (f32[32,2048]{1,0:T(8,128)S(1)}, f32[32,2048]{1,0:T(8,128)S(1)}, u32[]{:S(2)}, u32[]{:S(2)}) collective-permute-start(f32[32,2048]{1,0:T(8,128)S(1)} %apply_1.1.refs_0_), channel_id=1, source_target_pairs={{0,504},{8,16},{16,8},{24,32},{32,24},{40,48},{48,40},{56,64},{64,... | collective-permute-start | bytes 786440 | tf_op jit(solution)/shard_map/ppermute | solution.py:464
  43.8 7.4 %collective-permute-start.4 = (f32[32,2048]{1,0:T(8,128)S(1)}, f32[32,2048]{1,0:T(8,128)S(1)}, u32[]{:S(2)}, u32[]{:S(2)}) collective-permute-start(f32[32,2048]{1,0:T(8,128)S(1)} %apply_1.1.refs_0_), channel_id=1, source_target_pairs={{0,8},{8,0},{16,24},{24,16},{32,40},{40,32},{48,56},{56,48},{64,72... | collective-permute-start | bytes 786440 | tf_op jit(solution)/shard_map/ppermute | solution.py:463

commit v9 on v8

--- a/solution.py
+++ b/solution.py
@@ -416,19 +416,19 @@
     rows, bundles = lax.axis_size("row"), lax.axis_size("bundle")
     chips, planes = bundles // 2, 8
     line = rows // planes
-    part = chips * line
+    part = chips * planes
 
     def device(z, y, x, core):
         return ((z * line + y) * chips + x) * 2 + core
 
     plane = [
-        [device(z, y, x, core) for y in range(line) for x in range(chips)]
-        for z in range(planes)
+        [device(z, y, x, core) for z in range(planes) for x in range(chips)]
+        for y in range(line)
         for core in range(2)
     ]
     across = [
-        [device(z, y, x, core) for z in range(planes) for core in range(2)]
-        for y in range(line)
+        [device(z, y, x, core) for y in range(line) for core in range(2)]
+        for z in range(planes)
         for x in range(chips)
     ]
 
@@ -441,7 +441,7 @@
         return jnp.broadcast_to(x[None], (n,) + x.shape)
 
     mine = jnp.sum(exchange(packed.reshape(part, 1, -1), plane), axis=0)
-    mine = jnp.sum(exchange(copies(mine, 2 * planes), across), axis=0)
+    mine = jnp.sum(exchange(copies(mine, 2 * line), across), axis=0)
     return exchange(copies(mine, part), plane).reshape(packed.shape)
 
 

time: 114 us -> 114 us (level)
  no operation moved by 1% of the time
where the time goes in v9:
time: 114 us; the launch traced here: 113 us
  blocking collectives  53.5 us (47%)
  starting transfers between devices  28.5 us (25%)
  waiting for transfers between devices  14.6 us (13%)
  Pallas kernels  12.9 us (11%)
  local copies, waits for them, and re-layouts  2.21 us (2%)
    all_to_all x3, blocking collectives, exchange(): return lax.all_to_all(x, axes, 0, 0, axis_index_groups=groups, tiled=True)  38.8 us
    ppermute x3, starting transfers between devices, sides(): lax.ppermute(field, 'row', outside)  22.7 us
    all_to_all x1, blocking collectives, local(): lax.all_to_all(filtered.reshape(bundles, tiles // bundles, width, lanes),...  14.7 us
    ppermute x3, waiting for transfers between devices, sides(): lax.ppermute(field, 'row', outside)  9.75 us
    pallas_call x1, Pallas kernels, orthonormalize(): pl.pallas_call(solve_kernel, out_shape=(jax.ShapeDtypeStruct((k, n), F32)...  6.17 us
    ppermute x3, starting transfers between devices, sides(): lax.ppermute(field, 'row', inside)  5.76 us
    pallas_call x3, Pallas kernels, apply_step(): pl.pallas_call(functools.partial(apply_kernel, stage), out_shape=pltpu.VM...  5.14 us
    ppermute x3, waiting for transfers between devices, sides(): lax.ppermute(field, 'row', inside)  4.8 us
  transfers between devices with their start and end apart: 6, of which 6 were waited for; matrix products, arithmetic and copies ran while one was open for 1% of the time, Pallas kernels for 1%

profile of v9, /device:TPU:1, one launch (start us, length us, event | category | flops | bytes accessed | tf_op | source)
XLA Modules:
  0.0 113.3 jit_solution(6100181910204475156)
XLA Ops:
  0.6 14.4 %collective-permute-start.1 = (f32[32,2048]{1,0:T(8,128)}, f32[32,2048]{1,0:T(8,128)S(1)}, u32[]{:S(2)}, u32[]{:S(2)}) collective-permute-start(f32[32,2048]{1,0:T(8,128)} %refs_3_.1), channel_id=1, source_target_pairs={{0,504},{8,16},{16,8},{24,32},{32,24},{40,48},{48,40},{56,64},{64,... | collective-permute-start | bytes 786440 | tf_op jit(solution)/shard_map/ppermute | solution.py:464
  15.0 1.9 %collective-permute-start = (f32[32,2048]{1,0:T(8,128)}, f32[32,2048]{1,0:T(8,128)S(1)}, u32[]{:S(2)}, u32[]{:S(2)}) collective-permute-start(f32[32,2048]{1,0:T(8,128)} %refs_3_.1), channel_id=1, source_target_pairs={{0,8},{8,0},{16,24},{24,16},{32,40},{40,32},{48,56},{56,48},{64,72... | collective-permute-start | bytes 786440 | tf_op jit(solution)/shard_map/ppermute | solution.py:463
  17.0 0.8 fusion.5
  18.0 1.9 %copy-done = f32[32,64,384]{2,1,0:T(8,128)S(1)} copy-done((f32[32,64,384]{2,1,0:T(8,128)S(1)}, f32[32,64,384]{2,1,0:T(8,128)}, u32[]{:S(2)}) %copy-start) | copy-done | bytes 3145752
  19.8 1.1 %split_blocks.1.refs_3_.refs_4_ = bf16[32,384,128]{2,1,0:T(8,128)(2,1)S(1)} custom-call(f32[32,64,384]{2,1,0:T(8,128)S(1)} %copy-done), custom_call_target="tpu_custom_call" | custom-call | tf_op jit(solution)/shard_map/split_blocks/pallas_call | solution.py:45
  21.0 0.2 collective-permute-done.1.refs_2_
  21.2 2.8 %collective-permute-done.refs_1_ = f32[32,2048]{1,0:T(8,128)S(1)} collective-permute-done((f32[32,2048]{1,0:T(8,128)}, f32[32,2048]{1,0:T(8,128)S(1)}, u32[]{:S(2)}, u32[]{:S(2)}) %collective-permute-start) | collective-permute-done | bytes 262176 | tf_op jit(solution)/shard_map/ppermute | solution.py:463
  24.1 1.7 %apply_0.1.refs_0_.refs_3_ = f32[32,2048]{1,0:T(8,128)S(1)} custom-call(s32[192]{0:T(256)S(1)} %reshape.35.slot_ref, f32[2]{0:T(128)S(1)} %copy-done.2, f32[32,2048]{1,0:T(8,128)S(1)} %copy-done.1, f32[32,2048]{1,0:T(8,128)S(1)} %collective-permute-done.refs_1_, f32[32,2048]{1,0:T(8,128)S(1)} %collective-permute-done.1.refs_2_, ...), custom_call_target="tpu_custom_call" | custom-call | tf_op jit(solution)/shard_map/apply_0/pallas_call | solution.py:117
  25.8 3.6 %collective-permute-start.3 = (f32[32,2048]{1,0:T(8,128)S(1)}, f32[32,2048]{1,0:T(8,128)S(1)}, u32[]{:S(2)}, u32[]{:S(2)}) collective-permute-start(f32[32,2048]{1,0:T(8,128)S(1)} %apply_0.1.refs_0_.refs_3_), channel_id=1, source_target_pairs={{0,504},{8,16},{16,8},{24,32},{32,24},{40,48},{48,40},{56,64},{64,... | collective-permute-start | bytes 786440 | tf_op jit(solution)/shard_map/ppermute | solution.py:464
  29.4 1.9 %collective-permute-start.2 = (f32[32,2048]{1,0:T(8,128)S(1)}, f32[32,2048]{1,0:T(8,128)S(1)}, u32[]{:S(2)}, u32[]{:S(2)}) collective-permute-start(f32[32,2048]{1,0:T(8,128)S(1)} %apply_0.1.refs_0_.refs_3_), channel_id=1, source_target_pairs={{0,8},{8,0},{16,24},{24,16},{32,40},{40,32},{48,56},{56,48},{64,72... | collective-permute-start | bytes 786440 | tf_op jit(solution)/shard_map/ppermute | solution.py:463
  31.3 5.7 %collective-permute-done.3.refs_2_ = f32[32,2048]{1,0:T(8,128)S(1)} collective-permute-done((f32[32,2048]{1,0:T(8,128)S(1)}, f32[32,2048]{1,0:T(8,128)S(1)}, u32[]{:S(2)}, u32[]{:S(2)}) %collective-permute-start.3) | collective-permute-done | bytes 262176 | tf_op jit(solution)/shard_map/ppermute | solution.py:464
  37.0 0.3 collective-permute-done.2.refs_1_
  37.3 1.7 %apply_1.1.refs_0_ = f32[32,2048]{1,0:T(8,128)S(1)} custom-call(s32[192]{0:T(256)S(1)} %reshape.35.slot_ref, f32[2]{0:T(128)S(1)} %copy-done.2, f32[32,2048]{1,0:T(8,128)S(1)} %apply_0.1.refs_0_.refs_3_, f32[32,2048]{1,0:T(8,128)S(1)} %collective-permute-done.2.refs_1_, f32[32,2048]{1,0:T(8,128)S(1)} %collective-permute-done.3.refs_2_, ...), custom_call_target="tpu_custom_call" | custom-call | tf_op jit(solution)/shard_map/apply_1/pallas_call | solution.py:117
  39.0 4.7 %collective-permute-start.5 = (f32[32,2048]{1,0:T(8,128)S(1)}, f32[32,2048]{1,0:T(8,128)S(1)}, u32[]{:S(2)}, u32[]{:S(2)}) collective-permute-start(f32[32,2048]{1,0:T(8,128)S(1)} %apply_1.1.refs_0_), channel_id=1, source_target_pairs={{0,504},{8,16},{16,8},{24,32},{32,24},{40,48},{48,40},{56,64},{64,... | collective-permute-start | bytes 786440 | tf_op jit(solution)/shard_map/ppermute | solution.py:464
  43.8 1.9 %collective-permute-start.4 = (f32[32,2048]{1,0:T(8,128)S(1)}, f32[32,2048]{1,0:T(8,128)S(1)}, u32[]{:S(2)}, u32[]{:S(2)}) collective-permute-start(f32[32,2048]{1,0:T(8,128)S(1)} %apply_1.1.refs_0_), channel_id=1, source_target_pairs={{0,8},{8,0},{16,24},{24,16},{32,40},{40,32},{48,56},{56,48},{64,72... | collective-permute-start | bytes 786440 | tf_op jit(solution)/shard_map/ppermute | solution.py:463
  45.7 3.8 %collective-permute-done.5.refs_2_ = f32[32,2048]{1,0:T(8,128)S(1)} collective-permute-done((f32[32,2048]{1,0:T(8,128)S(1)}, f32[32,2048]{1,0:T(8,128)S(1)}, u32[]{:S(2)}, u32[]{:S(2)}) %collective-permute-start.5) | collective-permute-done | bytes 262176 | tf_op jit(solution)/shard_map/ppermute | solution.py:464
  49.5 1.7 %collective-permute-done.4.refs_1_ = f32[32,2048]{1,0:T(8,128)S(1)} collective-permute-done((f32[32,2048]{1,0:T(8,128)S(1)}, f32[32,2048]{1,0:T(8,128)S(1)}, u32[]{:S(2)}, u32[]{:S(2)}) %collective-permute-start.4) | collective-permute-done | bytes 262176 | tf_op jit(solution)/shard_map/ppermute | solution.py:463
  51.2 1.7 %apply_2.1 = f32[16,32,128]{2,1,0:T(8,128)S(1)} custom-call(s32[192]{0:T(256)S(1)} %reshape.35.slot_ref, f32[2]{0:T(128)S(1)} %copy-done.2, f32[32,2048]{1,0:T(8,128)S(1)} %apply_1.1.refs_0_, f32[32,2048]{1,0:T(8,128)S(1)} %collective-permute-done.4.refs_1_, f32[32,2048]{1,0:T(8,128)S(1)} %collective-permute-done.5.refs_2_, ...), custom_call_target="tpu_custom_call" | custom-call | tf_op jit(solution)/shard_map/apply_2/pallas_call | solution.py:117
  52.9 14.7 %all_to_all.20.s_ref = f32[8,2,32,128]{3,2,1,0:T(8,128)S(1)} all-to-all(f32[8,2,32,128]{3,2,1,0:T(8,128)S(1)} %bitcast.3), channel_id=1, replica_groups=mesh['row'=64,'bundle'=8] {'bundle'}, dimensions={0} | all-to-all | bytes 524288 | tf_op jit(solution)/shard_map/all_to_all | solution.py:481
  67.6 0.4 gram.1
  68.0 12.7 %all_to_all.21 = f32[32,1,1280]{2,1,0:T(1,128)S(1)} all-to-all(f32[32,1,1280]{2,1,0:T(1,128)S(1)} %bitcast.5), channel_id=1, replica_groups={{0,2,4,6,64,66,68,70,128,130,132,134,192,194,196,198,256,258,260,262,32..., dimensions={0} | all-to-all | bytes 327680 | tf_op jit(solution)/shard_map/all_to_all | solution.py:436
  80.8 13.0 %all_to_all.22 = f32[16,1,1280]{2,1,0:T(1,128)S(1)} all-to-all(f32[16,1,1280]{2,1,0:T(1,128)S(1)} %broadcast_in_dim.4), channel_id=1, replica_groups={{0,1,8,9,16,17,24,25,32,33,40,41,48,49,56,57},{2,3,10,11,18,19,26,27,34..., dimensions={0} | all-to-all | bytes 163840 | tf_op jit(solution)/shard_map/all_to_all | solution.py:436
  93.9 13.2 %all_to_all.23 = f32[32,1,1280]{2,1,0:T(1,128)S(1)} all-to-all(f32[32,1,1280]{2,1,0:T(1,128)S(1)} %broadcast_in_dim.5), channel_id=1, replica_groups={{0,2,4,6,64,66,68,70,128,130,132,134,192,194,196,198,256,258,260,262,32..., dimensions={0} | all-to-all | bytes 327680 | tf_op jit(solution)/shard_map/all_to_all | solution.py:436
  107.1 6.2 %orthonormalize.1 = (f32[256,256]{1,0:T(8,128)}, f32[256,256]{1,0:T(8,128)}) custom-call(f32[320,128]{1,0:T(8,128)S(1)} %bitcast.4, f32[8,2,32,128]{3,2,1,0:T(8,128)S(1)} %all_to_all.20.s_ref), custom_call_target="tpu_custom_call" | custom-call | tf_op jit(solution)/shard_map/orthonormalize/pallas_call | solution.py:395
  (12 shorter events, 0.5 us)
Async XLA Ops:
  0.6 20.6 %collective-permute-start.1 = (f32[32,2048]{1,0:T(8,128)}, f32[32,2048]{1,0:T(8,128)S(1)}, u32[]{:S(2)}, u32[]{:S(2)}) collective-permute-start(f32[32,2048]{1,0:T(8,128)} %refs_3_.1), channel_id=1, source_target_pairs={{0,504},{8,16},{16,8},{24,32},{32,24},{40,48},{48,40},{56,64},{64,... | collective-permute-start | bytes 786440 | tf_op jit(solution)/shard_map/ppermute | solution.py:464
  15.0 9.0 %collective-permute-start = (f32[32,2048]{1,0:T(8,128)}, f32[32,2048]{1,0:T(8,128)S(1)}, u32[]{:S(2)}, u32[]{:S(2)}) collective-permute-start(f32[32,2048]{1,0:T(8,128)} %refs_3_.1), channel_id=1, source_target_pairs={{0,8},{8,0},{16,24},{24,16},{32,40},{40,32},{48,56},{56,48},{64,72... | collective-permute-start | bytes 786440 | tf_op jit(solution)/shard_map/ppermute | solution.py:463
  17.9 1.9 %copy-start = (f32[32,64,384]{2,1,0:T(8,128)S(1)}, f32[32,64,384]{2,1,0:T(8,128)}, u32[]{:S(2)}) copy-start(f32[32,64,384]{2,1,0:T(8,128)} %b_ref.1) | copy-start | bytes 9437188
  19.8 4.2 %copy-start.1 = (f32[32,2048]{1,0:T(8,128)S(1)}, f32[32,2048]{1,0:T(8,128)}, u32[]{:S(2)}) copy-start(f32[32,2048]{1,0:T(8,128)} %refs_3_.1) | copy-start | bytes 786436
  19.8 4.2 %copy-start.2 = (f32[2]{0:T(128)S(1)}, f32[2]{0:T(128)}, u32[]{:S(2)}) copy-start(f32[2]{0:T(128)} %bounds_ref.5) | copy-start | bytes 28
  25.8 11.3 %collective-permute-start.3 = (f32[32,2048]{1,0:T(8,128)S(1)}, f32[32,2048]{1,0:T(8,128)S(1)}, u32[]{:S(2)}, u32[]{:S(2)}) collective-permute-start(f32[32,2048]{1,0:T(8,128)S(1)} %apply_0.1.refs_0_.refs_3_), channel_id=1, source_target_pairs={{0,504},{8,16},{16,8},{24,32},{32,24},{40,48},{48,40},{56,64},{64,... | collective-permute-start | bytes 786440 | tf_op jit(solution)/shard_map/ppermute | solution.py:464
  29.4 7.9 %collective-permute-start.2 = (f32[32,2048]{1,0:T(8,128)S(1)}, f32[32,2048]{1,0:T(8,128)S(1)}, u32[]{:S(2)}, u32[]{:S(2)}) collective-permute-start(f32[32,2048]{1,0:T(8,128)S(1)} %apply_0.1.refs_0_.refs_3_), channel_id=1, source_target_pairs={{0,8},{8,0},{16,24},{24,16},{32,40},{40,32},{48,56},{56,48},{64,72... | collective-permute-start | bytes 786440 | tf_op jit(solution)/shard_map/ppermute | solution.py:463
  39.0 10.4 %collective-permute-start.5 = (f32[32,2048]{1,0:T(8,128)S(1)}, f32[32,2048]{1,0:T(8,128)S(1)}, u32[]{:S(2)}, u32[]{:S(2)}) collective-permute-start(f32[32,2048]{1,0:T(8,128)S(1)} %apply_1.1.refs_0_), channel_id=1, source_target_pairs={{0,504},{8,16},{16,8},{24,32},{32,24},{40,48},{48,40},{56,64},{64,... | collective-permute-start | bytes 786440 | tf_op jit(solution)/shard_map/ppermute | solution.py:464
  43.8 7.4 %collective-permute-start.4 = (f32[32,2048]{1,0:T(8,128)S(1)}, f32[32,2048]{1,0:T(8,128)S(1)}, u32[]{:S(2)}, u32[]{:S(2)}) collective-permute-start(f32[32,2048]{1,0:T(8,128)S(1)} %apply_1.1.refs_0_), channel_id=1, source_target_pairs={{0,8},{8,0},{16,24},{24,16},{32,40},{40,32},{48,56},{56,48},{64,72... | collective-permute-start | bytes 786440 | tf_op jit(solution)/shard_map/ppermute | solution.py:463
